TPU v7x, 32 devices: a whole 2x2x4 slice. The times are simulated.
32 devices in a mesh: groups: 2 (over x), slab: 16 (over z, y, core).
Axes of the slice: x: 2, y: 2, z: 4, core: 2. Of those that a mesh axis runs over, the one named last changes fastest.
Arguments:
- conc_init: float32 [128, 16384], P(('groups', 'slab')), parts along dimension 0, may hold values from 0.2 to 2
- cover_init: float32 [128, 256], P(('groups', 'slab')), parts along dimension 0, may hold values from 0 to 0.9
- rate_on: float32 [128, 256], P(('groups', 'slab')), parts along dimension 0, may hold values from 0.05 to 0.5
- rate_off: float32 [128, 256], P(('groups', 'slab')), parts along dimension 0, may hold values from 0.02 to 0.2
- site_mask: int32 [128, 256], P(('groups', 'slab')), parts along dimension 0, may hold values 0 or 1
- inlet_profiles: float32 [16, 64], P('groups'), parts along dimension 0, may hold values from 0.5 to 2.5
- inlet_index: int32 [512], P('groups'), parts along dimension 0, may hold values from 0 to 7
- lift: float32 [3, 64], replicated, may hold values from -4.6 to 4.6
- mode_weight: bfloat16 [2048, 2, 64, 64], P('slab'), may hold values from -0.5 to 0.5
- point_weight: bfloat16 [64, 64], replicated, may hold values from -0.75 to 0.75
- point_bias: float32 [64], replicated, may hold values from -3 to 3
- readout: float32 [64], replicated, may hold values from -0.75 to 0.75
- cotangent: float32 [128, 16384], P(('groups', 'slab')), parts along dimension 0, may hold values from -6 to 6
Outputs:
- concentration: float32 [128, 16384], P(('groups', 'slab')), parts along dimension 0
- coverage: float32 [128, 256], P(('groups', 'slab')), parts along dimension 0
- prediction: float32 [128, 16384], P(('groups', 'slab')), parts along dimension 0
- grad_modes: float32 [4096, 2, 64, 64], P(('groups', 'slab')), parts along dimension 0
- grad_point: float32 [128, 64], P('groups'), parts along dimension 0
There are 2 independent parts, one for each index of `groups`. A program takes and returns all parts, laid end to end along the dimension named above; an argument that names none is the same for every part. Nothing has to cross between parts.
All inputs are finite; a program needn't handle non-finite values. No bound on the sum of `site_mask` on one device may be relied on, other than what follows from the above.
Results may differ from a plain program's by a relative error of at most 0.0061.
Values may be sent and summed in bfloat16 or wider, within the bound.
No kernel may reach another device: no remote copies, remote signals or barrier semaphores. Data moves between devices by JAX's collectives and lax.ppermute only.
A program may use at most 128 MiB of HBM per device.

v0:
```python
import math

import jax
import jax.numpy as jnp
from jax import lax
from jax.sharding import PartitionSpec as P

KX = 16
KY = 16
KZ = 8
STEPS = 4
PROFILES = 8


PEAK_SPEED = 0.6
DIFFUSIVITY = 0.06


def with_halo(x, sides, width):
    for axis, dim in sides:
        size, length = (lax.axis_size(axis), x.shape[dim])
        up = [(i, (i + 1) % size) for i in range(size - 1)]
        down = [(j, i) for i, j in up]
        last = lax.slice_in_dim(x, length - width, length, axis=dim)
        leading = lax.slice_in_dim(x, 0, width, axis=dim)
        before = lax.ppermute(last, axis, up)
        after = lax.ppermute(leading, axis, down)
        x = jnp.concatenate([before, x, after], axis=dim)
    return x


def flow_speed(depth_cells):
    height = (jnp.arange(depth_cells, dtype=jnp.float32) + 0.5) / depth_cells
    return PEAK_SPEED * 4.0 * height * (1.0 - height)


def advance(padded, coverage, rate_on, rate_off, site_open, velocity):
    centre = padded[1:-1]
    behind = padded[:-2]
    ahead = padded[2:]
    left_cells = jnp.roll(centre, 1, axis=1)
    right_cells = jnp.roll(centre, -1, axis=1)
    below_cells = jnp.concatenate([centre[:, :, :1], centre[:, :, :-1]], axis=2)
    above_cells = jnp.concatenate([centre[:, :, 1:], centre[:, :, -1:]], axis=2)
    laplace = behind + ahead + left_cells + right_cells + below_cells + above_cells - 6.0 * centre
    uptake = site_open * (rate_on * centre[:, :, 0] * (1.0 - coverage) - rate_off * coverage)
    updated = centre + DIFFUSIVITY * laplace - velocity[None, None, :] * (centre - behind)
    wall_layer = updated[:, :, :1] - uptake[:, :, None]
    updated = jnp.concatenate([wall_layer, updated[:, :, 1:]], axis=2)
    return (updated, coverage + uptake)


def cross_basis(span_cells, depth_cells):
    y_index = jnp.arange(span_cells, dtype=jnp.int32)[:, None, None, None]
    z_index = jnp.arange(depth_cells, dtype=jnp.int32)[None, :, None, None]
    wave_y = jnp.arange(KY, dtype=jnp.int32)[None, None, :, None]
    wave_z = jnp.arange(KZ, dtype=jnp.int32)[None, None, None, :]
    fraction = (wave_y * y_index % span_cells).astype(jnp.float32) / span_cells + (
        wave_z * z_index % depth_cells
    ).astype(jnp.float32) / depth_cells
    angles = 2.0 * math.pi * fraction
    basis = jnp.stack([jnp.cos(angles), -jnp.sin(angles)], axis=-1)
    return basis.reshape(span_cells * depth_cells, 2 * KY * KZ).astype(jnp.bfloat16)


def stream_factors(positions, length_x):
    wave_x = jnp.arange(KX, dtype=jnp.int32)[:, None]
    phases = 2.0 * math.pi * (wave_x * positions[None, :] % length_x).astype(jnp.float32) / length_x
    return (jnp.cos(phases), jnp.sin(phases))


def along_x_forward(columns, cos_table, sin_table):
    highest = lax.Precision.HIGHEST
    channels, stream_len, spread = columns.shape
    split = columns.reshape(channels, stream_len, spread // 2, 2)
    real_part = split[..., 0]
    imag_part = split[..., 1]
    out_real = jnp.einsum("kx,cxy->ykc", cos_table, real_part, precision=highest) + jnp.einsum(
        "kx,cxy->ykc", sin_table, imag_part, precision=highest
    )
    out_imag = jnp.einsum("kx,cxy->ykc", cos_table, imag_part, precision=highest) - jnp.einsum(
        "kx,cxy->ykc", sin_table, real_part, precision=highest
    )
    return jnp.concatenate([out_real, out_imag], axis=2).reshape(-1, 2 * channels)


def along_x_inverse(rows, cos_table, sin_table):
    highest = lax.Precision.HIGHEST
    channels = rows.shape[1] // 2
    stream_len = cos_table.shape[1]
    shaped = rows.reshape(-1, KX, 2 * channels)
    real_part = shaped[:, :, :channels]
    imag_part = shaped[:, :, channels:]
    out_real = jnp.einsum("kx,ykc->cxy", cos_table, real_part, precision=highest) - jnp.einsum(
        "kx,ykc->cxy", sin_table, imag_part, precision=highest
    )
    out_imag = jnp.einsum("kx,ykc->cxy", sin_table, real_part, precision=highest) + jnp.einsum(
        "kx,ykc->cxy", cos_table, imag_part, precision=highest
    )
    return jnp.stack([out_real, out_imag], axis=-1).reshape(channels, stream_len, -1)


def mode_mixing(spectrum, mode_weight):
    highest = lax.Precision.HIGHEST
    channels = spectrum.shape[1] // 2
    spec_real = spectrum[:, :channels]
    spec_imag = spectrum[:, channels:]
    weights = mode_weight.astype(jnp.float32)
    weight_real = weights[:, 0]
    weight_imag = weights[:, 1]
    out_real = jnp.einsum("mc,mco->mo", spec_real, weight_real, precision=highest) - jnp.einsum(
        "mc,mco->mo", spec_imag, weight_imag, precision=highest
    )
    out_imag = jnp.einsum("mc,mco->mo", spec_real, weight_imag, precision=highest) + jnp.einsum(
        "mc,mco->mo", spec_imag, weight_real, precision=highest
    )
    return jnp.concatenate([out_real, out_imag], axis=1).astype(jnp.bfloat16)


def outer_grad(spectrum, grad_spectrum):
    channels = spectrum.shape[1] // 2
    spec_real = spectrum[:, :channels, None]
    spec_imag = spectrum[:, channels:, None]
    grad_real = grad_spectrum[:, None, :channels]
    grad_imag = grad_spectrum[:, None, channels:]
    first = spec_real * grad_real + spec_imag * grad_imag
    second = spec_real * grad_imag - spec_imag * grad_real
    return jnp.stack([first, second], axis=1)


def lift_features(concentration, coverage, lift):
    depth_cells = concentration.shape[2]
    surface = (jnp.arange(depth_cells) == 0).astype(jnp.float32)
    wall = coverage[:, :, None] * surface[None, None, :]
    lifted = (
        lift[0][:, None, None, None] * concentration[None]
        + lift[1][:, None, None, None] * wall[None]
        + lift[2][:, None, None, None]
    )
    return lifted.astype(jnp.bfloat16)


def body(
    conc_init,
    cover_init,
    rate_on,
    rate_off,
    site_mask,
    inlet_profiles,
    inlet_index,
    lift,
    mode_weight,
    point_weight,
    point_bias,
    readout,
    cotangent,
):
    devices = lax.axis_size("slab")
    position = lax.axis_index("slab")
    local_x, plane_cells = conc_init.shape
    depth_cells = inlet_profiles.shape[1]
    span_cells = plane_cells // depth_cells
    channels = lift.shape[1]
    total_x = local_x * devices
    velocity = flow_speed(depth_cells)
    site_open = site_mask.astype(jnp.float32)
    choose = (inlet_index[:, None] == jnp.arange(PROFILES, dtype=jnp.int32)[None, :]).astype(
        jnp.float32
    )
    inlet_plane = jnp.dot(choose, inlet_profiles, precision=lax.Precision.HIGHEST).reshape(
        plane_cells
    )
    flat_conc = conc_init
    coverage = cover_init
    for substep in range(STEPS):
        padded = with_halo(flat_conc, (("slab", 0),), 1)
        upstream = jnp.where(position == 0, inlet_plane, padded[0])
        downstream = jnp.where(position == devices - 1, flat_conc[-1], padded[-1])
        padded = jnp.concatenate([upstream[None], flat_conc, downstream[None]], axis=0)
        updated, coverage = advance(
            padded.reshape(local_x + 2, span_cells, depth_cells),
            coverage,
            rate_on,
            rate_off,
            site_open,
            velocity,
        )
        flat_conc = updated.reshape(local_x, plane_cells)
    concentration = flat_conc.reshape(local_x, span_cells, depth_cells)
    basis = cross_basis(span_cells, depth_cells)
    positions = position * local_x + jnp.arange(local_x, dtype=jnp.int32)
    cos_local, sin_local = stream_factors(positions, total_x)
    forward_scale = 1.0 / math.sqrt(total_x * plane_cells)
    inverse_scale = 1.0 / math.sqrt(KX * KY * KZ)
    features = lift_features(concentration, coverage, lift)
    columns = jnp.dot(
        features.reshape(channels * local_x, plane_cells), basis, preferred_element_type=jnp.float32
    ).reshape(channels, local_x, -1)
    spectrum = lax.psum_scatter(
        forward_scale * along_x_forward(columns, cos_local, sin_local),
        "slab",
        scatter_dimension=0,
        tiled=True,
    )
    mixed = mode_mixing(spectrum, mode_weight)
    gathered = lax.all_gather(mixed, "slab", axis=0, tiled=True)
    inverse = (
        inverse_scale * along_x_inverse(gathered.astype(jnp.float32), cos_local, sin_local)
    ).astype(jnp.bfloat16)
    lifted = features.reshape(channels, local_x * plane_cells)
    spectral = lax.dot_general(
        inverse.reshape(channels * local_x, -1),
        basis,
        (((1,), (1,)), ((), ())),
        preferred_element_type=jnp.float32,
    )
    preact = (
        spectral.reshape(channels, -1)
        + jnp.dot(point_weight, lifted, preferred_element_type=jnp.float32)
        + point_bias[:, None]
    )
    hidden, gelu_back = jax.vjp(jax.nn.gelu, preact)
    prediction = jnp.sum(readout[:, None] * hidden, axis=0).reshape(local_x, plane_cells)
    (grad_pre,) = gelu_back(readout[:, None] * cotangent.reshape(1, -1))
    grad_pre = grad_pre.astype(jnp.bfloat16)
    point_local = lax.dot_general(
        grad_pre, lifted, (((1,), (1,)), ((), ())), preferred_element_type=jnp.float32
    )
    grad_point = lax.psum(point_local, "slab")
    grad_columns = (
        inverse_scale
        * jnp.dot(
            grad_pre.reshape(channels * local_x, plane_cells),
            basis,
            preferred_element_type=jnp.float32,
        )
    ).reshape(channels, local_x, -1)
    grad_spectrum = lax.psum_scatter(
        along_x_forward(grad_columns, cos_local, sin_local), "slab", scatter_dimension=0, tiled=True
    )
    grad_modes = outer_grad(spectrum, grad_spectrum)
    return (flat_conc, coverage, prediction, grad_modes, grad_point)


def solution(mesh):
    placed = (
        P(("groups", "slab"), None),
        P(("groups", "slab"), None),
        P(("groups", "slab"), None),
        P(("groups", "slab"), None),
        P(("groups", "slab"), None),
        P("groups", None),
        P("groups"),
        P(),
        P("slab", None, None, None),
        P(),
        P(),
        P(),
        P(("groups", "slab"), None),
    )
    return jax.shard_map(
        body,
        mesh=mesh,
        in_specs=placed,
        out_specs=(
            P(("groups", "slab"), None),
            P(("groups", "slab"), None),
            P(("groups", "slab"), None),
            P(("groups", "slab"), None, None, None),
            P("groups", None),
        ),
        check_vma=False,
    )
```

profile of v0, /device:TPU:0, one launch (start us, length us, event | category | flops | bytes accessed | tf_op | source)
XLA Modules:
  0.0 508.9 jit_solution(221969507463641684)
XLA Ops:
  7.2 1.0 slice.285
  8.2 1.3 collective-permute-start.1
  9.5 1.2 slice.281
  11.2 1.2 fusion.197
  12.3 1.0 fusion.198
  16.2 61.6 %fusion.12 = (bf16[256,64,16,8,1]{1,0,4,3,2:T(8,128)(2,1)S(1)}, bf16[256,64,16,8,1]{1,0,4,3,2:T(8,128)(2,1)S(1)}) fusion(f32[64,8]{0,1:T(8,128)S(1)} %fusion.97, f32[256,16]{0,1:T(8,128)S(1)} %fusion.91), kind=kLoop, calls=%fused_computation.22 | loop fusion | flops 10485760 | bytes 8407040 | tf_op jit(solution)/shard_map/cos | solution.py:62
  77.8 7.7 %maximum_convert_fusion = bf16[256,64,16,8,2]{1,0,4,3,2:T(8,128)(2,1)} fusion(bf16[256,64,16,8,1]{1,0,4,3,2:T(8,128)(2,1)S(1)} %get-tuple-element.70, bf16[256,64,16,8,1]{1,0,4,3,2:T(8,128)(2,1)S(1)} %get-tuple-element.69), kind=kLoop, calls=%fused_computation.3 | loop fusion | flops 4194304 | bytes 16777216 | tf_op jit(solution)/shard_map/convert_element_type | solution.py:63
  85.5 19.9 %convert_element_type.90 = bf16[16384,256]{0,1:T(8,128)(2,1)} reshape(bf16[256,64,16,8,2]{1,0,4,3,2:T(8,128)(2,1)} %maximum_convert_fusion) | data formatting | bytes 16777216 | tf_op jit(solution)/shard_map/convert_element_type | solution.py:63
  105.4 14.1 %dot_general.74 = bf16[128,2,16384]{2,1,0:T(2,128)(2,1)} reshape(bf16[256,16384]{1,0:T(8,128)(2,1)} %bitcast.137) | data formatting | bytes 16777216 | tf_op jit(solution)/shard_map/dot_general | solution.py:196
  120.7 3.0 collective-permute-start
  125.6 2.0 fusion.44
  128.5 1.3 slice_maximum_fusion.7
  130.3 1.3 collective-permute-start.3
  131.6 5.8 %collective-permute-start.2 = (f32[1,16384]{1,0:T(1,128)S(1)}, f32[1,16384]{1,0:T(1,128)S(1)}, u32[]{:S(2)}, u32[]{:S(2)}) collective-permute-start(f32[1,16384]{1,0:T(1,128)S(1)} %slice.299), channel_id=1, source_target_pairs={{0,1},{1,2},{2,3},{3,4},{4,5},{5,6},{6,7},{7,8},{8,9},{9,10},{10,1... | collective-permute-start | bytes 196616 | tf_op jit(solution)/shard_map/ppermute | solution.py:26
  140.4 1.2 slice.301
  141.6 1.1 slice.305
  142.7 1.9 fusion.51
  146.5 1.3 slice_maximum_fusion.4
  149.1 1.0 slice.315
  150.1 4.3 collective-permute-start.4
  154.4 1.0 slice.319
  155.4 1.3 collective-permute-start.5
  157.5 2.7 collective-permute-done.5
  160.3 1.0 pad_maximum_fusion.8
  161.3 1.2 slice.317
  162.5 2.0 slice.321
  164.6 1.9 fusion.58
  168.3 1.3 slice_maximum_fusion.1
  169.6 1.4 add_add_fusion
  171.5 1.6 slice.331
  173.1 5.5 %collective-permute-start.6 = (f32[1,16384]{1,0:T(1,128)}, f32[1,16384]{1,0:T(1,128)}, u32[]{:S(2)}, u32[]{:S(2)}) collective-permute-start(f32[1,16384]{1,0:T(1,128)} %slice.331), channel_id=1, source_target_pairs={{0,1},{1,2},{2,3},{3,4},{4,5},{5,6},{6,7},{7,8},{8,9},{9,10},{10,1... | collective-permute-start | bytes 196616 | tf_op jit(solution)/shard_map/ppermute | solution.py:26
  178.6 1.7 slice.335
  180.3 1.5 collective-permute-start.7
  183.6 1.7 broadcast_multiply_fusion.1
  186.4 1.0 pad_maximum_fusion.6
  187.4 1.2 slice.333
  188.7 2.0 slice.337
  190.7 1.9 fusion.65
  193.3 14.4 %fusion.15 = f32[64,4,128,2]{2,0,3,1:T(8,128)S(1)} fusion(bf16[128,2,16384]{2,1,0:T(2,128)(2,1)} %dot_general.74, f32[64]{0:T(128)} %get-tuple-element.72, f32[4,16384]{1,0:T(4,128)} %broadcast_multiply_fusion.1, f32[64]{0:T(128)} %get-tuple-element.73, f32[4,16384]{1,0:T(4,128)S(1)} %reshape.287, f32[64]{0:T(128)} %get-tuple-element.71), kind=kOutput, calls=%fused_computation.26 | convolution fusion | flops 2168455168 | bytes 9175808 | tf_op jit(solution)/shard_map/dot_general | solution.py:196
  210.9 1.6 copy.258
  212.5 1.7 slice_bitcast_fusion.1
  214.3 3.8 copy.277
  218.1 3.7 copy.280
  222.3 53.2 %reduce-scatter.3.cloned.1.call-done = f32[128,128]{1,0:T(8,128)} async-done(((f32[2048,128]{1,0:T(8,128)}), f32[128,128]{1,0:T(8,128)}) %reduce-scatter.3.cloned.1.call-update) | async-done | bytes 65552 | tf_op jit(solution)/shard_map/reduce_scatter | solution.py:199
  276.4 3.3 fusion.202
  279.7 3.3 fusion.204
  283.1 3.3 fusion.203
  286.4 3.3 fusion.205
  289.8 20.8 %all_gather.3 = bf16[2048,128]{1,0:T(8,128)(2,1)S(1)} all-gather(bf16[128,128]{1,0:T(8,128)(2,1)S(1)} %pad_maximum_fusion.14), channel_id=1, replica_groups=mesh['groups'=2,'slab'=16] {'slab'}, dimensions={0}, use_global_device_ids=true | all-gather | bytes 557056 | tf_op jit(solution)/shard_map/all_gather | solution.py:206
  313.6 7.6 %copy.265 = bf16[64,4,128,2]{1,0,3,2:T(8,128)(2,1)} copy(bf16[64,4,128,2]{2,0,3,1:T(8,128)(2,1)S(1)} %fusion.66) | data formatting | bytes 262144 | tf_op jit(solution)/shard_map/convert_element_type | solution.py:209
  321.2 8.9 %convert_element_type.93 = bf16[256,256]{0,1:T(8,128)(2,1)S(1)} reshape(bf16[64,4,128,2]{1,0,3,2:T(8,128)(2,1)} %copy.265) | data formatting | bytes 262144 | tf_op jit(solution)/shard_map/convert_element_type | solution.py:209
  330.1 11.5 %fusion.206 = f32[256,16384]{1,0:T(8,128)} fusion(bf16[256,256]{0,1:T(8,128)(2,1)S(1)} %convert_element_type.93, bf16[16384,256]{0,1:T(8,128)(2,1)} %convert_element_type.90), kind=kOutput, calls=%fused_computation.309 | convolution fusion | flops 2147483648 | bytes 25296896 | tf_op jit(solution)/shard_map/dot_general | solution.py:211
  341.6 17.0 %reshape.289 = f32[64,65536]{1,0:T(8,128)} reshape(f32[256,16384]{1,0:T(8,128)} %fusion.206) | data formatting | bytes 33554432 | tf_op jit(solution)/shard_map/reshape | solution.py:218
  358.7 21.8 %fusion.8 = (bf16[64,65536]{1,0:T(8,128)(2,1)}, f32[65536]{0:T(1024)S(1)}) fusion(f32[65536]{0:T(1024)S(1)} %bitcast.142, f32[64]{0:T(128)S(1)} %copy-done.16, f32[64]{0:T(128)S(1)} %copy-done.17, f32[64,65536]{1,0:T(8,128)} %reshape.289, bf16[64,64]{1,0:T(8,128)(2,1)S(1)} %copy-done, f32[64]{0:T(128)S(1)} %copy-done.14, f32[65536]{0:T(1024)S(1)} %mul.544, ...), kind=kOutput, calls=%fused_computation.14 | convolution fusion | flops 666828800 | bytes 26223872 | tf_op jit(solution)/shard_map/dot_general | solution.py:219
  380.5 11.4 %reshape.291 = bf16[256,16384]{1,0:T(8,128)(2,1)} reshape(bf16[64,65536]{1,0:T(8,128)(2,1)} %get-tuple-element.11) | data formatting | bytes 16777216 | tf_op jit(solution)/shard_map/reshape | solution.py:233
  391.9 8.1 %convolution_multiply_fusion = f32[256,256]{1,0:T(8,128)S(1)} fusion(bf16[256,16384]{1,0:T(8,128)(2,1)} %reshape.291, bf16[16384,256]{0,1:T(8,128)(2,1)} %convert_element_type.90), kind=kOutput, calls=%fused_computation.55 | convolution fusion | flops 2147549184 | bytes 17039360 | tf_op jit(solution)/shard_map/dot_general | solution.py:232
  400.2 10.3 %reshape_reshape.4 = f32[64,4,128,2]{1,0,3,2:T(8,128)} reshape(f32[256,256]{0,1:T(8,128)S(1)} %copy.267) | data formatting | bytes 524288 | tf_op jit(solution)/shard_map/reshape;reshape | solution.py:75
  410.5 8.5 %fusion.195 = (f32[64,4,128,1]{1,0,3,2:T(8,128)}, f32[64,4,128,1]{1,0,3,2:T(8,128)}) fusion(f32[64,4,128,2]{1,0,3,2:T(8,128)} %reshape_reshape.4), kind=kLoop, calls=%fused_computation.298 | loop fusion | bytes 524288 | tf_op jit(solution)/shard_map/slice | solution.py:76
  419.0 3.8 copy.286
  423.5 3.8 copy.287
  429.6 1.6 copy.270
  432.2 6.8 %fusion.13 = f32[64,64]{1,0:T(8,128)S(1)} fusion(bf16[64,65536]{1,0:T(8,128)(2,1)} %get-tuple-element.11, f32[64]{0:T(128)S(1)} %copy-done.14, f32[65536]{0:T(1024)S(1)} %mul.544, f32[64]{0:T(128)S(1)} %copy-done.15, f32[65536]{0:T(1024)S(1)} %mul.538, f32[64]{0:T(128)S(1)} %copy-done.13), kind=kOutput, calls=%fused_computation.24 | convolution fusion | flops 557842432 | bytes 8930048 | tf_op jit(solution)/shard_map/dot_general | solution.py:226
  439.1 58.7 %psum.7 = f32[64,64]{1,0:T(8,128)} all-reduce(f32[64,64]{1,0:T(8,128)S(1)} %fusion.13), channel_id=1, replica_groups=mesh['groups'=2,'slab'=16] {'slab'}, use_global_device_ids=true, to_apply=%region_3.4 | all-reduce | flops 4096 | bytes 32768 | tf_op jit(solution)/shard_map/psum | solution.py:229
  499.6 2.3 pad_maximum_fusion
  (144 shorter events, 33.9 us)
Async XLA Ops:
  7.2 351.4 %copy-start = (bf16[64,64]{1,0:T(8,128)(2,1)S(1)}, bf16[64,64]{1,0:T(8,128)(2,1)}, u32[]{:S(2)}) copy-start(bf16[64,64]{1,0:T(8,128)(2,1)} %param.22) | copy-start | bytes 24580
  7.2 268.2 %reduce-scatter.3.cloned.1.call-start = ((), (), s32[]{:S(2)}) async-start(), calls=%async_computation.2 | async-start | bytes 1114112 | tf_op jit(solution)/shard_map/reduce_scatter | solution.py:199
  8.2 112.4 %collective-permute-start.1 = (f32[1,16384]{1,0:T(1,128)S(1)}, f32[1,16384]{1,0:T(1,128)S(1)}, u32[]{:S(2)}, u32[]{:S(2)}) collective-permute-start(f32[1,16384]{1,0:T(1,128)S(1)} %slice.285), channel_id=1, source_target_pairs={{1,0},{2,1},{3,2},{4,3},{5,4},{6,5},{7,6},{8,7},{9,8},{10,9},{11,1... | collective-permute-start | bytes 196616 | tf_op jit(solution)/shard_map/ppermute | solution.py:27
  11.1 66.6 %copy-start.5 = (f32[4,256]{1,0:T(4,128)}, f32[4,256]{1,0:T(4,128)S(1)}, u32[]{:S(2)}) copy-start(f32[4,256]{1,0:T(4,128)S(1)} %get-tuple-element.40) | copy-start | bytes 12292
  13.9 71.6 %copy-start.10 = (f32[64]{0:T(128)}, f32[64]{0:T(128)S(1)}, u32[]{:S(2)}) copy-start(f32[64]{0:T(128)S(1)} %compare_convert_fusion) | copy-start | bytes 772
  85.5 34.0 %copy-start.12 = (f32[3,64]{1,0:T(4,128)S(1)}, f32[3,64]{1,0:T(4,128)}, u32[]{:S(2)}) copy-start(f32[3,64]{1,0:T(4,128)} %param.20) | copy-start | bytes 2308
  85.5 35.1 %copy-start.2 = (f32[4,16384]{1,0:T(4,128)S(1)}, f32[4,16384]{1,0:T(4,128)}, u32[]{:S(2)}) copy-start(f32[4,16384]{1,0:T(4,128)} %param.13) | copy-start | bytes 786436
  120.7 3.9 collective-permute-start
  128.2 11.1 %copy-start.7 = (f32[4,256]{1,0:T(4,128)}, f32[4,256]{1,0:T(4,128)S(1)}, u32[]{:S(2)}) copy-start(f32[4,256]{1,0:T(4,128)S(1)} %get-tuple-element.9) | copy-start | bytes 12292
  130.3 9.0 %collective-permute-start.3 = (f32[1,16384]{1,0:T(1,128)S(1)}, f32[1,16384]{1,0:T(1,128)S(1)}, u32[]{:S(2)}, u32[]{:S(2)}) collective-permute-start(f32[1,16384]{1,0:T(1,128)S(1)} %slice.303), channel_id=1, source_target_pairs={{1,0},{2,1},{3,2},{4,3},{5,4},{6,5},{7,6},{8,7},{9,8},{10,9},{11,1... | collective-permute-start | bytes 196616 | tf_op jit(solution)/shard_map/ppermute | solution.py:27
  131.6 7.7 %collective-permute-start.2 = (f32[1,16384]{1,0:T(1,128)S(1)}, f32[1,16384]{1,0:T(1,128)S(1)}, u32[]{:S(2)}, u32[]{:S(2)}) collective-permute-start(f32[1,16384]{1,0:T(1,128)S(1)} %slice.299), channel_id=1, source_target_pairs={{0,1},{1,2},{2,3},{3,4},{4,5},{5,6},{6,7},{7,8},{8,9},{9,10},{10,1... | collective-permute-start | bytes 196616 | tf_op jit(solution)/shard_map/ppermute | solution.py:26
  145.2 3.4 copy-start.9
  150.1 7.3 %collective-permute-start.4 = (f32[1,16384]{1,0:T(1,128)S(1)}, f32[1,16384]{1,0:T(1,128)S(1)}, u32[]{:S(2)}, u32[]{:S(2)}) collective-permute-start(f32[1,16384]{1,0:T(1,128)S(1)} %slice.315), channel_id=1, source_target_pairs={{0,1},{1,2},{2,3},{3,4},{4,5},{5,6},{6,7},{7,8},{8,9},{9,10},{10,1... | collective-permute-start | bytes 196616 | tf_op jit(solution)/shard_map/ppermute | solution.py:26
  155.4 4.7 collective-permute-start.5
  173.1 12.2 %collective-permute-start.6 = (f32[1,16384]{1,0:T(1,128)}, f32[1,16384]{1,0:T(1,128)}, u32[]{:S(2)}, u32[]{:S(2)}) collective-permute-start(f32[1,16384]{1,0:T(1,128)} %slice.331), channel_id=1, source_target_pairs={{0,1},{1,2},{2,3},{3,4},{4,5},{5,6},{6,7},{7,8},{8,9},{9,10},{10,1... | collective-permute-start | bytes 196616 | tf_op jit(solution)/shard_map/ppermute | solution.py:26
  180.3 5.2 %collective-permute-start.7 = (f32[1,16384]{1,0:T(1,128)}, f32[1,16384]{1,0:T(1,128)}, u32[]{:S(2)}, u32[]{:S(2)}) collective-permute-start(f32[1,16384]{1,0:T(1,128)} %slice.335), channel_id=1, source_target_pairs={{1,0},{2,1},{3,2},{4,3},{5,4},{6,5},{7,6},{8,7},{9,8},{10,9},{11,1... | collective-permute-start | bytes 196616 | tf_op jit(solution)/shard_map/ppermute | solution.py:27
  193.3 14.4 %copy-start.3 = (f32[4,16384]{1,0:T(4,128)}, f32[4,16384]{1,0:T(4,128)S(1)}, u32[]{:S(2)}) copy-start(f32[4,16384]{1,0:T(4,128)S(1)} %reshape.287) | copy-start | bytes 786436
  193.3 14.5 %copy-start.6 = (s32[4]{0:T(128)S(1)}, s32[4]{0:T(128)}, u32[]{:S(2)}) copy-start(s32[4]{0:T(128)} %iota_add_fusion) | copy-start | bytes 52
  207.7 14.0 %copy-start.4 = (f32[4,16384]{1,0:T(4,128)S(1)}, f32[4,16384]{1,0:T(4,128)}, u32[]{:S(2)}) copy-start(f32[4,16384]{1,0:T(4,128)} %param.25) | copy-start | bytes 786436
  207.7 14.0 %copy-start.8 = (f32[4,256]{1,0:T(4,128)S(1)}, f32[4,256]{1,0:T(4,128)}, u32[]{:S(2)}) copy-start(f32[4,256]{1,0:T(4,128)} %get-tuple-element.67) | copy-start | bytes 12292
  207.8 14.0 %copy-start.11 = (f32[64]{0:T(128)S(1)}, f32[64]{0:T(128)}, u32[]{:S(2)}) copy-start(f32[64]{0:T(128)} %copy-done.10) | copy-start | bytes 772
  212.5 285.3 %reduce-scatter.5.cloned.1.call-start = ((), (), s32[]{:S(2)}) async-start(), calls=%async_computation.3 | async-start | bytes 1114112 | tf_op jit(solution)/shard_map/reduce_scatter | solution.py:238
  341.6 17.0 %copy-start.13 = (f32[64]{0:T(128)S(1)}, f32[64]{0:T(128)}, u32[]{:S(2)}) copy-start(f32[64]{0:T(128)} %get-tuple-element.71) | copy-start | bytes 772
  341.6 17.0 %copy-start.14 = (f32[64]{0:T(128)S(1)}, f32[64]{0:T(128)}, u32[]{:S(2)}) copy-start(f32[64]{0:T(128)} %get-tuple-element.72) | copy-start | bytes 772
  341.6 17.0 %copy-start.15 = (f32[64]{0:T(128)S(1)}, f32[64]{0:T(128)}, u32[]{:S(2)}) copy-start(f32[64]{0:T(128)} %get-tuple-element.73) | copy-start | bytes 772
  341.6 17.0 %copy-start.16 = (f32[64]{0:T(128)S(1)}, f32[64]{0:T(128)}, u32[]{:S(2)}) copy-start(f32[64]{0:T(128)} %param.24) | copy-start | bytes 772
  341.6 17.0 %copy-start.17 = (f32[64]{0:T(128)S(1)}, f32[64]{0:T(128)}, u32[]{:S(2)}) copy-start(f32[64]{0:T(128)} %param.23) | copy-start | bytes 772
  431.4 70.5 %copy-start.1 = (bf16[64,64]{1,0:T(8,128)(2,1)S(1)}, bf16[64,64]{1,0:T(8,128)(2,1)}, u32[]{:S(2)}) copy-start(bf16[64,64]{1,0:T(8,128)(2,1)} %param.22) | copy-start | bytes 24580
Sparse Core Ops, SparseCore 0:
  212.6 62.7 reduce-scatter.2
  431.4 54.8 reduce-scatter.4
where the time goes:
time: 519 us; the launch traced here: 509 us
  local copies, waits for them, and re-layouts  148 us (29%)
  other arithmetic  102 us (20%)
  matrix products  84.3 us (16%)
  blocking collectives  79.5 us (15%)
  waiting for transfers between devices  56.2 us (11%)
  starting transfers between devices  24 us (5%)
  between operations  15 us (3%)
    cos x1, other arithmetic, cross_basis(): basis = jnp.stack([jnp.cos(angles), -jnp.sin(angles)], axis=-1)  61.6 us
    psum x1, blocking collectives, body(): grad_point = lax.psum(point_local, 'slab')  58.7 us
    reduce_scatter x1, waiting for transfers between devices, body(): lax.psum_scatter(forward_scale * along_x_forward(columns, cos_local, sin_...  53.2 us
    dot_general x1, matrix products, body(): jnp.dot(point_weight, lifted, preferred_element_type=jnp.float32)  21.8 us
    all_gather x1, blocking collectives, body(): gathered = lax.all_gather(mixed, 'slab', axis=0, tiled=True)  20.8 us
    convert_element_type x1, local copies, waits for them, and re-layouts, cross_basis(): basis.reshape(span_cells * depth_cells, 2 * KY * KZ).astype(jnp.bfloat16)  19.9 us
    ppermute x4, starting transfers between devices, with_halo(): before = lax.ppermute(last, axis, up)  18.5 us
    reshape x1, local copies, waits for them, and re-layouts, body(): spectral.reshape(channels, -1)  17 us
  transfers between devices with their start and end apart: 10, of which 3 were waited for; matrix products, arithmetic and copies ran while one was open for 27% of the time, Pallas kernels for 0%

commit v1 on v0

v1 whole, which is shorter than its diff:
```python
import functools
import math

import jax
import jax.numpy as jnp
import numpy as np
from jax import lax
from jax.experimental import pallas as pl
from jax.experimental.pallas import tpu as pltpu
from jax.sharding import PartitionSpec as P

KX = 16
KY = 16
KZ = 8
STEPS = 4
PROFILES = 8

PEAK_SPEED = 0.6
DIFFUSIVITY = 0.06
CENTRE = 1.1
ZG = 4

HI = lax.Precision.HIGHEST
F32 = jnp.float32
BF16 = jnp.bfloat16


def dot(a, b, precision=None):
    return jnp.dot(a, b, preferred_element_type=F32, precision=precision)


def dot_nt(a, b, precision=None):
    return lax.dot_general(a, b, (((1,), (1,)), ((), ())), preferred_element_type=F32, precision=precision)


def dot_tn(a, b, precision=None):
    return lax.dot_general(a, b, (((0,), (0,)), ((), ())), preferred_element_type=F32, precision=precision)


def tables(span, depth, total_x, devices, local_x):
    half = span // 2
    own_j = KY * KZ // devices
    tab = {}
    lane = np.arange(half)
    perm = np.zeros((half, 4 * half), np.float32)
    for h in range(2):
        for par in range(2):
            k = (h * half + lane - par) / 2.0
            good = (k == np.floor(k)) & (k >= 0)
            perm[lane[good], (2 * h + par) * half + k[good].astype(int)] = 1.0
    tab["perm"] = perm
    back = np.zeros((span, span), np.float32)
    for par in range(2):
        back[par * half + lane, 2 * lane + par] = 1.0
    tab["back"] = back
    ky = np.arange(KY)
    kz = np.arange(KZ)
    kx = np.arange(KX)
    y_of = np.concatenate([2 * lane, 2 * lane + 1])
    alpha = 2 * np.pi * ((y_of[:, None] * ky[None, :]) % span) / span
    tab["wave_y"] = np.concatenate([np.cos(alpha), np.sin(alpha)], axis=1).astype(np.float32)
    z = np.arange(depth)
    beta = 2 * np.pi * ((kz[:, None] * z[None, :]) % depth) / depth
    tab["wave_z"] = np.concatenate([np.cos(beta), np.sin(beta)], axis=0).astype(np.float32)
    pairs = 2 * KY
    ez = np.zeros((2 * KY * KZ, depth, KY, 2), np.float32)
    for j in range(KY * KZ):
        a, b = j // KZ, j % KZ
        row = (j // own_j) * 2 * own_j + j % own_j
        ez[row, :, a, 0] = np.cos(beta[b])
        ez[row + own_j, :, a, 0] = -np.sin(beta[b])
        ez[row, :, a, 1] = -np.sin(beta[b])
        ez[row + own_j, :, a, 1] = -np.cos(beta[b])
    tab["ez"] = ez.reshape(2 * KY * KZ, depth * pairs).astype(jnp.bfloat16)
    by = np.stack([np.cos(alpha), np.sin(alpha)], axis=2).reshape(span, pairs)
    fwd = np.zeros((ZG, ZG * pairs + 16, span), np.float32)
    bwd = np.zeros((ZG, span, ZG * pairs), np.float32)
    for i in range(ZG):
        fwd[i, i * pairs : (i + 1) * pairs] = by.T
        fwd[i, ZG * pairs : ZG * pairs + 2] = 1.0
        bwd[i, :, i * pairs : (i + 1) * pairs] = by
    tab["fwd"] = fwd.astype(jnp.bfloat16)
    tab["bwd"] = bwd.reshape(ZG * span, ZG * pairs).astype(jnp.bfloat16)
    x = np.arange(total_x)
    gamma = 2 * np.pi * ((x[:, None] * kx[None, :]) % total_x) / total_x
    cg, sg = np.cos(gamma), np.sin(gamma)
    scale = 1.0 / math.sqrt(total_x * span * depth)
    ax = np.zeros((total_x, 2, 2, KX))
    ax[:, 0, 0], ax[:, 1, 0] = cg, sg
    ax[:, 0, 1], ax[:, 1, 1] = -sg, cg
    rep = np.repeat(ax[:, :, :, None, :], own_j, axis=3) * scale
    tab["ax"] = rep.reshape(2 * total_x, 2 * own_j * KX).astype(np.float32)
    iscale = 1.0 / math.sqrt(KX * KY * KZ)
    bx = np.zeros((total_x, 2, 2, KX))
    bx[:, 0, 0], bx[:, 0, 1] = cg, -sg
    bx[:, 1, 0], bx[:, 1, 1] = sg, cg
    bx = bx.reshape(devices, local_x, 2, 2 * KX).transpose(1, 0, 2, 3) * iscale
    tab["bx"] = bx.reshape(2 * total_x, 2 * KX).astype(np.float32)
    gx = ax.reshape(devices, local_x, 2, 2 * KX).transpose(1, 3, 0, 2).reshape(local_x, 2 * KX, 2 * devices)
    high = gx.astype(np.float32).astype(jnp.bfloat16)
    low = (gx - high.astype(np.float64)).astype(np.float32).astype(jnp.bfloat16)
    tab["gx"] = np.concatenate([high, low], axis=1)
    return tab


def transport_kernel(
    flags, own, up, down, index, profiles, cot, perm, back, wave_y, wave_z,
    conc_out, cover_out, conc_z, cot_z, cover_z, wave_c, wave_w, buf,
):
    local_x = own.shape[0]
    half = cot.shape[2]
    depth = profiles.shape[1]
    rows = 3 * local_x
    packs = (up, own, down)
    for r in range(rows):
        buf[0, r] = packs[r // local_x][r % local_x, :half, :].T
    walls = jnp.concatenate(
        [packs[r // local_x][r % local_x, half:, :] for r in range(rows)]
        + [jnp.concatenate([index[...], jnp.zeros((6, half), F32)], axis=0)],
        axis=0,
    )
    spread = dot(walls, perm[...], HI)
    fields = [
        spread[8 * r : 8 * r + 4, : 2 * half] + spread[8 * r + 4 : 8 * r + 8, 2 * half :]
        for r in range(rows)
    ]
    chosen = spread[8 * rows : 8 * rows + 1, : 2 * half] + spread[8 * rows + 1 : 8 * rows + 2, 2 * half :]
    pick = lax.broadcasted_iota(jnp.int32, (PROFILES, 2 * half), 0).astype(F32)
    onehot = (jnp.abs(pick - chosen) < 0.5).astype(F32)
    inlet = dot_tn(profiles[...], onehot, HI)
    inlet = jnp.concatenate([inlet[:, :half], inlet[:, half:]], axis=0)
    height = lax.broadcasted_iota(jnp.int32, (depth, half), 0).astype(F32)
    height = (height + 0.5) / depth
    speed = PEAK_SPEED * 4.0 * height * (1.0 - height)
    speed = jnp.concatenate([speed, speed], axis=0)
    first = flags[0] == 1
    last = flags[1] == 1
    cover = [f[0:1] for f in fields]
    for step in range(STEPS):
        cur, nxt = step % 2, (step + 1) % 2
        for r in range(1 + step, rows - 1 - step):
            c = buf[cur, r]
            behind = buf[cur, r - 1]
            ahead = buf[cur, r + 1]
            if r == local_x:
                behind = jnp.where(first, inlet, behind)
            if r == 2 * local_x - 1:
                ahead = jnp.where(last, c, ahead)
            even, odd = c[:depth], c[depth:]
            side = jnp.concatenate(
                [odd + pltpu.roll(odd, 1, 1), even + pltpu.roll(even, half - 1, 1)], axis=0
            )
            below = jnp.concatenate(
                [even[:1], even[:-1], odd[:1], odd[:-1]], axis=0
            )
            above = jnp.concatenate(
                [even[1:], even[-1:], odd[1:], odd[-1:]], axis=0
            )
            laplace = behind + ahead + side + below + above - 6.0 * c
            f = fields[r]
            wall = jnp.concatenate([even[:1], odd[:1]], axis=1)
            uptake = f[3:4] * (f[1:2] * wall * (1.0 - cover[r]) - f[2:3] * cover[r])
            new = c + DIFFUSIVITY * laplace - speed * (c - behind)
            buf[nxt, r] = new
            buf[nxt, r, 0:1] = new[0:1] - uptake[:, :half]
            buf[nxt, r, depth : depth + 1] = new[depth : depth + 1] - uptake[:, half:]
            cover[r] = cover[r] + uptake
    cur = STEPS % 2
    covers = jnp.concatenate(cover[local_x : 2 * local_x], axis=0)
    cover_z[...] = covers
    cover_out[...] = dot(covers, back[...], HI)
    wave_w[...] = dot(covers, wave_y[...], HI)
    planes = [buf[cur, local_x + i] for i in range(local_x)]
    evens = jnp.concatenate([p[:depth] for p in planes], axis=0)
    odds = jnp.concatenate([p[depth:] for p in planes], axis=0)
    along_y = dot(evens, wave_y[:half], HI) + dot(odds, wave_y[half:], HI)
    for i in range(local_x):
        wave_c[i] = dot(wave_z[...], along_y[i * depth : (i + 1) * depth], HI)
        conc_out[i] = planes[i].T
        conc_z[:, i, :] = planes[i]
        cot_z[:, i, :] = cot[i].T


def mixing_kernel(place, waves, ax, bx, lift, weight, inv_out, spec_out, stage):
    modes = weight.shape[3]
    channels = weight.shape[1]
    own_j = modes // KX
    span2 = waves.shape[1]
    local_x = inv_out.shape[1] // channels
    blocks = inv_out.shape[0] // own_j
    spread = dot(waves[...], ax[...], HI)
    mode_j = lax.broadcasted_iota(jnp.int32, (own_j, 2 * modes), 1) % modes // KX
    keep = mode_j == lax.broadcasted_iota(jnp.int32, (own_j, 2 * modes), 0)
    rows = [
        jnp.sum(jnp.where(keep, spread[f * own_j : (f + 1) * own_j], 0.0), axis=0, keepdims=True)
        for f in range(2)
    ]
    lane = lax.broadcasted_iota(jnp.int32, (1, 2 * modes), 1)
    rows.append(jnp.where((lane == 0) & (place[0] == 0), place[1].astype(F32), 0.0))
    fields = jnp.concatenate(rows + [jnp.zeros((5, 2 * modes), F32)], axis=0)
    factors = jnp.concatenate([lift[...], jnp.zeros((5, channels), F32)], axis=0)
    spec = dot_tn(factors, fields, HI)
    spec_r, spec_i = spec[:, :modes], spec[:, modes:]
    spec_out[0] = spec_r
    spec_out[1] = spec_i

    acc_r = jnp.zeros((channels, modes), F32)
    acc_i = jnp.zeros((channels, modes), F32)
    for c in range(channels):
        wr = weight[0, c].astype(F32)
        wi = weight[1, c].astype(F32)
        vr = spec_r[c : c + 1]
        vi = spec_i[c : c + 1]
        acc_r = acc_r + (vr * wr - vi * wi)
        acc_i = acc_i + (vr * wi + vi * wr)
    mixed_r = acc_r.astype(BF16).astype(F32).T
    mixed_i = acc_i.astype(BF16).astype(F32).T
    for j in range(own_j):
        rhs = jnp.concatenate([mixed_r[j * KX : (j + 1) * KX], mixed_i[j * KX : (j + 1) * KX]], axis=0)
        out = dot(bx[...], rhs, HI)
        line = jnp.concatenate([out[i * blocks : (i + 1) * blocks] for i in range(local_x)], axis=1)
        if own_j == 1:
            stage[...] = line
        else:
            for h in range(line.shape[1] // 128):
                stage[h, pl.ds(j, blocks, own_j), :] = line[:, h * 128 : (h + 1) * 128]
    if own_j == 1:
        inv_out[...] = stage[...].astype(BF16)
    else:
        for h in range(stage.shape[0]):
            inv_out[:, h * 128 : (h + 1) * 128] = stage[h].astype(BF16)


def tail_blocks(own_j):
    return -(-3 // (2 * own_j))


def layer_kernel(
    own_j, inv, conc_z, cot_z, cover_z, lift, point_weight, bias, readout, ez, fwd, bwd,
    pred_out, grad_out, lhs, grads, ext_all, waves, pred, point,
):
    channels = lift.shape[1]
    local_x = cover_z.shape[0]
    half = cot_z.shape[2]
    span = 2 * half
    depth = cot_z.shape[0] // 2
    rows = local_x * channels
    wide = ZG * 2 * KY
    iscale = 1.0 / math.sqrt(KX * KY * KZ)

    factors = jnp.concatenate([lift[...], jnp.zeros((5, channels), F32)], axis=0)
    mapped = dot_nt(point_weight[...].astype(F32), factors, HI)
    eye = (
        lax.broadcasted_iota(jnp.int32, (channels, channels), 0)
        == lax.broadcasted_iota(jnp.int32, (channels, channels), 1)
    ).astype(F32)
    columns = dot_nt(eye, jnp.concatenate([bias[...], readout[...], jnp.zeros((6, channels), F32)], axis=0), HI)
    a0, a1 = mapped[:, 0:1], mapped[:, 1:2]
    a2 = mapped[:, 2:3] + columns[:, 0:1] + CENTRE * a0
    half_readout = 0.5 * columns[:, 1:2]

    def high(v):
        return v.astype(BF16).astype(F32)

    lane = lax.broadcasted_iota(jnp.int32, (channels, 32), 1)
    a0_high, a2_high = high(a0), high(a2)
    for x in range(local_x):
        block = jnp.zeros((channels, 32), F32)
        for at, value in (
            (0, a2_high), (1, a2 - a2_high),
            (16 + x, a0_high), (20 + x, a0_high), (24 + x, a0 - a0_high), (28 + x, a1),
        ):
            block = jnp.where(lane == at, value, block)
        block = block.astype(BF16)
        for g in range(depth // ZG):
            lhs[g, x * channels : (x + 1) * channels, wide : wide + 32] = block
    flipped = inv[...].astype(F32).T.astype(BF16)
    lifted = dot(flipped, ez[...]).astype(BF16)
    for g in range(depth // ZG):
        lhs[g, :, :wide] = lifted[:, g * wide : (g + 1) * wide]
    point[...] = jnp.zeros(point.shape, F32)
    scale_rows = jnp.broadcast_to(half_readout, (channels, span))
    c1 = math.sqrt(2.0 / math.pi)
    c2 = c1 * 0.044715

    def group(g, carry):
        for i in range(ZG):
            z = g * ZG + i
            conc = jnp.concatenate([conc_z[z], conc_z[depth + z]], axis=1) - CENTRE
            cot = jnp.concatenate([cot_z[z], cot_z[depth + z]], axis=1)
            conc_high = high(conc)
            wall = jnp.where(z == 0, cover_z[...], 0.0)
            ext = jnp.concatenate([conc_high, conc - conc_high, conc_high, wall], axis=0).astype(BF16)
            ext_all[:, i * span : (i + 1) * span] = ext
            pre = dot(lhs[g], jnp.concatenate([fwd[i], ext], axis=0))
            for x in range(local_x):
                v = pre[x * channels : (x + 1) * channels]
                p = c1 + c2 * (v * v)
                t = jnp.tanh(v * p)
                s = 1.0 + t
                line = jnp.sum(scale_rows * (v * s), axis=0, keepdims=True)
                pred[x, pl.ds(z, 1), :] = line[:, :half]
                pred[x, pl.ds(depth + z, 1), :] = line[:, half:]
                slope = v * (3.0 * p - 2.0 * c1)
                grad = s * (1.0 + slope * (1.0 - t)) * cot[x : x + 1]
                grads[x * channels : (x + 1) * channels, i * span : (i + 1) * span] = grad.astype(BF16)
        waves[g] = dot(grads[...], bwd[...]).astype(BF16)
        point[...] += dot_nt(grads[...], ext_all[...])
        return carry

    lax.fori_loop(0, depth // ZG, group, 0)
    for x in range(local_x):
        pred_out[x] = pred[x].T
    total = jnp.zeros((rows, ez.shape[0]), F32)
    for g in range(depth // ZG):
        total = total + dot_nt(waves[g], ez[:, g * wide : (g + 1) * wide])
    lane16 = lax.broadcasted_iota(jnp.int32, (channels, 16), 1)
    lane128 = lax.broadcasted_iota(jnp.int32, (channels, 128), 1)
    cols = []
    extra = []
    for x in range(local_x):
        here = slice(x * channels, (x + 1) * channels)
        pt = point[here, :]
        with_conc = jnp.sum(jnp.where((lane16 == x) | (lane16 == 4 + x), pt, 0.0), axis=1, keepdims=True)
        with_wall = jnp.sum(jnp.where(lane16 == 12 + x, pt, 0.0), axis=1, keepdims=True)
        alone = total[here, 0:1]
        e = jnp.where(lane128 == 0, with_conc, jnp.where(lane128 == 1, with_wall, jnp.where(lane128 == 2, alone, 0.0)))
        extra.append(half_readout * e)
        cols.append((iscale * half_readout) * total[here])
    sums = extra[0]
    for e in extra[1:]:
        sums = sums + e
    sums = sums.T[:16]
    sums_high = high(sums)
    both = jnp.concatenate([sums_high, sums - sums_high], axis=1).astype(BF16)
    out_rows = grad_out.shape[0]
    grad_out[:, :rows] = jnp.concatenate(cols, axis=0).T.astype(BF16)
    for b in range(tail_blocks(own_j)):
        row = lax.broadcasted_iota(jnp.int32, (out_rows, 16), 0) % (2 * own_j) + b * 2 * own_j
        pick = (row == lax.broadcasted_iota(jnp.int32, (out_rows, 16), 1)).astype(BF16)
        grad_out[:, rows + b * 128 : rows + (b + 1) * 128] = dot(pick, both).astype(BF16)


def outer_kernel(own_j, got, spec, gx, lift, modes_out, point_out, d_r, d_i, stage):
    channels = spec.shape[1]
    modes = spec.shape[2]
    rows = got.shape[1] - 128 * tail_blocks(own_j)
    local_x = rows // channels
    per = modes_out.shape[1]

    @pl.when(pl.program_id(0) == 0)
    def _():
        for h in range(rows // 128):
            stage[h] = got[:, h * 128 : (h + 1) * 128].astype(F32)
        blocks = got.shape[0] // own_j
        parts_r, parts_i = [], []
        for j in range(own_j):
            line = jnp.concatenate(
                [stage[h, pl.ds(j, blocks, own_j), :] if own_j > 1 else stage[h] for h in range(rows // 128)], axis=1
            ).astype(BF16)
            acc = jnp.zeros((4 * KX, channels), F32)
            for x in range(local_x):
                acc = acc + dot(gx[x], line[:, x * channels : (x + 1) * channels])
            acc = acc[: 2 * KX] + acc[2 * KX :]
            parts_r.append(acc[:KX])
            parts_i.append(acc[KX:])
        d_r[...] = jnp.concatenate(parts_r, axis=0).T
        d_i[...] = jnp.concatenate(parts_i, axis=0).T
        sums = jnp.zeros((8, 128), F32)
        for b in range(tail_blocks(own_j)):
            tail = got[:, rows + b * 128 : rows + (b + 1) * 128]
            at = lax.broadcasted_iota(jnp.int32, (8, got.shape[0]), 1) % (2 * own_j) + b * 2 * own_j
            pick = (at == lax.broadcasted_iota(jnp.int32, (8, got.shape[0]), 0)).astype(BF16)
            sums = sums + dot(pick, tail)
        sums = sums[:, :channels] + sums[:, channels:]
        row = lax.broadcasted_iota(jnp.int32, (8, channels), 0)
        base = jnp.concatenate([lift[...], jnp.zeros((5, channels), F32)], axis=0)
        base = jnp.where(row == 2, base + CENTRE * lift[0:1], base)
        point_out[...] = dot_tn(jnp.where(row < 3, sums, 0.0), base, HI)

    start = pl.program_id(0) * per
    dr = d_r[...]
    di = d_i[...]
    for c in range(per):
        vr = spec[0, pl.ds(start + c, 1), :]
        vi = spec[1, pl.ds(start + c, 1), :]
        modes_out[0, c] = vr * dr + vi * di
        modes_out[1, c] = vr * di - vi * dr


def params(**kw):
    return pltpu.CompilerParams(vmem_limit_bytes=56 * 1024 * 1024, **kw)


def vmem(count):
    return [pl.BlockSpec(memory_space=pltpu.VMEM) for _ in range(count)]


def body(
    conc_init, cover_init, rate_on, rate_off, site_mask, inlet_profiles, inlet_index, lift,
    mode_weight, point_weight, point_bias, readout, cotangent,
):
    devices = lax.axis_size("slab")
    position = lax.axis_index("slab")
    local_x, plane = conc_init.shape
    depth = inlet_profiles.shape[1]
    span = plane // depth
    half = span // 2
    channels = lift.shape[1]
    modes = mode_weight.shape[0]
    own_j = modes // KX
    total_x = local_x * devices
    tab = {k: jnp.asarray(v) for k, v in tables(span, depth, total_x, devices, local_x).items()}
    sds = jax.ShapeDtypeStruct
    smem = pl.BlockSpec(memory_space=pltpu.SMEM)

    walls = jnp.stack([cover_init, rate_on, rate_off, site_mask.astype(F32)], axis=1)
    walls = walls.reshape(local_x, 4, 2, half).transpose(0, 2, 1, 3).reshape(local_x, 8, half)
    pack = jnp.concatenate([conc_init.reshape(local_x, half, 2 * depth), walls], axis=1)
    up = lax.ppermute(pack, "slab", [(i, i + 1) for i in range(devices - 1)])
    down = lax.ppermute(pack, "slab", [(i + 1, i) for i in range(devices - 1)])
    flags = jnp.stack([position == 0, position == devices - 1]).astype(jnp.int32)
    index = inlet_index.astype(F32).reshape(2, half)
    conc_out, cover_out, conc_z, cot_z, cover_z, wave_c, wave_w = pl.pallas_call(
        transport_kernel,
        name="transport",
        out_shape=(
            sds((local_x, half, 2 * depth), F32),
            sds((local_x, span), F32),
            sds((2 * depth, local_x, half), F32),
            sds((2 * depth, local_x, half), F32),
            sds((local_x, span), F32),
            sds((local_x, 2 * KZ, 2 * KY), F32),
            sds((local_x, 2 * KY), F32),
        ),
        in_specs=[smem] + vmem(10),
        out_specs=vmem(7),
        scratch_shapes=[pltpu.VMEM((2, 3 * local_x, 2 * depth, half), F32)],
        compiler_params=params(),
    )(
        flags, pack, up, down, index, inlet_profiles, cotangent.reshape(local_x, half, 2 * depth),
        tab["perm"], tab["back"], tab["wave_y"], tab["wave_z"],
    )
    conc_re = wave_c[:, :KZ, :KY] - wave_c[:, KZ:, KY:]
    conc_im = -(wave_c[:, :KZ, KY:] + wave_c[:, KZ:, :KY])
    wall_re = jnp.broadcast_to(wave_w[:, None, :KY], conc_re.shape)
    wall_im = jnp.broadcast_to(-wave_w[:, None, KY:], conc_re.shape)
    send = jnp.stack([conc_re, conc_im, wall_re, wall_im], axis=0)
    send = send.transpose(3, 2, 0, 1).reshape(devices, own_j * 4 * local_x)
    got = lax.all_to_all(send, "slab", 0, 0, tiled=True)
    got = got.reshape(devices, own_j, 2, 2, local_x).transpose(2, 1, 0, 4, 3)
    got = got.reshape(2 * own_j, 2 * total_x)
    ones = math.sqrt(total_x * plane)
    place = jnp.stack([position.astype(F32), jnp.float32(ones)])
    inv, spec = pl.pallas_call(
        mixing_kernel,
        name="mixing",
        out_shape=(
            sds((2 * KY * KZ, local_x * channels), BF16),
            sds((2, channels, modes), F32),
        ),
        in_specs=[smem] + vmem(5),
        out_specs=vmem(2),
        scratch_shapes=[
            pltpu.VMEM((local_x * channels // 128, 2 * KY * KZ, 128), F32)
            if own_j > 1
            else pltpu.VMEM((2 * KY * KZ, local_x * channels), F32)
        ],
        compiler_params=params(),
    )(place, got, tab["ax"], tab["bx"], lift, mode_weight.transpose(1, 2, 3, 0))
    inv = lax.all_to_all(inv, "slab", 0, 0, tiled=True)
    rows = local_x * channels
    wide = ZG * 2 * KY
    pred, grad = pl.pallas_call(
        functools.partial(layer_kernel, own_j),
        name="layer",
        out_shape=(
            sds((local_x, half, 2 * depth), F32),
            sds((2 * KY * KZ, rows + 128 * tail_blocks(own_j)), BF16),
        ),
        in_specs=vmem(11),
        out_specs=vmem(2),
        scratch_shapes=[
            pltpu.VMEM((depth // ZG, rows, wide + 32), BF16),
            pltpu.VMEM((rows, ZG * span), BF16),
            pltpu.VMEM((16, ZG * span), BF16),
            pltpu.VMEM((depth // ZG, rows, wide), BF16),
            pltpu.VMEM((local_x, 2 * depth, half), F32),
            pltpu.VMEM((rows, 16), F32),
        ],
        compiler_params=params(),
    )(
        inv, conc_z, cot_z, cover_z, lift, point_weight, point_bias.reshape(1, -1), readout.reshape(1, -1),
        tab["ez"], tab["fwd"], tab["bwd"],
    )
    grad = lax.all_to_all(grad, "slab", 0, 0, tiled=True)
    blocks = 8
    per = channels // blocks
    whole = lambda s: pl.BlockSpec(s, lambda i: (0,) * len(s))
    grad_modes, grad_point = pl.pallas_call(
        functools.partial(outer_kernel, own_j),
        name="outer",
        grid=(blocks,),
        out_shape=(
            sds((2, channels, channels, modes), F32),
            sds((channels, channels), F32),
        ),
        in_specs=[whole(grad.shape), whole(spec.shape), whole(tab["gx"].shape), whole(lift.shape)],
        out_specs=(
            pl.BlockSpec((2, per, channels, modes), lambda i: (0, i, 0, 0)),
            whole((channels, channels)),
        ),
        scratch_shapes=[
            pltpu.VMEM((channels, modes), F32),
            pltpu.VMEM((channels, modes), F32),
            pltpu.VMEM((rows // 128, 2 * KY * KZ, 128), F32),
        ],
        compiler_params=params(),
    )(grad, spec, tab["gx"], lift)
    return (
        conc_out.reshape(local_x, plane),
        cover_out,
        pred.reshape(local_x, plane),
        grad_modes.transpose(3, 0, 1, 2),
        grad_point,
    )


def solution(mesh):
    placed = (
        P(("groups", "slab"), None),
        P(("groups", "slab"), None),
        P(("groups", "slab"), None),
        P(("groups", "slab"), None),
        P(("groups", "slab"), None),
        P("groups", None),
        P("groups"),
        P(),
        P("slab", None, None, None),
        P(),
        P(),
        P(),
        P(("groups", "slab"), None),
    )
    return jax.shard_map(
        body,
        mesh=mesh,
        in_specs=placed,
        out_specs=(
            P(("groups", "slab"), None),
            P(("groups", "slab"), None),
            P(("groups", "slab"), None),
            P(("groups", "slab"), None, None, None),
            P("groups", None),
        ),
        check_vma=False,
    )
```

time: 519 us -> 94 us (0.18); the launches traced: 509 us -> 93.2 us
  local copies, waits for them, and re-layouts: 148 us -> 10 us
  other arithmetic: 102 us -> 4.89 us
  matrix products: 84.3 us -> 0 us
  blocking collectives: 79.5 us -> 12.1 us
  waiting for transfers between devices: 56.2 us -> 12.6 us
  Pallas kernels: 0 us -> 34.8 us
  between operations: 15 us -> 0.79 us
  starting transfers between devices: 24 us -> 18 us
    dot_general x22 -> x0, matrix products: 84.3 us -> none  [the longest x1 21.8 us: body(): jnp.dot(point_weight, lifted, preferred_element_type=jnp.float32)]
    cos x1 -> x0, other arithmetic: 61.6 us -> none  [cross_basis(): basis = jnp.stack([jnp.cos(angles), -jnp.sin(angles)], axis=-1)]
    psum x1 -> x0, blocking collectives: 58.7 us -> none  [body(): grad_point = lax.psum(point_local, 'slab')]
    reduce_scatter x2 -> x0, waiting for transfers between devices: 53.2 us -> none  [the longest x1 53.2 us: body(): lax.psum_scatter(forward_scale * along_x_forward(columns, cos_local, sin_...]
    convert_element_type x3 -> x0, local copies, waits for them, and re-layouts: 36.4 us -> none  [the longest x1 19.9 us: cross_basis(): basis.reshape(span_cells * depth_cells, 2 * KY * KZ).astype(jnp.bfloat16)]
    pallas_call x0 -> x4, Pallas kernels: none -> 34.8 us  [the longest x1 20.7 us: body(): pl.pallas_call(functools.partial(layer_kernel, own_j), name='layer', out_...]
    slice x32 -> x0, local copies, waits for them, and re-layouts: 32.3 us -> none  [the longest x1 8.55 us: along_x_forward(): real_part = split[..., 0]]
    reshape x8 -> x3, local copies, waits for them, and re-layouts: 30.3 us -> 2.88 us  [the longest x1 2.08 us: body(): pred.reshape(local_x, plane)]
  transfers between devices with their start and end apart: 10 -> 4, of which waited for: 3 -> 2; matrix products, arithmetic and copies ran while one was open for 27% -> 7% of each run, Pallas kernels for 0% -> 0%
where the time goes in v1:
time: 94 us; the launch traced here: 93.2 us
  Pallas kernels  34.8 us (37%)
  starting transfers between devices  18 us (19%)
  waiting for transfers between devices  12.6 us (13%)
  blocking collectives  12.1 us (13%)
  local copies, waits for them, and re-layouts  10 us (11%)
  other arithmetic  4.89 us (5%)
    pallas_call x1, Pallas kernels, body(): pl.pallas_call(functools.partial(layer_kernel, own_j), name='layer', out_...  20.7 us
    all_to_all x1, blocking collectives, body(): inv = lax.all_to_all(inv, 'slab', 0, 0, tiled=True)  12.1 us
    all_to_all x1, starting transfers between devices, body(): got = lax.all_to_all(send, 'slab', 0, 0, tiled=True)  10.2 us
    all_to_all x1, waiting for transfers between devices, body(): grad = lax.all_to_all(grad, 'slab', 0, 0, tiled=True)  6.84 us
    all_to_all x1, waiting for transfers between devices, body(): got = lax.all_to_all(send, 'slab', 0, 0, tiled=True)  5.77 us
    pallas_call x1, Pallas kernels, body(): pl.pallas_call(functools.partial(outer_kernel, own_j), name='outer', grid...  5.31 us
    pallas_call x1, Pallas kernels, body(): pl.pallas_call(transport_kernel, name='transport', out_shape=(sds((local_...  4.6 us
    pallas_call x1, Pallas kernels, body(): pl.pallas_call(mixing_kernel, name='mixing', out_shape=(sds((2 * KY * KZ,...  4.25 us
  transfers between devices with their start and end apart: 4, of which 2 were waited for; matrix products, arithmetic and copies ran while one was open for 7% of the time, Pallas kernels for 0%

profile of v1, /device:TPU:0, one launch (start us, length us, event | category | flops | bytes accessed | tf_op | source)
XLA Modules:
  0.0 93.2 jit_solution(16132906873722528825)
XLA Ops:
  0.6 0.7 stack.42
  1.3 0.7 stack.43
  2.0 0.7 stack.44
  2.7 0.7 convert_element_type.13
  3.4 1.0 %copy.57 = f32[1,4,128,128]{3,2,1,0:T(8,128)S(1)} copy(f32[1,4,128,128]{3,1,2,0:T(4,128)} %bitcast.52) | data formatting | bytes 524288
  4.5 0.0 copy-start
  4.5 1.3 %collective-permute-start.1 = (f32[4,136,128]{2,1,0:T(8,128)S(1)}, f32[4,136,128]{2,1,0:T(8,128)S(1)}, u32[]{:S(2)}, u32[]{:S(2)}) collective-permute-start(f32[4,136,128]{2,1,0:T(8,128)S(1)} %pad_maximum_fusion.own), channel_id=1, source_target_pairs={{1,0},{2,1},{3,2},{4,3},{5,4},{6,5},{7,6},{8,7},{9,8},{10,9},{11,1... | collective-permute-start | bytes 835592 | tf_op jit(solution)/shard_map/ppermute | solution.py:421
  5.8 3.0 %collective-permute-start = (f32[4,136,128]{2,1,0:T(8,128)S(1)}, f32[4,136,128]{2,1,0:T(8,128)S(1)}, u32[]{:S(2)}, u32[]{:S(2)}) collective-permute-start(f32[4,136,128]{2,1,0:T(8,128)S(1)} %pad_maximum_fusion.own), channel_id=1, source_target_pairs={{0,1},{1,2},{2,3},{3,4},{4,5},{5,6},{6,7},{7,8},{8,9},{9,10},{10,1... | collective-permute-start | bytes 835592 | tf_op jit(solution)/shard_map/ppermute | solution.py:420
  8.8 0.6 add_convert_fusion.flags
  9.4 1.7 %copy.56 = f32[1,4,128,128]{3,2,1,0:T(8,128)} copy(f32[1,4,128,128]{3,1,2,0:T(4,128)} %bitcast.53) | data formatting | bytes 524288
  11.1 1.3 %convert_bitcast_fusion.index = f32[2,128]{1,0:T(2,128)} fusion(s32[256]{0:T(256)} %param.29), kind=kLoop, calls=%fused_computation.11 | loop fusion | flops 256 | bytes 2048 | tf_op jit(solution)/shard_map/reshape | solution.py:423
  12.4 0.0 collective-permute-done.1.down
  12.4 0.0 copy-start.2
  12.4 0.0 collective-permute-done.up
  12.4 0.0 copy-start.3
  12.4 0.0 copy-done
  12.4 0.7 copy-done.2
  13.1 0.1 copy-done.3
  13.2 4.6 %transport.1 = (f32[4,128,128]{2,1,0:T(8,128)}, f32[4,256]{1,0:T(4,128)}, f32[128,4,128]{2,1,0:T(4,128)}, f32[128,4,128]{2,1,0:T(4,128)}, f32[4,256]{1,0:T(4,128...) custom-call(s32[2]{0:T(128)} %add_convert_fusion.flags, f32[4,136,128]{2,1,0:T(8,128)} %copy-done, f32[4,136,128]{2,1,0:T(8,128)} %copy-done.3, ...), custom_call_target="tpu_custom_call" | custom-call | tf_op jit(solution)/shard_map/transport/pallas_call | solution.py:424
  17.8 0.0 copy-start.4
  17.8 0.8 fusion
  18.6 0.9 subtract_bitcast_fusion
  19.6 0.7 copy.44
  20.2 10.2 %all-to-all-start = ((f32[16,1,128]{2,1,0:T(1,128)}), f32[16,1,128]{2,1,0:T(1,128)S(1)}, u32[]{:S(2)}, u32[]{:S(2)}) async-start(f32[16,1,128]{2,1,0:T(1,128)} %copy.44), calls=%async_computation | async-start | bytes 16384 | tf_op jit(solution)/shard_map/all_to_all | solution.py:450
  30.4 0.6 pad_maximum_fusion.2.place
  31.0 5.8 %all-to-all-done = f32[16,1,128]{2,1,0:T(1,128)S(1)} async-done(((f32[16,1,128]{2,1,0:T(1,128)}), f32[16,1,128]{2,1,0:T(1,128)S(1)}, u32[]{:S(2)}, u32[]{:S(2)}) %all-to-all-start) | async-done | bytes 8224 | tf_op jit(solution)/shard_map/all_to_all | solution.py:450
  36.8 0.1 copy.45
  36.9 0.2 copy.46
  37.0 0.1 reshape.70
  37.2 0.7 copy.47.waves
  37.8 4.2 %mixing.1 = (bf16[256,256]{1,0:T(8,128)(2,1)}, f32[2,64,128]{2,1,0:T(8,128)}) custom-call(f32[2]{0:T(128)} %pad_maximum_fusion.2.place, f32[16,128]{1,0:T(8,128)} %copy.47.waves, f32[128,256]{1,0:T(8,128)} %constant.37.clone.ax, f32[128,32]{1,0:T(8,128)} %constant.38.clone.bx, f32[3,64]{1,0:T(4,128)} %lift.5, bf16[2,64,64,128]{3,2,1,0:T(8,128)(2,1)} %bitcast.46), custom_call_target="tpu_custom_call" | custom-call | tf_op jit(solution)/shard_map/mixing/pallas_call | solution.py:455
  42.1 12.1 %all_to_all.31 = bf16[16,16,256]{2,1,0:T(8,128)(2,1)} all-to-all(bf16[16,16,256]{2,1,0:T(8,128)(2,1)} %bitcast.58), channel_id=1, replica_groups=mesh['groups'=2,'slab'=16] {'slab'}, dimensions={0} | all-to-all | bytes 262144 | tf_op jit(solution)/shard_map/all_to_all | solution.py:471
  54.1 20.7 %layer.1 = (f32[4,128,128]{2,1,0:T(8,128)}, bf16[256,384]{1,0:T(8,128)(2,1)}) custom-call(bf16[256,256]{1,0:T(8,128)(2,1)} %bitcast.50, f32[128,4,128]{2,1,0:T(4,128)} %get-tuple-element.23.conc_z, f32[128,4,128]{2,1,0:T(4,128)} %get-tuple-element.24.cot_z, f32[4,256]{1,0:T(4,128)} %get-tuple-element.25.cover_z, f32[3,64]{1,0:T(4,128)} %lift.5, ...), custom_call_target="tpu_custom_call" | custom-call | tf_op jit(solution)/shard_map/layer/pallas_call | solution.py:474
  74.8 3.5 %all-to-all-start.2 = ((bf16[16,16,384]{2,1,0:T(8,128)(2,1)}), bf16[16,16,384]{2,1,0:T(8,128)(2,1)S(1)}, u32[]{:S(2)}, u32[]{:S(2)}) async-start(bf16[16,16,384]{2,1,0:T(8,128)(2,1)} %bitcast.57), calls=%async_computation.2 | async-start | bytes 393216 | tf_op jit(solution)/shard_map/all_to_all | solution.py:496
  78.3 0.0 copy-done.4
  78.3 2.1 %copy_bitcast_fusion = (f32[4,16384]{1,0:T(4,128)}, f32[4,16384]{1,0:T(4,128)}) fusion(f32[1,4,128,128]{3,2,1,0:T(8,128)} %bitcast.56, f32[1,4,128,128]{3,2,1,0:T(8,128)S(1)} %bitcast.55), kind=kLoop, calls=%fused_computation.1 | loop fusion | bytes 1048576 | tf_op jit(solution)/shard_map/reshape | solution.py:523
  80.4 6.8 %all-to-all-done.2 = bf16[16,16,384]{2,1,0:T(8,128)(2,1)S(1)} async-done(((bf16[16,16,384]{2,1,0:T(8,128)(2,1)}), bf16[16,16,384]{2,1,0:T(8,128)(2,1)S(1)}, u32[]{:S(2)}, u32[]{:S(2)}) %all-to-all-start.2) | async-done | bytes 196640 | tf_op jit(solution)/shard_map/all_to_all | solution.py:496
  87.3 0.0 copy-start.1
  87.3 0.7 copy-done.1
  87.9 5.3 %outer.1 = (f32[2,64,64,128]{3,2,1,0:T(8,128)}, f32[64,64]{1,0:T(8,128)}) custom-call(bf16[256,384]{1,0:T(8,128)(2,1)} %bitcast.49, f32[2,64,128]{2,1,0:T(8,128)} %get-tuple-element.28.spec, bf16[4,64,32]{2,1,0:T(8,128)(2,1)} %constant.39.clone.gx, f32[3,64]{1,0:T(4,128)} %lift.5), custom_call_target="tpu_custom_call" | custom-call | tf_op jit(solution)/shard_map/outer/pallas_call | solution.py:500
  (7 shorter events, 0.1 us)
Async XLA Ops:
  4.5 7.9 %copy-start = (f32[4,136,128]{2,1,0:T(8,128)}, f32[4,136,128]{2,1,0:T(8,128)S(1)}, u32[]{:S(2)}) copy-start(f32[4,136,128]{2,1,0:T(8,128)S(1)} %pad_maximum_fusion.own) | copy-start | bytes 835588
  4.5 7.9 %collective-permute-start.1 = (f32[4,136,128]{2,1,0:T(8,128)S(1)}, f32[4,136,128]{2,1,0:T(8,128)S(1)}, u32[]{:S(2)}, u32[]{:S(2)}) collective-permute-start(f32[4,136,128]{2,1,0:T(8,128)S(1)} %pad_maximum_fusion.own), channel_id=1, source_target_pairs={{1,0},{2,1},{3,2},{4,3},{5,4},{6,5},{7,6},{8,7},{9,8},{10,9},{11,1... | collective-permute-start | bytes 835592 | tf_op jit(solution)/shard_map/ppermute | solution.py:421
  5.8 6.6 %collective-permute-start = (f32[4,136,128]{2,1,0:T(8,128)S(1)}, f32[4,136,128]{2,1,0:T(8,128)S(1)}, u32[]{:S(2)}, u32[]{:S(2)}) collective-permute-start(f32[4,136,128]{2,1,0:T(8,128)S(1)} %pad_maximum_fusion.own), channel_id=1, source_target_pairs={{0,1},{1,2},{2,3},{3,4},{4,5},{5,6},{6,7},{7,8},{8,9},{9,10},{10,1... | collective-permute-start | bytes 835592 | tf_op jit(solution)/shard_map/ppermute | solution.py:420
  12.4 0.7 copy-start.2
  12.4 0.8 copy-start.3
  17.8 60.5 %copy-start.4 = (f32[4,128,128]{2,1,0:T(8,128)S(1)}, f32[4,128,128]{2,1,0:T(8,128)}, u32[]{:S(2)}) copy-start(f32[4,128,128]{2,1,0:T(8,128)} %get-tuple-element.18) | copy-start | bytes 786436
  20.2 16.5 %all-to-all-start = ((f32[16,1,128]{2,1,0:T(1,128)}), f32[16,1,128]{2,1,0:T(1,128)S(1)}, u32[]{:S(2)}, u32[]{:S(2)}) async-start(f32[16,1,128]{2,1,0:T(1,128)} %copy.44), calls=%async_computation | async-start | bytes 16384 | tf_op jit(solution)/shard_map/all_to_all | solution.py:450
  74.8 12.5 %all-to-all-start.2 = ((bf16[16,16,384]{2,1,0:T(8,128)(2,1)}), bf16[16,16,384]{2,1,0:T(8,128)(2,1)S(1)}, u32[]{:S(2)}, u32[]{:S(2)}) async-start(bf16[16,16,384]{2,1,0:T(8,128)(2,1)} %bitcast.57), calls=%async_computation.2 | async-start | bytes 393216 | tf_op jit(solution)/shard_map/all_to_all | solution.py:496
  87.3 0.7 copy-start.1

commit v2 on v1

v2 whole, which is shorter than its diff:
```python
import functools
import math

import jax
import jax.numpy as jnp
import numpy as np
from jax import lax
from jax.experimental import pallas as pl
from jax.experimental.pallas import tpu as pltpu
from jax.sharding import PartitionSpec as P

KX = 16
KY = 16
KZ = 8
STEPS = 4
PROFILES = 8

PEAK_SPEED = 0.6
DIFFUSIVITY = 0.06
CENTRE = 1.1
ZG = 4

HI = lax.Precision.HIGHEST
F32 = jnp.float32
BF16 = jnp.bfloat16


def dot(a, b, precision=None):
    return jnp.dot(a, b, preferred_element_type=F32, precision=precision)


def dot_nt(a, b, precision=None):
    return lax.dot_general(a, b, (((1,), (1,)), ((), ())), preferred_element_type=F32, precision=precision)


def dot_tn(a, b, precision=None):
    return lax.dot_general(a, b, (((0,), (0,)), ((), ())), preferred_element_type=F32, precision=precision)


def split(table):
    high = table.astype(np.float32).astype(jnp.bfloat16)
    return high, (table - high.astype(np.float64)).astype(np.float32).astype(jnp.bfloat16)


def tables(span, depth, total_x, devices, local_x):
    half = span // 2
    own_j = KY * KZ // devices
    tab = {}
    lane = np.arange(half)
    perm = np.zeros((half, 4 * half), np.float32)
    for h in range(2):
        for par in range(2):
            k = (h * half + lane - par) / 2.0
            good = (k == np.floor(k)) & (k >= 0)
            perm[lane[good], (2 * h + par) * half + k[good].astype(int)] = 1.0
    tab["perm"] = perm
    back = np.zeros((span, span), np.float32)
    for par in range(2):
        back[par * half + lane, 2 * lane + par] = 1.0
    tab["back"] = back
    ky = np.arange(KY)
    kz = np.arange(KZ)
    kx = np.arange(KX)
    y_of = np.concatenate([2 * lane, 2 * lane + 1])
    alpha = 2 * np.pi * ((y_of[:, None] * ky[None, :]) % span) / span
    tab["wave_yt"] = np.concatenate([np.cos(alpha), np.sin(alpha)], axis=1).T.astype(np.float32)
    z = np.arange(depth)
    beta = 2 * np.pi * ((kz[:, None] * z[None, :]) % depth) / depth
    place_c = np.zeros((2, local_x, depth, 2, 2, local_x, KZ), np.float32)
    place_w = np.zeros((2, 8, 2, 2, local_x, KZ), np.float32)
    for i in range(local_x):
        place_c[0, i, :, 0, 0, i] = np.cos(beta).T
        place_c[1, i, :, 0, 0, i] = -np.sin(beta).T
        place_c[0, i, :, 0, 1, i] = -np.sin(beta).T
        place_c[1, i, :, 0, 1, i] = -np.cos(beta).T
        place_w[0, i, 1, 0, i] = 1.0
        place_w[1, i, 1, 1, i] = -1.0
    tab["place_c"] = place_c.reshape(2, local_x * depth, 4 * local_x * KZ)
    tab["place_w"] = place_w.reshape(2, 8, 4 * local_x * KZ)
    pairs = 2 * KY
    ez = np.zeros((2 * KY * KZ, depth, KY, 2), np.float32)
    for j in range(KY * KZ):
        a, b = j // KZ, j % KZ
        row = (j // own_j) * 2 * own_j + j % own_j
        ez[row, :, a, 0] = np.cos(beta[b])
        ez[row + own_j, :, a, 0] = -np.sin(beta[b])
        ez[row, :, a, 1] = -np.sin(beta[b])
        ez[row + own_j, :, a, 1] = -np.cos(beta[b])
    tab["ez"] = ez.reshape(2 * KY * KZ, depth * pairs).astype(jnp.bfloat16)
    by = np.stack([np.cos(alpha), np.sin(alpha)], axis=2).reshape(span, pairs)
    fwd = np.zeros((ZG, ZG * pairs + 16, span), np.float32)
    bwd = np.zeros((ZG, span, ZG * pairs), np.float32)
    for i in range(ZG):
        fwd[i, i * pairs : (i + 1) * pairs] = by.T
        fwd[i, ZG * pairs : ZG * pairs + 2] = 1.0
        bwd[i, :, i * pairs : (i + 1) * pairs] = by
    tab["fwd"] = fwd.astype(jnp.bfloat16)
    tab["bwd"] = bwd.reshape(ZG * span, ZG * pairs).astype(jnp.bfloat16)
    x = np.arange(total_x)
    gamma = 2 * np.pi * ((x[:, None] * kx[None, :]) % total_x) / total_x
    cg, sg = np.cos(gamma), np.sin(gamma)
    scale = 1.0 / math.sqrt(total_x * span * depth)
    ax = np.zeros((total_x, 2, 2, KX))
    ax[:, 0, 0], ax[:, 1, 0] = cg, sg
    ax[:, 0, 1], ax[:, 1, 1] = -sg, cg
    by_owner = ax.reshape(devices, local_x, 2, 2 * KX)
    tab["ax"] = (by_owner.transpose(0, 2, 1, 3) * scale).reshape(devices, -1).astype(np.float32)
    iscale = 1.0 / math.sqrt(KX * KY * KZ)
    bx = np.zeros((total_x, 2, 2, KX))
    bx[:, 0, 0], bx[:, 0, 1] = cg, -sg
    bx[:, 1, 0], bx[:, 1, 1] = sg, cg
    bx = bx.reshape(devices, local_x, 2, 2 * KX).transpose(1, 0, 2, 3) * iscale
    tab["bx"] = np.stack(split(bx.reshape(2 * total_x, 2 * KX)))
    gx = by_owner.transpose(3, 1, 0, 2).reshape(2 * KX, 2 * total_x)
    tab["gx"] = np.concatenate(split(gx), axis=0)
    return tab


def pack_kernel(conc, cover, rate_on, rate_off, mask, packed, conc_out, walls_out):
    local_x = conc.shape[0]
    half = conc_out.shape[1]
    for k in range(half):
        conc_out[:, k, :] = conc[:, k * 128 : (k + 1) * 128]
    for f, ref in enumerate((cover, rate_on, rate_off, mask)):
        for h in range(2):
            walls_out[:, h * 4 + f, :] = ref[:, h * half : (h + 1) * half].astype(F32)
    for x in range(local_x):
        packed[x, :half, :] = (conc_out[x] - CENTRE).astype(BF16)
        tail = jnp.concatenate([walls_out[x], jnp.zeros((8, half), F32)], axis=0)
        packed[x, half:, :] = tail.astype(BF16)


def prepare_kernel(cot, lift, weight, cot_z, mapped, flat):
    local_x = cot.shape[0]
    half = flat.shape[1]
    for k in range(half):
        flat[:, k, :] = cot[:, k * 128 : (k + 1) * 128]
    for x in range(local_x):
        cot_z[:, x, :] = flat[x].T
    channels = weight.shape[1]
    for p in range(2):
        acc = [jnp.zeros(weight.shape[2:], F32) for _ in range(3)]
        for c in range(channels):
            w = weight[p, c].astype(F32)
            acc = [acc[r] + lift[r, c] * w for r in range(3)]
        for r in range(3):
            mapped[r, p] = acc[r]


def transport_kernel(
    flags, own, own_walls, up, down, index, profiles, perm, back, wave_yt, place_c, place_w,
    conc_out, cover_out, conc_z, cover_z, send, buf,
):
    local_x = own.shape[0]
    half = own.shape[1]
    depth = profiles.shape[1]
    rows = 3 * local_x
    walls = []
    for r in range(rows):
        x = r % local_x
        if r // local_x == 1:
            buf[0, r] = own[x].T
            walls.append(own_walls[x])
        else:
            ref = up if r < local_x else down
            buf[0, r] = (ref[x, :half, :].astype(F32) + CENTRE).T
            walls.append(ref[x, half:, :].astype(F32)[:8])
    walls.append(jnp.concatenate([index[...], jnp.zeros((6, half), F32)], axis=0))
    spread = dot(jnp.concatenate(walls, axis=0), perm[...], HI)
    fields = [
        spread[8 * r : 8 * r + 4, : 2 * half] + spread[8 * r + 4 : 8 * r + 8, 2 * half :]
        for r in range(rows)
    ]
    chosen = spread[8 * rows : 8 * rows + 1, : 2 * half] + spread[8 * rows + 1 : 8 * rows + 2, 2 * half :]
    pick = lax.broadcasted_iota(jnp.int32, (PROFILES, 2 * half), 0).astype(F32)
    onehot = (jnp.abs(pick - chosen) < 0.5).astype(F32)
    inlet = dot_tn(profiles[...], onehot, HI)
    inlet = jnp.concatenate([inlet[:, :half], inlet[:, half:]], axis=0)
    height = lax.broadcasted_iota(jnp.int32, (depth, half), 0).astype(F32)
    height = (height + 0.5) / depth
    speed = PEAK_SPEED * 4.0 * height * (1.0 - height)
    speed = jnp.concatenate([speed, speed], axis=0)
    first = flags[0] == 1
    last = flags[1] == 1
    cover = [f[0:1] for f in fields]
    for step in range(STEPS):
        cur, nxt = step % 2, (step + 1) % 2
        for r in range(1 + step, rows - 1 - step):
            c = buf[cur, r]
            behind = buf[cur, r - 1]
            ahead = buf[cur, r + 1]
            if r == local_x:
                behind = jnp.where(first, inlet, behind)
            if r == 2 * local_x - 1:
                ahead = jnp.where(last, c, ahead)
            even, odd = c[:depth], c[depth:]
            side = jnp.concatenate(
                [odd + pltpu.roll(odd, 1, 1), even + pltpu.roll(even, half - 1, 1)], axis=0
            )
            below = jnp.concatenate([even[:1], even[:-1], odd[:1], odd[:-1]], axis=0)
            above = jnp.concatenate([even[1:], even[-1:], odd[1:], odd[-1:]], axis=0)
            laplace = behind + ahead + side + below + above - 6.0 * c
            f = fields[r]
            wall = jnp.concatenate([even[:1], odd[:1]], axis=1)
            uptake = f[3:4] * (f[1:2] * wall * (1.0 - cover[r]) - f[2:3] * cover[r])
            new = c + DIFFUSIVITY * laplace - speed * (c - behind)
            buf[nxt, r] = new
            buf[nxt, r, 0:1] = new[0:1] - uptake[:, :half]
            buf[nxt, r, depth : depth + 1] = new[depth : depth + 1] - uptake[:, half:]
            cover[r] = cover[r] + uptake
    cur = STEPS % 2
    covers = jnp.concatenate(cover[local_x : 2 * local_x], axis=0)
    cover_z[...] = covers
    planes = [buf[cur, local_x + i] for i in range(local_x)]
    evens = jnp.concatenate([p[:depth] for p in planes], axis=0)
    odds = jnp.concatenate([p[depth:] for p in planes], axis=0)
    along = dot_nt(wave_yt[:, :half], evens, HI) + dot_nt(wave_yt[:, half:], odds, HI)
    padded = jnp.concatenate([covers, jnp.zeros((8 - local_x, 2 * half), F32)], axis=0)
    walls_y = dot_nt(wave_yt[...], padded, HI)
    send[...] = (
        dot(along[:KY], place_c[0], HI)
        + dot(along[KY:], place_c[1], HI)
        + dot(walls_y[:KY], place_w[0], HI)
        + dot(walls_y[KY:], place_w[1], HI)
    )
    cover_out[...] = dot(covers, back[...], HI)
    for i in range(local_x):
        conc_out[i] = planes[i].T
        conc_z[:, i, :] = planes[i]


def mixing_kernel(place, got, ax, bx, mapped, inv_out, spec_out, stage):
    modes = mapped.shape[3]
    channels = mapped.shape[2]
    own_j = modes // KX
    local_x = inv_out.shape[1] // channels
    blocks = inv_out.shape[0] // own_j
    spread = dot_tn(got[...], ax[...], HI)
    keep = lax.broadcasted_iota(jnp.int32, (own_j, modes), 1) // KX == lax.broadcasted_iota(
        jnp.int32, (own_j, modes), 0
    )
    spec = []
    for f in range(2):
        acc = jnp.zeros((own_j, 2 * KX), F32)
        for k in range(2 * local_x):
            at = (f * 2 * local_x + k) * own_j
            acc = acc + spread[at : at + own_j, k * 2 * KX : (k + 1) * 2 * KX]
        for q in range(2):
            tiled = jnp.concatenate([acc[:, q * KX : (q + 1) * KX]] * own_j, axis=1)
            spec.append(jnp.sum(jnp.where(keep, tiled, 0.0), axis=0, keepdims=True))
    cr, ci, wr, wi = spec
    lane = lax.broadcasted_iota(jnp.int32, (1, modes), 1)
    ones = jnp.where((lane == 0) & (place[0] == 0.0), place[1], 0.0)
    zero = jnp.zeros((1, modes), F32)
    spec_out[:, :modes] = jnp.concatenate([cr, wr, ones] + [zero] * 5, axis=0)
    spec_out[:, modes:] = jnp.concatenate([ci, wi] + [zero] * 6, axis=0)
    mixed_r = cr * mapped[0, 0] - ci * mapped[0, 1] + wr * mapped[1, 0] - wi * mapped[1, 1] + ones * mapped[2, 0]
    mixed_i = cr * mapped[0, 1] + ci * mapped[0, 0] + wr * mapped[1, 1] + wi * mapped[1, 0] + ones * mapped[2, 1]
    mixed_r = mixed_r.astype(BF16).astype(F32).T
    mixed_i = mixed_i.astype(BF16).astype(F32).T
    for j in range(own_j):
        rhs = jnp.concatenate([mixed_r[j * KX : (j + 1) * KX], mixed_i[j * KX : (j + 1) * KX]], axis=0)
        rhs = rhs.astype(BF16)
        out = dot(bx[0], rhs) + dot(bx[1], rhs)
        line = jnp.concatenate([out[i * blocks : (i + 1) * blocks] for i in range(local_x)], axis=1)
        for h in range(line.shape[1] // 128):
            if own_j == 1:
                stage[h] = line[:, h * 128 : (h + 1) * 128]
            else:
                stage[h, pl.ds(j, blocks, own_j), :] = line[:, h * 128 : (h + 1) * 128]
    for h in range(stage.shape[0]):
        inv_out[:, h * 128 : (h + 1) * 128] = stage[h].astype(BF16)


def tail_blocks(own_j):
    return -(-3 // (2 * own_j))


def layer_kernel(
    own_j, inv, conc_z, cot_z, cover_z, lift, point_weight, bias, readout, ez, fwd, bwd,
    pred_out, grad_out, lhs, grads_a, grads_b, ext_a, ext_b, waves, pred, point, ahead,
):
    channels = lift.shape[1]
    local_x = cover_z.shape[0]
    half = cot_z.shape[2]
    span = 2 * half
    depth = cot_z.shape[0] // 2
    groups = depth // ZG
    rows = local_x * channels
    wide = ZG * 2 * KY
    iscale = 1.0 / math.sqrt(KX * KY * KZ)
    c1 = math.sqrt(2.0 / math.pi)
    unit = (c1 * 0.044715) ** (1.0 / 3.0)
    kappa = c1 / unit

    def high(v):
        return v.astype(BF16).astype(F32)

    factors = jnp.concatenate([lift[...], jnp.zeros((5, channels), F32)], axis=0)
    mapped = dot_nt(point_weight[...].astype(F32), factors, HI)
    eye = (
        lax.broadcasted_iota(jnp.int32, (channels, channels), 0)
        == lax.broadcasted_iota(jnp.int32, (channels, channels), 1)
    ).astype(F32)
    columns = dot_nt(eye, jnp.concatenate([bias[...], readout[...], jnp.zeros((6, channels), F32)], axis=0), HI)
    a0, a1 = unit * mapped[:, 0:1], unit * mapped[:, 1:2]
    a2 = unit * (mapped[:, 2:3] + columns[:, 0:1]) + CENTRE * a0
    half_readout = 0.5 * columns[:, 1:2]

    lane = lax.broadcasted_iota(jnp.int32, (channels, 32), 1)
    a0_high, a2_high = high(a0), high(a2)
    for x in range(local_x):
        block = jnp.zeros((channels, 32), F32)
        for at, value in (
            (0, a2_high), (1, a2 - a2_high),
            (16 + x, a0_high), (20 + x, a0_high), (24 + x, a0 - a0_high), (28 + x, a1),
        ):
            block = jnp.where(lane == at, value, block)
        block = block.astype(BF16)
        for g in range(groups):
            lhs[g, x * channels : (x + 1) * channels, wide : wide + 32] = block
    flipped = inv[...].astype(F32).T.astype(BF16)
    lifted = (unit * dot(flipped, ez[...])).astype(BF16)
    for g in range(groups):
        lhs[g, :, :wide] = lifted[:, g * wide : (g + 1) * wide]
    wide_readout = jnp.concatenate([(0.5 / unit) * readout[...]] * local_x, axis=1)
    owner = lax.broadcasted_iota(jnp.int32, (16, rows), 1) // channels
    slot = lax.broadcasted_iota(jnp.int32, (16, rows), 0)
    readout_high = high(wide_readout)
    weigh = jnp.where(
        slot == owner, readout_high, jnp.where(slot - 8 == owner, wide_readout - readout_high, 0.0)
    ).astype(BF16)
    point[...] = jnp.zeros(point.shape, F32)
    grads_b[...] = jnp.zeros(grads_b.shape, BF16)
    ext_b[...] = jnp.zeros(ext_b.shape, BF16)

    def before(g, i, ext_ref):
        z = g * ZG + i
        conc = jnp.concatenate([conc_z[z], conc_z[depth + z]], axis=1) - CENTRE
        conc_high = high(conc)
        wall = jnp.where(z == 0, cover_z[...], 0.0)
        ext = jnp.concatenate([conc_high, conc - conc_high, conc_high, wall], axis=0).astype(BF16)
        ext_ref[:, i * span : (i + 1) * span] = ext
        return dot(lhs[g], jnp.concatenate([fwd[i], ext], axis=0))

    def collect(at, grads, ext):
        waves[:, pl.ds(pl.multiple_of(at * wide, wide), wide)] = dot(grads[...], bwd[...]).astype(BF16)
        point[...] += dot_nt(grads[...], ext[...])

    def group(g, grads, ext, grads_other, ext_other):
        collect(jnp.maximum(g - 1, 0), grads_other, ext_other)
        for i in range(ZG):
            pre = ahead[...] if i == 0 else nxt
            if i < ZG - 1:
                nxt = before(g, i + 1, ext)
            else:
                nxt = before(jnp.minimum(g + 1, groups - 1), 0, ext_other)
            z = g * ZG + i
            cot = jnp.concatenate([cot_z[z], cot_z[depth + z]], axis=1)
            hidden = []
            for x in range(local_x):
                y = pre[x * channels : (x + 1) * channels]
                p = y * y + kappa
                t = jnp.tanh(y * p)
                s = 1.0 + t
                hidden.append((y * s).astype(BF16))
                slope = y * (3.0 * p - 2.0 * kappa)
                grad = s * (1.0 + slope * (1.0 - t)) * cot[x : x + 1]
                grads[x * channels : (x + 1) * channels, i * span : (i + 1) * span] = grad.astype(BF16)
            line = dot(weigh, jnp.concatenate(hidden, axis=0))
            line = line[:local_x] + line[8 : 8 + local_x]
            pred[z] = line[:, :half]
            pred[depth + z] = line[:, half:]
        ahead[...] = nxt

    ahead[...] = before(0, 0, ext_a)

    def pair(h, carry):
        group(2 * h, grads_a, ext_a, grads_b, ext_b)
        group(2 * h + 1, grads_b, ext_b, grads_a, ext_a)
        return carry

    lax.fori_loop(0, groups // 2, pair, 0)
    collect(groups - 1, grads_b, ext_b)
    for x in range(local_x):
        pred_out[x] = pred[:, x, :].T
    total = dot_nt(waves[...], ez[...])
    lane16 = lax.broadcasted_iota(jnp.int32, (channels, 16), 1)
    lane128 = lax.broadcasted_iota(jnp.int32, (channels, 128), 1)
    cols = []
    sums = jnp.zeros((channels, 128), F32)
    for x in range(local_x):
        here = slice(x * channels, (x + 1) * channels)
        pt = point[here, :]
        with_conc = jnp.sum(jnp.where((lane16 == x) | (lane16 == 4 + x), pt, 0.0), axis=1, keepdims=True)
        with_wall = jnp.sum(jnp.where(lane16 == 12 + x, pt, 0.0), axis=1, keepdims=True)
        alone = total[here, 0:1]
        sums = sums + jnp.where(
            lane128 == 0, with_conc, jnp.where(lane128 == 1, with_wall, jnp.where(lane128 == 2, alone, 0.0))
        )
        cols.append((iscale * half_readout) * total[here])
    sums = (half_readout * sums).T[:16]
    sums_high = high(sums)
    both = jnp.concatenate([sums_high, sums - sums_high], axis=1).astype(BF16)
    out_rows = grad_out.shape[0]
    grad_out[:, :rows] = jnp.concatenate(cols, axis=0).T.astype(BF16)
    for b in range(tail_blocks(own_j)):
        row = lax.broadcasted_iota(jnp.int32, (out_rows, 16), 0) % (2 * own_j) + b * 2 * own_j
        pick = (row == lax.broadcasted_iota(jnp.int32, (out_rows, 16), 1)).astype(BF16)
        grad_out[:, rows + b * 128 : rows + (b + 1) * 128] = dot(pick, both).astype(BF16)


def outer_kernel(own_j, got, spec, gx, lift, modes_out, point_out, v_r, v_i, d_r, d_i, stage):
    channels = lift.shape[1]
    modes = spec.shape[1] // 2
    rows = got.shape[1] - 128 * tail_blocks(own_j)
    local_x = rows // channels
    per = modes_out.shape[1]

    @pl.when(pl.program_id(0) == 0)
    def _():
        factors = jnp.concatenate([lift[...], jnp.zeros((5, channels), F32)], axis=0)
        v = dot_tn(factors, spec[...], HI)
        v_r[...] = v[:, :modes]
        v_i[...] = v[:, modes:]
        blocks = got.shape[0] // own_j
        halves = rows // 128
        for h in range(halves):
            stage[h] = got[:, h * 128 : (h + 1) * 128].astype(F32)
        lines = [
            [stage[h, pl.ds(j, blocks, own_j), :] if own_j > 1 else stage[h] for h in range(halves)]
            for j in range(own_j)
        ]
        per_half = 128 // channels
        parts_r, parts_i = [], []
        tall = []
        for x in range(local_x):
            h, at = x // per_half, (x % per_half) * channels
            tall.append(jnp.concatenate([lines[j][h][:, at : at + channels] for j in range(own_j)], axis=1))
        acc = dot(gx[...], jnp.concatenate(tall, axis=0).astype(BF16))
        acc = acc[: 2 * KX] + acc[2 * KX :]
        for j in range(own_j):
            parts_r.append(acc[:KX, j * channels : (j + 1) * channels])
            parts_i.append(acc[KX:, j * channels : (j + 1) * channels])
        d_r[...] = jnp.concatenate(parts_r, axis=0).T
        d_i[...] = jnp.concatenate(parts_i, axis=0).T
        sums = jnp.zeros((8, 128), F32)
        for b in range(tail_blocks(own_j)):
            tail = got[:, rows + b * 128 : rows + (b + 1) * 128]
            at = lax.broadcasted_iota(jnp.int32, (8, got.shape[0]), 1) % (2 * own_j) + b * 2 * own_j
            pick = (at == lax.broadcasted_iota(jnp.int32, (8, got.shape[0]), 0)).astype(BF16)
            sums = sums + dot(pick, tail)
        sums = sums[:, :channels] + sums[:, channels:]
        row = lax.broadcasted_iota(jnp.int32, (8, channels), 0)
        base = jnp.where(row == 2, factors + CENTRE * lift[0:1], factors)
        point_out[...] = dot_tn(jnp.where(row < 3, sums, 0.0), base, HI)

    start = pl.program_id(0) * per
    dr = d_r[...]
    di = d_i[...]
    for c in range(per):
        vr = v_r[pl.ds(start + c, 1), :]
        vi = v_i[pl.ds(start + c, 1), :]
        modes_out[0, c] = vr * dr + vi * di
        modes_out[1, c] = vr * di - vi * dr


def params(**kw):
    return pltpu.CompilerParams(vmem_limit_bytes=56 * 1024 * 1024, **kw)


def vmem(count):
    return [pl.BlockSpec(memory_space=pltpu.VMEM) for _ in range(count)]


def body(
    conc_init, cover_init, rate_on, rate_off, site_mask, inlet_profiles, inlet_index, lift,
    mode_weight, point_weight, point_bias, readout, cotangent,
):
    devices = lax.axis_size("slab")
    position = lax.axis_index("slab")
    local_x, plane = conc_init.shape
    depth = inlet_profiles.shape[1]
    span = plane // depth
    half = span // 2
    channels = lift.shape[1]
    modes = mode_weight.shape[0]
    own_j = modes // KX
    total_x = local_x * devices
    tab = {k: jnp.asarray(v) for k, v in tables(span, depth, total_x, devices, local_x).items()}
    sds = jax.ShapeDtypeStruct
    smem = pl.BlockSpec(memory_space=pltpu.SMEM)

    pack, conc, walls = pl.pallas_call(
        pack_kernel,
        name="pack",
        out_shape=(
            sds((local_x, half + 16, 2 * depth), BF16),
            sds((local_x, half, 2 * depth), F32),
            sds((local_x, 8, half), F32),
        ),
        in_specs=vmem(5),
        out_specs=vmem(3),
        compiler_params=params(),
    )(conc_init, cover_init, rate_on, rate_off, site_mask)
    up = lax.ppermute(pack, "slab", [(i, i + 1) for i in range(devices - 1)])
    down = lax.ppermute(pack, "slab", [(i + 1, i) for i in range(devices - 1)])
    cot_z, mapped = pl.pallas_call(
        prepare_kernel,
        name="prepare",
        out_shape=(
            sds((2 * depth, local_x, half), F32),
            sds((3, 2, channels, modes), F32),
        ),
        in_specs=vmem(1) + [smem] + vmem(1),
        out_specs=vmem(2),
        scratch_shapes=[pltpu.VMEM((local_x, half, 2 * depth), F32)],
        compiler_params=params(),
    )(cotangent, lift, mode_weight.transpose(1, 2, 3, 0))
    flags = jnp.stack([position == 0, position == devices - 1]).astype(jnp.int32)
    index = inlet_index.astype(F32).reshape(2, half)
    conc_out, cover_out, conc_z, cover_z, send = pl.pallas_call(
        transport_kernel,
        name="transport",
        out_shape=(
            sds((local_x, half, 2 * depth), F32),
            sds((local_x, span), F32),
            sds((2 * depth, local_x, half), F32),
            sds((local_x, span), F32),
            sds((KY, 4 * local_x * KZ), F32),
        ),
        in_specs=[smem] + vmem(11),
        out_specs=vmem(5),
        scratch_shapes=[pltpu.VMEM((2, 3 * local_x, 2 * depth, half), F32)],
        compiler_params=params(),
    )(
        flags, conc, walls, up, down, index, inlet_profiles,
        tab["perm"], tab["back"], tab["wave_yt"], tab["place_c"], tab["place_w"],
    )
    if own_j != KZ:
        send = send.reshape(KY, 4 * local_x, KZ // own_j, own_j).transpose(0, 2, 1, 3)
        send = send.reshape(devices, 4 * local_x * own_j)
    got = lax.all_to_all(send, "slab", 0, 0, tiled=True)
    ones = math.sqrt(total_x * plane)
    place = jnp.stack([position.astype(F32), jnp.float32(ones)])
    inv, spec = pl.pallas_call(
        mixing_kernel,
        name="mixing",
        out_shape=(
            sds((2 * KY * KZ, local_x * channels), BF16),
            sds((8, 2 * modes), F32),
        ),
        in_specs=[smem] + vmem(4),
        out_specs=vmem(2),
        scratch_shapes=[pltpu.VMEM((local_x * channels // 128, 2 * KY * KZ, 128), F32)],
        compiler_params=params(),
    )(place, got, tab["ax"], tab["bx"], mapped)
    inv = lax.all_to_all(inv, "slab", 0, 0, tiled=True)
    rows = local_x * channels
    wide = ZG * 2 * KY
    pred, grad = pl.pallas_call(
        functools.partial(layer_kernel, own_j),
        name="layer",
        out_shape=(
            sds((local_x, half, 2 * depth), F32),
            sds((2 * KY * KZ, rows + 128 * tail_blocks(own_j)), BF16),
        ),
        in_specs=vmem(11),
        out_specs=vmem(2),
        scratch_shapes=[
            pltpu.VMEM((depth // ZG, rows, wide + 32), BF16),
            pltpu.VMEM((rows, ZG * span), BF16),
            pltpu.VMEM((rows, ZG * span), BF16),
            pltpu.VMEM((16, ZG * span), BF16),
            pltpu.VMEM((16, ZG * span), BF16),
            pltpu.VMEM((rows, depth * 2 * KY), BF16),
            pltpu.VMEM((2 * depth, local_x, half), F32),
            pltpu.VMEM((rows, 16), F32),
            pltpu.VMEM((rows, span), F32),
        ],
        compiler_params=params(),
    )(
        inv, conc_z, cot_z, cover_z, lift, point_weight, point_bias.reshape(1, -1), readout.reshape(1, -1),
        tab["ez"], tab["fwd"], tab["bwd"],
    )
    grad = lax.all_to_all(grad, "slab", 0, 0, tiled=True)
    blocks = 8
    per = channels // blocks
    whole = lambda s: pl.BlockSpec(s, lambda i: (0,) * len(s))
    grad_modes, grad_point = pl.pallas_call(
        functools.partial(outer_kernel, own_j),
        name="outer",
        grid=(blocks,),
        out_shape=(
            sds((2, channels, channels, modes), F32),
            sds((channels, channels), F32),
        ),
        in_specs=[whole(grad.shape), whole(spec.shape), whole(tab["gx"].shape), whole(lift.shape)],
        out_specs=(
            pl.BlockSpec((2, per, channels, modes), lambda i: (0, i, 0, 0)),
            whole((channels, channels)),
        ),
        scratch_shapes=[
            pltpu.VMEM((channels, modes), F32),
            pltpu.VMEM((channels, modes), F32),
            pltpu.VMEM((channels, modes), F32),
            pltpu.VMEM((channels, modes), F32),
            pltpu.VMEM((rows // 128, 2 * KY * KZ, 128), F32),
        ],
        compiler_params=params(),
    )(grad, spec, tab["gx"], lift)
    return (
        conc_out.reshape(local_x, plane),
        cover_out,
        pred.reshape(local_x, plane),
        grad_modes.transpose(3, 0, 1, 2),
        grad_point,
    )


def solution(mesh):
    placed = (
        P(("groups", "slab"), None),
        P(("groups", "slab"), None),
        P(("groups", "slab"), None),
        P(("groups", "slab"), None),
        P(("groups", "slab"), None),
        P("groups", None),
        P("groups"),
        P(),
        P("slab", None, None, None),
        P(),
        P(),
        P(),
        P(("groups", "slab"), None),
    )
    return jax.shard_map(
        body,
        mesh=mesh,
        in_specs=placed,
        out_specs=(
            P(("groups", "slab"), None),
            P(("groups", "slab"), None),
            P(("groups", "slab"), None),
            P(("groups", "slab"), None, None, None),
            P("groups", None),
        ),
        check_vma=False,
    )
```

time: 94 us -> 84.7 us (0.901)
  local copies, waits for them, and re-layouts: 10 us -> 4.07 us
  waiting for transfers between devices: 12.6 us -> 8.94 us
  Pallas kernels: 34.8 us -> 37.4 us
  other arithmetic: 4.89 us -> 2.41 us
    pallas_call x0 -> x2, Pallas kernels: none -> 5.7 us  [the longest x1 3.75 us: body(): pl.pallas_call(prepare_kernel, name='prepare', out_shape=(sds((2 * depth,...]
    all_to_all x1, waiting for transfers between devices: 5.77 us -> 2.1 us  [body(): got = lax.all_to_all(send, 'slab', 0, 0, tiled=True)]
    another operation x6 -> x0, local copies, waits for them, and re-layouts: 2.12 us -> none  [the longest x4 2.12 us: body(): jnp.stack([cover_init, rate_on, rate_off, site_mask.astype(F32)], axis=1)]
    unnamed x12 -> x10, local copies, waits for them, and re-layouts: 4.09 us -> 1.99 us
    pallas_call x1, Pallas kernels: 4.25 us -> 2.72 us  [body(): pl.pallas_call(mixing_kernel, name='mixing', out_shape=(sds((2 * KY * KZ,...]
    pallas_call x1, Pallas kernels: 20.7 us -> 19.3 us  [body(): pl.pallas_call(functools.partial(layer_kernel, own_j), name='layer', out_...]
  transfers between devices with their start and end apart: 4 -> 4, of which waited for: 2 -> 2; matrix products, arithmetic and copies ran while one was open for 7% -> 5% of each run, Pallas kernels for 0% -> 4%
where the time goes in v2:
time: 84.7 us; the launch traced here: 84.1 us
  Pallas kernels  37.4 us (44%)
  starting transfers between devices  18.5 us (22%)
  blocking collectives  12.1 us (14%)
  waiting for transfers between devices  8.94 us (11%)
  local copies, waits for them, and re-layouts  4.07 us (5%)
  other arithmetic  2.41 us (3%)
    pallas_call x1, Pallas kernels, body(): pl.pallas_call(functools.partial(layer_kernel, own_j), name='layer', out_...  19.3 us
    all_to_all x1, blocking collectives, body(): inv = lax.all_to_all(inv, 'slab', 0, 0, tiled=True)  12.1 us
    all_to_all x1, starting transfers between devices, body(): got = lax.all_to_all(send, 'slab', 0, 0, tiled=True)  10.7 us
    all_to_all x1, waiting for transfers between devices, body(): grad = lax.all_to_all(grad, 'slab', 0, 0, tiled=True)  6.84 us
    pallas_call x1, Pallas kernels, body(): pl.pallas_call(functools.partial(outer_kernel, own_j), name='outer', grid...  5.1 us
    pallas_call x1, Pallas kernels, body(): pl.pallas_call(transport_kernel, name='transport', out_shape=(sds((local_...  4.57 us
    pallas_call x1, Pallas kernels, body(): pl.pallas_call(prepare_kernel, name='prepare', out_shape=(sds((2 * depth,...  3.75 us
    all_to_all x1, starting transfers between devices, body(): grad = lax.all_to_all(grad, 'slab', 0, 0, tiled=True)  3.52 us
  transfers between devices with their start and end apart: 4, of which 2 were waited for; matrix products, arithmetic and copies ran while one was open for 5% of the time, Pallas kernels for 4%

profile of v2, /device:TPU:0, one launch (start us, length us, event | category | flops | bytes accessed | tf_op | source)
XLA Modules:
  0.0 84.1 jit_solution(1560003138157305935)
XLA Ops:
  0.6 2.0 %pack.1 = (bf16[4,144,128]{2,1,0:T(8,128)(2,1)}, f32[4,128,128]{2,1,0:T(8,128)}, f32[4,8,128]{2,1,0:T(8,128)}) custom-call(f32[4,16384]{1,0:T(4,128)} %conc.1, f32[4,256]{1,0:T(4,128)} %cover.1, f32[4,256]{1,0:T(4,128)} %rate_on.1, f32[4,256]{1,0:T(4,128)} %rate_off.1, s32[4,256]{1,0:T(4,128)} %mask.1), custom_call_target="tpu_custom_call" | custom-call | tf_op jit(solution)/shard_map/pack/pallas_call | solution.py:494
  2.6 1.3 %collective-permute-start.1 = (bf16[4,144,128]{2,1,0:T(8,128)(2,1)}, bf16[4,144,128]{2,1,0:T(8,128)(2,1)S(1)}, u32[]{:S(2)}, u32[]{:S(2)}) collective-permute-start(bf16[4,144,128]{2,1,0:T(8,128)(2,1)} %get-tuple-element.23), channel_id=1, source_target_pairs={{1,0},{2,1},{3,2},{4,3},{5,4},{6,5},{7,6},{8,7},{9,8},{10,9},{11,1... | collective-permute-start | bytes 442376 | tf_op jit(solution)/shard_map/ppermute | solution.py:507
  3.9 3.0 %collective-permute-start = (bf16[4,144,128]{2,1,0:T(8,128)(2,1)}, bf16[4,144,128]{2,1,0:T(8,128)(2,1)S(1)}, u32[]{:S(2)}, u32[]{:S(2)}) collective-permute-start(bf16[4,144,128]{2,1,0:T(8,128)(2,1)} %get-tuple-element.23), channel_id=1, source_target_pairs={{0,1},{1,2},{2,3},{3,4},{4,5},{5,6},{6,7},{7,8},{8,9},{9,10},{10,1... | collective-permute-start | bytes 442376 | tf_op jit(solution)/shard_map/ppermute | solution.py:506
  6.9 1.3 %convert_bitcast_fusion.index = f32[2,128]{1,0:T(2,128)} fusion(s32[256]{0:T(256)} %param.30), kind=kLoop, calls=%fused_computation.3 | loop fusion | flops 256 | bytes 2048 | tf_op jit(solution)/shard_map/reshape | solution.py:521
  8.2 0.6 add_convert_fusion.flags
  8.8 0.0 collective-permute-done.1.down
  8.8 0.0 copy-start.2
  8.8 0.0 collective-permute-done.up
  8.8 0.0 copy-start.3
  8.8 0.6 copy-done.2
  9.4 0.1 copy-done.3
  9.5 4.6 %transport.1 = (f32[4,128,128]{2,1,0:T(8,128)}, f32[4,256]{1,0:T(4,128)}, f32[128,4,128]{2,1,0:T(4,128)}, f32[4,256]{1,0:T(4,128)}, f32[16,128]{1,0:T(8,128)}) custom-call(s32[2]{0:T(128)} %add_convert_fusion.flags, f32[4,128,128]{2,1,0:T(8,128)} %get-tuple-element.21.own, f32[4,8,128]{2,1,0:T(8,128)} %get-tuple-element.22.own_walls, ...), custom_call_target="tpu_custom_call" | custom-call | tf_op jit(solution)/shard_map/transport/pallas_call | solution.py:522
  14.1 0.0 copy-start.1
  14.1 10.7 %all-to-all-start = ((f32[16,1,128]{2,1,0:T(1,128)}), f32[16,1,128]{2,1,0:T(1,128)S(1)}, u32[]{:S(2)}, u32[]{:S(2)}) async-start(f32[16,1,128]{2,1,0:T(1,128)} %bitcast.31), calls=%async_computation | async-start | bytes 16384 | tf_op jit(solution)/shard_map/all_to_all | solution.py:543
  24.8 0.6 pad_maximum_fusion.place
  25.3 3.7 %prepare.1 = (f32[128,4,128]{2,1,0:T(4,128)}, f32[3,2,64,128]{3,2,1,0:T(8,128)}) custom-call(f32[4,16384]{1,0:T(4,128)} %cot.1, f32[3,64]{1,0:T(4,128)} %lift.5, bf16[2,64,64,128]{3,2,1,0:T(8,128)(2,1)} %bitcast.23), custom_call_target="tpu_custom_call" | custom-call | tf_op jit(solution)/shard_map/prepare/pallas_call | solution.py:508
  29.1 2.1 %all-to-all-done = f32[16,1,128]{2,1,0:T(1,128)S(1)} async-done(((f32[16,1,128]{2,1,0:T(1,128)}), f32[16,1,128]{2,1,0:T(1,128)S(1)}, u32[]{:S(2)}, u32[]{:S(2)}) %all-to-all-start) | async-done | bytes 8224 | tf_op jit(solution)/shard_map/all_to_all | solution.py:543
  31.2 0.0 copy-start.4
  31.2 0.6 copy-done.4
  31.8 2.7 %mixing.1 = (bf16[256,256]{1,0:T(8,128)(2,1)}, f32[8,256]{1,0:T(8,128)}) custom-call(f32[2]{0:T(128)} %pad_maximum_fusion.place, f32[16,128]{1,0:T(8,128)} %bitcast.30, f32[16,256]{1,0:T(8,128)} %constant.40.clone.ax, bf16[2,128,32]{2,1,0:T(8,128)(2,1)} %constant.41.clone.bx, f32[3,2,64,128]{3,2,1,0:T(8,128)} %get-tuple-element.27.mapped), custom_call_target="tpu_custom_call" | custom-call | tf_op jit(solution)/shard_map/mixing/pallas_call | solution.py:546
  34.5 12.1 %all_to_all.33 = bf16[16,16,256]{2,1,0:T(8,128)(2,1)} all-to-all(bf16[16,16,256]{2,1,0:T(8,128)(2,1)} %bitcast.29), channel_id=1, replica_groups=mesh['groups'=2,'slab'=16] {'slab'}, dimensions={0} | all-to-all | bytes 262144 | tf_op jit(solution)/shard_map/all_to_all | solution.py:558
  46.6 19.3 %layer.1 = (f32[4,128,128]{2,1,0:T(8,128)}, bf16[256,384]{1,0:T(8,128)(2,1)}) custom-call(bf16[256,256]{1,0:T(8,128)(2,1)} %bitcast.25, f32[128,4,128]{2,1,0:T(4,128)} %get-tuple-element.29.conc_z, f32[128,4,128]{2,1,0:T(4,128)} %get-tuple-element.30.cot_z, f32[4,256]{1,0:T(4,128)} %get-tuple-element.31.cover_z, f32[3,64]{1,0:T(4,128)} %lift.5, ...), custom_call_target="tpu_custom_call" | custom-call | tf_op jit(solution)/shard_map/layer/pallas_call | solution.py:561
  65.9 3.5 %all-to-all-start.2 = ((bf16[16,16,384]{2,1,0:T(8,128)(2,1)}), bf16[16,16,384]{2,1,0:T(8,128)(2,1)S(1)}, u32[]{:S(2)}, u32[]{:S(2)}) async-start(bf16[16,16,384]{2,1,0:T(8,128)(2,1)} %bitcast.28), calls=%async_computation.2 | async-start | bytes 393216 | tf_op jit(solution)/shard_map/all_to_all | solution.py:586
  69.4 0.0 copy-done.1
  69.4 2.1 %copy_bitcast_fusion = (f32[4,16384]{1,0:T(4,128)}, f32[4,16384]{1,0:T(4,128)}) fusion(f32[1,4,128,128]{3,2,1,0:T(8,128)} %bitcast.27, f32[1,4,128,128]{3,2,1,0:T(8,128)S(1)} %bitcast.26), kind=kLoop, calls=%fused_computation | loop fusion | bytes 1048576 | tf_op jit(solution)/shard_map/reshape | solution.py:615
  71.5 6.8 %all-to-all-done.2 = bf16[16,16,384]{2,1,0:T(8,128)(2,1)S(1)} async-done(((bf16[16,16,384]{2,1,0:T(8,128)(2,1)}), bf16[16,16,384]{2,1,0:T(8,128)(2,1)S(1)}, u32[]{:S(2)}, u32[]{:S(2)}) %all-to-all-start.2) | async-done | bytes 196640 | tf_op jit(solution)/shard_map/all_to_all | solution.py:586
  78.3 0.0 copy-start
  78.3 0.7 copy-done
  79.0 5.1 %outer.1 = (f32[2,64,64,128]{3,2,1,0:T(8,128)}, f32[64,64]{1,0:T(8,128)}) custom-call(bf16[256,384]{1,0:T(8,128)(2,1)} %bitcast.24, f32[8,256]{1,0:T(8,128)} %get-tuple-element.34.spec, bf16[64,128]{1,0:T(8,128)(2,1)} %constant.42.clone.gx, f32[3,64]{1,0:T(4,128)} %lift.5), custom_call_target="tpu_custom_call" | custom-call | tf_op jit(solution)/shard_map/outer/pallas_call | solution.py:590
Async XLA Ops:
  2.6 6.2 %collective-permute-start.1 = (bf16[4,144,128]{2,1,0:T(8,128)(2,1)}, bf16[4,144,128]{2,1,0:T(8,128)(2,1)S(1)}, u32[]{:S(2)}, u32[]{:S(2)}) collective-permute-start(bf16[4,144,128]{2,1,0:T(8,128)(2,1)} %get-tuple-element.23), channel_id=1, source_target_pairs={{1,0},{2,1},{3,2},{4,3},{5,4},{6,5},{7,6},{8,7},{9,8},{10,9},{11,1... | collective-permute-start | bytes 442376 | tf_op jit(solution)/shard_map/ppermute | solution.py:507
  3.9 4.9 %collective-permute-start = (bf16[4,144,128]{2,1,0:T(8,128)(2,1)}, bf16[4,144,128]{2,1,0:T(8,128)(2,1)S(1)}, u32[]{:S(2)}, u32[]{:S(2)}) collective-permute-start(bf16[4,144,128]{2,1,0:T(8,128)(2,1)} %get-tuple-element.23), channel_id=1, source_target_pairs={{0,1},{1,2},{2,3},{3,4},{4,5},{5,6},{6,7},{7,8},{8,9},{9,10},{10,1... | collective-permute-start | bytes 442376 | tf_op jit(solution)/shard_map/ppermute | solution.py:506
  8.8 0.7 copy-start.2
  8.8 0.7 copy-start.3
  14.1 55.3 %copy-start.1 = (f32[4,128,128]{2,1,0:T(8,128)S(1)}, f32[4,128,128]{2,1,0:T(8,128)}, u32[]{:S(2)}) copy-start(f32[4,128,128]{2,1,0:T(8,128)} %get-tuple-element.24) | copy-start | bytes 786436
  14.1 17.1 %all-to-all-start = ((f32[16,1,128]{2,1,0:T(1,128)}), f32[16,1,128]{2,1,0:T(1,128)S(1)}, u32[]{:S(2)}, u32[]{:S(2)}) async-start(f32[16,1,128]{2,1,0:T(1,128)} %bitcast.31), calls=%async_computation | async-start | bytes 16384 | tf_op jit(solution)/shard_map/all_to_all | solution.py:543
  31.2 0.6 copy-start.4
  65.9 12.5 %all-to-all-start.2 = ((bf16[16,16,384]{2,1,0:T(8,128)(2,1)}), bf16[16,16,384]{2,1,0:T(8,128)(2,1)S(1)}, u32[]{:S(2)}, u32[]{:S(2)}) async-start(bf16[16,16,384]{2,1,0:T(8,128)(2,1)} %bitcast.28), calls=%async_computation.2 | async-start | bytes 393216 | tf_op jit(solution)/shard_map/all_to_all | solution.py:586
  78.3 0.7 copy-start

commit v3 on v2

--- a/solution.py
+++ b/solution.py
@@ -89,13 +89,10 @@
     tab["ez"] = ez.reshape(2 * KY * KZ, depth * pairs).astype(jnp.bfloat16)
     by = np.stack([np.cos(alpha), np.sin(alpha)], axis=2).reshape(span, pairs)
     fwd = np.zeros((ZG, ZG * pairs + 16, span), np.float32)
-    bwd = np.zeros((ZG, span, ZG * pairs), np.float32)
     for i in range(ZG):
         fwd[i, i * pairs : (i + 1) * pairs] = by.T
         fwd[i, ZG * pairs : ZG * pairs + 2] = 1.0
-        bwd[i, :, i * pairs : (i + 1) * pairs] = by
     tab["fwd"] = fwd.astype(jnp.bfloat16)
-    tab["bwd"] = bwd.reshape(ZG * span, ZG * pairs).astype(jnp.bfloat16)
     x = np.arange(total_x)
     gamma = 2 * np.pi * ((x[:, None] * kx[None, :]) % total_x) / total_x
     cg, sg = np.cos(gamma), np.sin(gamma)
@@ -116,7 +113,16 @@
     return tab
 
 
-def pack_kernel(conc, cover, rate_on, rate_off, mask, packed, conc_out, walls_out):
+def pack_kernel(
+    conc_hbm, cover_hbm, on_hbm, off_hbm, mask_hbm, packed, conc_out, walls_out,
+    conc, cover, rate_on, rate_off, mask, sems,
+):
+    pairs = ((cover_hbm, cover), (on_hbm, rate_on), (off_hbm, rate_off), (mask_hbm, mask), (conc_hbm, conc))
+    copies = [pltpu.make_async_copy(src, dst, sems.at[k]) for k, (src, dst) in enumerate(pairs)]
+    for copy in copies:
+        copy.start()
+    for copy in copies:
+        copy.wait()
     local_x = conc.shape[0]
     half = conc_out.shape[1]
     for k in range(half):
@@ -130,7 +136,12 @@
         packed[x, half:, :] = tail.astype(BF16)
 
 
-def prepare_kernel(cot, lift, weight, cot_z, mapped, flat):
+def prepare_kernel(cot_hbm, lift, weight_hbm, cot_z, mapped, flat, cot, weight, sems):
+    cot_copy = pltpu.make_async_copy(cot_hbm, cot, sems.at[0])
+    halves = [pltpu.make_async_copy(weight_hbm.at[p], weight.at[p], sems.at[1 + p]) for p in range(2)]
+    for copy in (cot_copy, *halves):
+        copy.start()
+    cot_copy.wait()
     local_x = cot.shape[0]
     half = flat.shape[1]
     for k in range(half):
@@ -139,6 +150,7 @@
         cot_z[:, x, :] = flat[x].T
     channels = weight.shape[1]
     for p in range(2):
+        halves[p].wait()
         acc = [jnp.zeros(weight.shape[2:], F32) for _ in range(3)]
         for c in range(channels):
             w = weight[p, c].astype(F32)
@@ -148,9 +160,17 @@
 
 
 def transport_kernel(
-    flags, own, own_walls, up, down, index, profiles, perm, back, wave_yt, place_c, place_w,
-    conc_out, cover_out, conc_z, cover_z, send, buf,
+    devices, own, own_walls, up, down, index_hbm, profiles_hbm, perm_hbm, back_hbm, wave_hbm, place_c_hbm, place_w_hbm,
+    conc_out, cover_out, conc_z, cover_z, send,
+    buf, index, profiles, perm, back, wave_yt, place_c, place_w, sems,
 ):
+    moves = (
+        (index_hbm, index), (perm_hbm, perm), (profiles_hbm, profiles), (wave_hbm, wave_yt),
+        (place_c_hbm, place_c), (place_w_hbm, place_w), (back_hbm, back),
+    )
+    copies = [pltpu.make_async_copy(src, dst, sems.at[k]) for k, (src, dst) in enumerate(moves)]
+    for copy in copies:
+        copy.start()
     local_x = own.shape[0]
     half = own.shape[1]
     depth = profiles.shape[1]
@@ -165,7 +185,10 @@
             ref = up if r < local_x else down
             buf[0, r] = (ref[x, :half, :].astype(F32) + CENTRE).T
             walls.append(ref[x, half:, :].astype(F32)[:8])
-    walls.append(jnp.concatenate([index[...], jnp.zeros((6, half), F32)], axis=0))
+    for copy in copies[:3]:
+        copy.wait()
+    profile = index[...].astype(F32)
+    walls.append(jnp.concatenate([profile[:, :half], profile[:, half:], jnp.zeros((6, half), F32)], axis=0))
     spread = dot(jnp.concatenate(walls, axis=0), perm[...], HI)
     fields = [
         spread[8 * r : 8 * r + 4, : 2 * half] + spread[8 * r + 4 : 8 * r + 8, 2 * half :]
@@ -180,8 +203,8 @@
     height = (height + 0.5) / depth
     speed = PEAK_SPEED * 4.0 * height * (1.0 - height)
     speed = jnp.concatenate([speed, speed], axis=0)
-    first = flags[0] == 1
-    last = flags[1] == 1
+    first = lax.axis_index("slab") == 0
+    last = lax.axis_index("slab") == devices - 1
     cover = [f[0:1] for f in fields]
     for step in range(STEPS):
         cur, nxt = step % 2, (step + 1) % 2
@@ -208,6 +231,8 @@
             buf[nxt, r, 0:1] = new[0:1] - uptake[:, :half]
             buf[nxt, r, depth : depth + 1] = new[depth : depth + 1] - uptake[:, half:]
             cover[r] = cover[r] + uptake
+    for copy in copies[3:]:
+        copy.wait()
     cur = STEPS % 2
     covers = jnp.concatenate(cover[local_x : 2 * local_x], axis=0)
     cover_z[...] = covers
@@ -229,7 +254,7 @@
         conc_z[:, i, :] = planes[i]
 
 
-def mixing_kernel(place, got, ax, bx, mapped, inv_out, spec_out, stage):
+def mixing_kernel(ones_value, got, ax, bx, mapped, inv_out, spec_out, stage):
     modes = mapped.shape[3]
     channels = mapped.shape[2]
     own_j = modes // KX
@@ -250,7 +275,7 @@
             spec.append(jnp.sum(jnp.where(keep, tiled, 0.0), axis=0, keepdims=True))
     cr, ci, wr, wi = spec
     lane = lax.broadcasted_iota(jnp.int32, (1, modes), 1)
-    ones = jnp.where((lane == 0) & (place[0] == 0.0), place[1], 0.0)
+    ones = jnp.where((lane == 0) & (lax.axis_index("slab") == 0), ones_value, 0.0)
     zero = jnp.zeros((1, modes), F32)
     spec_out[:, :modes] = jnp.concatenate([cr, wr, ones] + [zero] * 5, axis=0)
     spec_out[:, modes:] = jnp.concatenate([ci, wi] + [zero] * 6, axis=0)
@@ -277,8 +302,8 @@
 
 
 def layer_kernel(
-    own_j, inv, conc_z, cot_z, cover_z, lift, point_weight, bias, readout, ez, fwd, bwd,
-    pred_out, grad_out, lhs, grads_a, grads_b, ext_a, ext_b, waves, pred, point, ahead,
+    own_j, inv, conc_z, cot_z, cover_z, lift, point_weight, bias, readout, ez, fwd,
+    pred_out, grad_out, lhs, ext_all, waves, pred, point, pre_a, pre_b, hidden_a, hidden_b, grads_a, grads_b,
 ):
     channels = lift.shape[1]
     local_x = cover_z.shape[0]
@@ -287,7 +312,8 @@
     depth = cot_z.shape[0] // 2
     groups = depth // ZG
     rows = local_x * channels
-    wide = ZG * 2 * KY
+    pairs = 2 * KY
+    wide = ZG * pairs
     iscale = 1.0 / math.sqrt(KX * KY * KZ)
     c1 = math.sqrt(2.0 / math.pi)
     unit = (c1 * 0.044715) ** (1.0 / 3.0)
@@ -302,10 +328,9 @@
         lax.broadcasted_iota(jnp.int32, (channels, channels), 0)
         == lax.broadcasted_iota(jnp.int32, (channels, channels), 1)
     ).astype(F32)
-    columns = dot_nt(eye, jnp.concatenate([bias[...], readout[...], jnp.zeros((6, channels), F32)], axis=0), HI)
+    columns = dot_nt(eye, jnp.concatenate([bias[...], jnp.zeros((7, channels), F32)], axis=0), HI)
     a0, a1 = unit * mapped[:, 0:1], unit * mapped[:, 1:2]
     a2 = unit * (mapped[:, 2:3] + columns[:, 0:1]) + CENTRE * a0
-    half_readout = 0.5 * columns[:, 1:2]
 
     lane = lax.broadcasted_iota(jnp.int32, (channels, 32), 1)
     a0_high, a2_high = high(a0), high(a2)
@@ -323,87 +348,78 @@
     lifted = (unit * dot(flipped, ez[...])).astype(BF16)
     for g in range(groups):
         lhs[g, :, :wide] = lifted[:, g * wide : (g + 1) * wide]
-    wide_readout = jnp.concatenate([(0.5 / unit) * readout[...]] * local_x, axis=1)
+    wide_readout = jnp.concatenate([readout[...]] * local_x, axis=1)
     owner = lax.broadcasted_iota(jnp.int32, (16, rows), 1) // channels
     slot = lax.broadcasted_iota(jnp.int32, (16, rows), 0)
-    readout_high = high(wide_readout)
-    weigh = jnp.where(
-        slot == owner, readout_high, jnp.where(slot - 8 == owner, wide_readout - readout_high, 0.0)
-    ).astype(BF16)
+    scaled = (0.5 / unit) * wide_readout
+    weigh = jnp.where(slot == owner, high(scaled), jnp.where(slot - 8 == owner, scaled - high(scaled), 0.0))
+    weigh = weigh.astype(BF16)
     point[...] = jnp.zeros(point.shape, F32)
     grads_b[...] = jnp.zeros(grads_b.shape, BF16)
-    ext_b[...] = jnp.zeros(ext_b.shape, BF16)
-
-    def before(g, i, ext_ref):
+    hidden_b[...] = jnp.zeros(hidden_b.shape, BF16)
+    by = fwd[0, :pairs, :]
+    pres, hiddens, grads = (pre_a, pre_b), (hidden_a, hidden_b), (grads_a, grads_b)
+
+    def before(g, i, pre):
         z = g * ZG + i
         conc = jnp.concatenate([conc_z[z], conc_z[depth + z]], axis=1) - CENTRE
         conc_high = high(conc)
         wall = jnp.where(z == 0, cover_z[...], 0.0)
         ext = jnp.concatenate([conc_high, conc - conc_high, conc_high, wall], axis=0).astype(BF16)
-        ext_ref[:, i * span : (i + 1) * span] = ext
-        return dot(lhs[g], jnp.concatenate([fwd[i], ext], axis=0))
-
-    def collect(at, grads, ext):
-        waves[:, pl.ds(pl.multiple_of(at * wide, wide), wide)] = dot(grads[...], bwd[...]).astype(BF16)
-        point[...] += dot_nt(grads[...], ext[...])
-
-    def group(g, grads, ext, grads_other, ext_other):
-        collect(jnp.maximum(g - 1, 0), grads_other, ext_other)
+        ext_all[z] = ext
+        pre[...] = dot(lhs[g], jnp.concatenate([fwd[i], ext], axis=0))
+
+    def after(z, hidden, grad):
+        line = dot(weigh, hidden[...])
+        line = line[:local_x] + line[8 : 8 + local_x]
+        pred[z] = line[:, :half]
+        pred[depth + z] = line[:, half:]
+        sums = dot_nt(jnp.concatenate([by, ext_all[z]], axis=0), grad[...])
+        waves[pl.ds(pl.multiple_of(z * pairs, pairs), pairs), :] = sums[:pairs].astype(BF16)
+        point[:16] += sums[pairs:]
+        point[16:] += sums[:8]
+
+    before(0, 0, pre_a)
+
+    def group(g, carry):
         for i in range(ZG):
-            pre = ahead[...] if i == 0 else nxt
+            z = g * ZG + i
+            this, other = i % 2, (i + 1) % 2
             if i < ZG - 1:
-                nxt = before(g, i + 1, ext)
+                before(g, i + 1, pres[other])
             else:
-                nxt = before(jnp.minimum(g + 1, groups - 1), 0, ext_other)
-            z = g * ZG + i
+                before(jnp.minimum(g + 1, groups - 1), 0, pres[other])
+            after(jnp.maximum(z - 1, 0), hiddens[other], grads[other])
             cot = jnp.concatenate([cot_z[z], cot_z[depth + z]], axis=1)
-            hidden = []
             for x in range(local_x):
-                y = pre[x * channels : (x + 1) * channels]
-                p = y * y + kappa
-                t = jnp.tanh(y * p)
+                here = slice(x * channels, (x + 1) * channels)
+                y = pres[this][here, :]
+                u = y * (y * y + kappa)
+                t = jnp.tanh(u)
                 s = 1.0 + t
-                hidden.append((y * s).astype(BF16))
-                slope = y * (3.0 * p - 2.0 * kappa)
-                grad = s * (1.0 + slope * (1.0 - t)) * cot[x : x + 1]
-                grads[x * channels : (x + 1) * channels, i * span : (i + 1) * span] = grad.astype(BF16)
-            line = dot(weigh, jnp.concatenate(hidden, axis=0))
-            line = line[:local_x] + line[8 : 8 + local_x]
-            pred[z] = line[:, :half]
-            pred[depth + z] = line[:, half:]
-        ahead[...] = nxt
-
-    ahead[...] = before(0, 0, ext_a)
-
-    def pair(h, carry):
-        group(2 * h, grads_a, ext_a, grads_b, ext_b)
-        group(2 * h + 1, grads_b, ext_b, grads_a, ext_a)
+                hiddens[this][here, :] = (y * s).astype(BF16)
+                slope = u - (2.0 / 3.0 * kappa) * y
+                grad = s * (1.0 / 3.0 + slope * (1.0 - t)) * cot[x : x + 1]
+                grads[this][here, :] = grad.astype(BF16)
         return carry
 
-    lax.fori_loop(0, groups // 2, pair, 0)
-    collect(groups - 1, grads_b, ext_b)
+    lax.fori_loop(0, groups, group, 0)
+    after(depth - 1, hidden_b, grads_b)
     for x in range(local_x):
         pred_out[x] = pred[:, x, :].T
-    total = dot_nt(waves[...], ez[...])
-    lane16 = lax.broadcasted_iota(jnp.int32, (channels, 16), 1)
-    lane128 = lax.broadcasted_iota(jnp.int32, (channels, 128), 1)
-    cols = []
-    sums = jnp.zeros((channels, 128), F32)
-    for x in range(local_x):
-        here = slice(x * channels, (x + 1) * channels)
-        pt = point[here, :]
-        with_conc = jnp.sum(jnp.where((lane16 == x) | (lane16 == 4 + x), pt, 0.0), axis=1, keepdims=True)
-        with_wall = jnp.sum(jnp.where(lane16 == 12 + x, pt, 0.0), axis=1, keepdims=True)
-        alone = total[here, 0:1]
-        sums = sums + jnp.where(
-            lane128 == 0, with_conc, jnp.where(lane128 == 1, with_wall, jnp.where(lane128 == 2, alone, 0.0))
-        )
-        cols.append((iscale * half_readout) * total[here])
-    sums = (half_readout * sums).T[:16]
-    sums_high = high(sums)
-    both = jnp.concatenate([sums_high, sums - sums_high], axis=1).astype(BF16)
+    total = dot(ez[...], waves[...])
+    grad_row = 1.5 * wide_readout
+    grad_out[:, :rows] = (total * (iscale * grad_row)).astype(BF16)
+    mine = point[:16]
+    with_conc = jnp.sum(jnp.where((slot < 8) & (slot % 4 == owner), mine, 0.0), axis=0, keepdims=True)
+    with_wall = jnp.sum(jnp.where(slot == 12 + owner, mine, 0.0), axis=0, keepdims=True)
+    sums = jnp.concatenate([with_conc, with_wall, point[16:17], jnp.zeros((13, rows), F32)], axis=0) * grad_row
+    parts = [sums[:, x * channels : (x + 1) * channels] for x in range(local_x)]
+    sums = parts[0]
+    for part in parts[1:]:
+        sums = sums + part
+    both = jnp.concatenate([high(sums), sums - high(sums)], axis=1).astype(BF16)
     out_rows = grad_out.shape[0]
-    grad_out[:, :rows] = jnp.concatenate(cols, axis=0).T.astype(BF16)
     for b in range(tail_blocks(own_j)):
         row = lax.broadcasted_iota(jnp.int32, (out_rows, 16), 0) % (2 * own_j) + b * 2 * own_j
         pick = (row == lax.broadcasted_iota(jnp.int32, (out_rows, 16), 1)).astype(BF16)
@@ -465,8 +481,16 @@
         modes_out[1, c] = vr * di - vi * dr
 
 
-def params(**kw):
-    return pltpu.CompilerParams(vmem_limit_bytes=56 * 1024 * 1024, **kw)
+def params(mib):
+    return pltpu.CompilerParams(vmem_limit_bytes=mib * 1024 * 1024)
+
+
+def in_hbm(array):
+    return pltpu.with_memory_space_constraint(array, pltpu.HBM)
+
+
+def hbm(count):
+    return [pl.BlockSpec(memory_space=pltpu.HBM) for _ in range(count)]
 
 
 def vmem(count):
@@ -478,7 +502,6 @@
     mode_weight, point_weight, point_bias, readout, cotangent,
 ):
     devices = lax.axis_size("slab")
-    position = lax.axis_index("slab")
     local_x, plane = conc_init.shape
     depth = inlet_profiles.shape[1]
     span = plane // depth
@@ -499,10 +522,14 @@
             sds((local_x, half, 2 * depth), F32),
             sds((local_x, 8, half), F32),
         ),
-        in_specs=vmem(5),
+        in_specs=hbm(5),
         out_specs=vmem(3),
-        compiler_params=params(),
-    )(conc_init, cover_init, rate_on, rate_off, site_mask)
+        scratch_shapes=[pltpu.VMEM(conc_init.shape, F32)]
+        + [pltpu.VMEM(cover_init.shape, F32)] * 3
+        + [pltpu.VMEM(site_mask.shape, jnp.int32), pltpu.SemaphoreType.DMA((5,))],
+        compiler_params=params(4),
+        cost_estimate=pl.CostEstimate(flops=180000000, transcendentals=0, bytes_accessed=1020000),
+    )(*map(in_hbm, (conc_init, cover_init, rate_on, rate_off, site_mask)))
     up = lax.ppermute(pack, "slab", [(i, i + 1) for i in range(devices - 1)])
     down = lax.ppermute(pack, "slab", [(i + 1, i) for i in range(devices - 1)])
     cot_z, mapped = pl.pallas_call(
@@ -512,15 +539,23 @@
             sds((2 * depth, local_x, half), F32),
             sds((3, 2, channels, modes), F32),
         ),
-        in_specs=vmem(1) + [smem] + vmem(1),
+        in_specs=hbm(1) + [smem] + hbm(1),
         out_specs=vmem(2),
-        scratch_shapes=[pltpu.VMEM((local_x, half, 2 * depth), F32)],
-        compiler_params=params(),
-    )(cotangent, lift, mode_weight.transpose(1, 2, 3, 0))
-    flags = jnp.stack([position == 0, position == devices - 1]).astype(jnp.int32)
-    index = inlet_index.astype(F32).reshape(2, half)
+        scratch_shapes=[
+            pltpu.VMEM((local_x, half, 2 * depth), F32),
+            pltpu.VMEM(cotangent.shape, F32),
+            pltpu.VMEM((2, channels, channels, modes), BF16),
+            pltpu.SemaphoreType.DMA((3,)),
+        ],
+        compiler_params=params(8),
+        cost_estimate=pl.CostEstimate(flops=1200000000, transcendentals=0, bytes_accessed=6800000),
+    )(in_hbm(cotangent), lift, in_hbm(mode_weight.transpose(1, 2, 3, 0)))
+    fixed = (
+        inlet_index.reshape(1, span), inlet_profiles,
+        tab["perm"], tab["back"], tab["wave_yt"], tab["place_c"], tab["place_w"],
+    )
     conc_out, cover_out, conc_z, cover_z, send = pl.pallas_call(
-        transport_kernel,
+        functools.partial(transport_kernel, devices),
         name="transport",
         out_shape=(
             sds((local_x, half, 2 * depth), F32),
@@ -529,32 +564,34 @@
             sds((local_x, span), F32),
             sds((KY, 4 * local_x * KZ), F32),
         ),
-        in_specs=[smem] + vmem(11),
+        in_specs=vmem(4) + hbm(7),
         out_specs=vmem(5),
-        scratch_shapes=[pltpu.VMEM((2, 3 * local_x, 2 * depth, half), F32)],
-        compiler_params=params(),
+        scratch_shapes=[pltpu.VMEM((2, 3 * local_x, 2 * depth, half), F32)]
+        + [pltpu.VMEM(v.shape, v.dtype) for v in fixed]
+        + [pltpu.SemaphoreType.DMA((len(fixed),))],
+        compiler_params=params(8),
+        cost_estimate=pl.CostEstimate(flops=2220000000, transcendentals=0, bytes_accessed=12580000),
     )(
-        flags, conc, walls, up, down, index, inlet_profiles,
-        tab["perm"], tab["back"], tab["wave_yt"], tab["place_c"], tab["place_w"],
+        conc, walls, up, down, *map(in_hbm, fixed),
     )
     if own_j != KZ:
         send = send.reshape(KY, 4 * local_x, KZ // own_j, own_j).transpose(0, 2, 1, 3)
         send = send.reshape(devices, 4 * local_x * own_j)
     got = lax.all_to_all(send, "slab", 0, 0, tiled=True)
     ones = math.sqrt(total_x * plane)
-    place = jnp.stack([position.astype(F32), jnp.float32(ones)])
     inv, spec = pl.pallas_call(
-        mixing_kernel,
+        functools.partial(mixing_kernel, ones),
         name="mixing",
         out_shape=(
             sds((2 * KY * KZ, local_x * channels), BF16),
             sds((8, 2 * modes), F32),
         ),
-        in_specs=[smem] + vmem(4),
+        in_specs=vmem(4),
         out_specs=vmem(2),
         scratch_shapes=[pltpu.VMEM((local_x * channels // 128, 2 * KY * KZ, 128), F32)],
-        compiler_params=params(),
-    )(place, got, tab["ax"], tab["bx"], mapped)
+        compiler_params=params(4),
+        cost_estimate=pl.CostEstimate(flops=960000000, transcendentals=0, bytes_accessed=5440000),
+    )(got, tab["ax"], tab["bx"], mapped)
     inv = lax.all_to_all(inv, "slab", 0, 0, tiled=True)
     rows = local_x * channels
     wide = ZG * 2 * KY
@@ -565,23 +602,22 @@
             sds((local_x, half, 2 * depth), F32),
             sds((2 * KY * KZ, rows + 128 * tail_blocks(own_j)), BF16),
         ),
-        in_specs=vmem(11),
+        in_specs=vmem(10),
         out_specs=vmem(2),
         scratch_shapes=[
             pltpu.VMEM((depth // ZG, rows, wide + 32), BF16),
-            pltpu.VMEM((rows, ZG * span), BF16),
-            pltpu.VMEM((rows, ZG * span), BF16),
-            pltpu.VMEM((16, ZG * span), BF16),
-            pltpu.VMEM((16, ZG * span), BF16),
-            pltpu.VMEM((rows, depth * 2 * KY), BF16),
+            pltpu.VMEM((depth, 16, span), BF16),
+            pltpu.VMEM((depth * 2 * KY, rows), BF16),
             pltpu.VMEM((2 * depth, local_x, half), F32),
-            pltpu.VMEM((rows, 16), F32),
-            pltpu.VMEM((rows, span), F32),
-        ],
-        compiler_params=params(),
+            pltpu.VMEM((24, rows), F32),
+        ]
+        + [pltpu.VMEM((rows, span), F32)] * 2
+        + [pltpu.VMEM((rows, span), BF16)] * 4,
+        compiler_params=params(16),
+        cost_estimate=pl.CostEstimate(flops=7440000000, transcendentals=0, bytes_accessed=42160000),
     )(
         inv, conc_z, cot_z, cover_z, lift, point_weight, point_bias.reshape(1, -1), readout.reshape(1, -1),
-        tab["ez"], tab["fwd"], tab["bwd"],
+        tab["ez"], tab["fwd"],
     )
     grad = lax.all_to_all(grad, "slab", 0, 0, tiled=True)
     blocks = 8
@@ -607,7 +643,8 @@
             pltpu.VMEM((channels, modes), F32),
             pltpu.VMEM((rows // 128, 2 * KY * KZ, 128), F32),
         ],
-        compiler_params=params(),
+        compiler_params=params(8),
+        cost_estimate=pl.CostEstimate(flops=2520000000, transcendentals=0, bytes_accessed=14280000),
     )(grad, spec, tab["gx"], lift)
     return (
         conc_out.reshape(local_x, plane),

time: 84.7 us -> 70.4 us (0.83)
  Pallas kernels: 37.4 us -> 26.2 us
  waiting for transfers between devices: 8.94 us -> 12 us
  local copies, waits for them, and re-layouts: 4.07 us -> 1.19 us
  other arithmetic: 2.41 us -> 0 us
  blocking collectives: 12.1 us -> 10.5 us
    pallas_call x1, Pallas kernels: 19.3 us -> 12.5 us  [body(): pl.pallas_call(functools.partial(layer_kernel, own_j), name='layer', out_...]
    pallas_call x2, Pallas kernels: 7.29 us -> 5.09 us  [the longest x1 4.02 us: body(): pl.pallas_call(functools.partial(transport_kernel, devices), name='transp...]
    unnamed x10 -> x18, local copies, waits for them, and re-layouts: 1.99 us -> 0.06 us
    all_to_all x1, blocking collectives: 12.1 us -> 10.5 us  [body(): inv = lax.all_to_all(inv, 'slab', 0, 0, tiled=True)]
    reshape x1 -> x0, other arithmetic: 1.26 us -> none  [body(): index = inlet_index.astype(F32).reshape(2, half)]
    all_to_all x1, waiting for transfers between devices: 2.1 us -> 3.21 us  [body(): got = lax.all_to_all(send, 'slab', 0, 0, tiled=True)]
    ppermute x1, waiting for transfers between devices: 0.01 us -> 0.97 us  [body(): up = lax.ppermute(pack, 'slab', [(i, i + 1) for i in range(devices - 1)])]
    all_to_all x1, waiting for transfers between devices: 6.84 us -> 7.8 us  [body(): grad = lax.all_to_all(grad, 'slab', 0, 0, tiled=True)]
  transfers between devices with their start and end apart: 4 -> 4, of which waited for: 2 -> 3; matrix products, arithmetic and copies ran while one was open for 5% -> 2% of each run, Pallas kernels for 4% -> 4%
where the time goes in v3:
time: 70.4 us; the launch traced here: 69.9 us
  Pallas kernels  26.2 us (37%)
  starting transfers between devices  19.2 us (27%)
  waiting for transfers between devices  12 us (17%)
  blocking collectives  10.5 us (15%)
  local copies, waits for them, and re-layouts  1.19 us (2%)
  between operations  0.81 us (1%)
    pallas_call x1, Pallas kernels, body(): pl.pallas_call(functools.partial(layer_kernel, own_j), name='layer', out_...  12.5 us
    all_to_all x1, starting transfers between devices, body(): got = lax.all_to_all(send, 'slab', 0, 0, tiled=True)  11.4 us
    all_to_all x1, blocking collectives, body(): inv = lax.all_to_all(inv, 'slab', 0, 0, tiled=True)  10.5 us
    all_to_all x1, waiting for transfers between devices, body(): grad = lax.all_to_all(grad, 'slab', 0, 0, tiled=True)  7.8 us
    pallas_call x1, Pallas kernels, body(): pl.pallas_call(functools.partial(outer_kernel, own_j), name='outer', grid...  4.15 us
    pallas_call x1, Pallas kernels, body(): pl.pallas_call(functools.partial(transport_kernel, devices), name='transp...  4.02 us
    all_to_all x1, starting transfers between devices, body(): grad = lax.all_to_all(grad, 'slab', 0, 0, tiled=True)  3.52 us
    all_to_all x1, waiting for transfers between devices, body(): got = lax.all_to_all(send, 'slab', 0, 0, tiled=True)  3.21 us
  transfers between devices with their start and end apart: 4, of which 3 were waited for; matrix products, arithmetic and copies ran while one was open for 2% of the time, Pallas kernels for 4%

profile of v3, /device:TPU:0, one launch (start us, length us, event | category | flops | bytes accessed | tf_op | source)
XLA Modules:
  0.0 69.9 jit_solution(16003675695101111538)
XLA Ops:
  0.6 1.3 %pack.1 = (bf16[4,144,128]{2,1,0:T(8,128)(2,1)S(1)}, f32[4,128,128]{2,1,0:T(8,128)S(1)}, f32[4,8,128]{2,1,0:T(8,128)S(1)}) custom-call(f32[4,16384]{1,0:T(4,128)} %conc_hbm.1, f32[4,256]{1,0:T(4,128)} %cover_hbm.1, f32[4,256]{1,0:T(4,128)} %on_hbm.1, f32[4,256]{1,0:T(4,128)} %off_hbm.1, s32[4,256]{1,0:T(4,128)} %mask_hbm.1), custom_call_target="tpu_custom_call" | custom-call | flops 180000000 | bytes 1020000 | tf_op jit(solution)/shard_map/pack/pallas_call | solution.py:517
  1.9 0.0 copy-start.1
  1.9 1.3 %collective-permute-start.1 = (bf16[4,144,128]{2,1,0:T(8,128)(2,1)S(1)}, bf16[4,144,128]{2,1,0:T(8,128)(2,1)S(1)}, u32[]{:S(2)}, u32[]{:S(2)}) collective-permute-start(bf16[4,144,128]{2,1,0:T(8,128)(2,1)S(1)} %get-tuple-element.23), channel_id=1, source_target_pairs={{1,0},{2,1},{3,2},{4,3},{5,4},{6,5},{7,6},{8,7},{9,8},{10,9},{11,1... | collective-permute-start | bytes 442376 | tf_op jit(solution)/shard_map/ppermute | solution.py:534
  3.2 3.0 %collective-permute-start = (bf16[4,144,128]{2,1,0:T(8,128)(2,1)S(1)}, bf16[4,144,128]{2,1,0:T(8,128)(2,1)S(1)}, u32[]{:S(2)}, u32[]{:S(2)}) collective-permute-start(bf16[4,144,128]{2,1,0:T(8,128)(2,1)S(1)} %get-tuple-element.23), channel_id=1, source_target_pairs={{0,1},{1,2},{2,3},{3,4},{4,5},{5,6},{6,7},{7,8},{8,9},{9,10},{10,1... | collective-permute-start | bytes 442376 | tf_op jit(solution)/shard_map/ppermute | solution.py:533
  6.3 0.0 collective-permute-done.1.down
  6.3 1.0 %collective-permute-done.up = bf16[4,144,128]{2,1,0:T(8,128)(2,1)S(1)} collective-permute-done((bf16[4,144,128]{2,1,0:T(8,128)(2,1)S(1)}, bf16[4,144,128]{2,1,0:T(8,128)(2,1)S(1)}, u32[]{:S(2)}, u32[]{:S(2)}) %collective-permute-start) | collective-permute-done | bytes 147488 | tf_op jit(solution)/shard_map/ppermute | solution.py:533
  7.3 4.0 %transport.1 = (f32[4,128,128]{2,1,0:T(8,128)S(1)}, f32[4,256]{1,0:T(4,128)}, f32[128,4,128]{2,1,0:T(4,128)S(1)}, f32[4,256]{1,0:T(4,128)S(1)}, f32[16,128]{1,0:T(8,128)}) custom-call(f32[4,128,128]{2,1,0:T(8,128)S(1)} %get-tuple-element.21.own, f32[4,8,128]{2,1,0:T(8,128)S(1)} %get-tuple-element.22.own_walls, ...), custom_call_target="tpu_custom_call" | custom-call | flops 2220000000 | bytes 12580000 | tf_op jit(solution)/shard_map/transport/pallas_call | solution.py:557
  11.3 0.0 copy-start.6
  11.3 0.0 copy-start.8
  11.3 0.0 copy-start
  11.3 0.0 copy-start.2
  11.4 0.0 copy-start.3
  11.4 0.0 copy-start.4
  11.4 0.0 copy-start.5
  11.4 11.4 %all-to-all-start = ((f32[16,1,128]{2,1,0:T(1,128)}), f32[16,1,128]{2,1,0:T(1,128)S(1)}, u32[]{:S(2)}, u32[]{:S(2)}) async-start(f32[16,1,128]{2,1,0:T(1,128)} %bitcast.2), calls=%async_computation | async-start | bytes 16384 | tf_op jit(solution)/shard_map/all_to_all | solution.py:580
  22.8 0.0 copy-done.1
  22.8 3.1 %prepare.1 = (f32[128,4,128]{2,1,0:T(4,128)S(1)}, f32[3,2,64,128]{3,2,1,0:T(8,128)S(1)}) custom-call(f32[4,16384]{1,0:T(4,128)} %cot_hbm.1, f32[3,64]{1,0:T(4,128)S(1)} %copy-done.1, bf16[2,64,64,128]{3,2,1,0:T(8,128)(2,1)} %bitcast.27), custom_call_target="tpu_custom_call" | custom-call | flops 1200000000 | bytes 6800000 | tf_op jit(solution)/shard_map/prepare/pallas_call | solution.py:535
  25.9 3.2 %all-to-all-done = f32[16,1,128]{2,1,0:T(1,128)S(1)} async-done(((f32[16,1,128]{2,1,0:T(1,128)}), f32[16,1,128]{2,1,0:T(1,128)S(1)}, u32[]{:S(2)}, u32[]{:S(2)}) %all-to-all-start) | async-done | bytes 8224 | tf_op jit(solution)/shard_map/all_to_all | solution.py:580
  29.2 0.0 copy-done.6
  29.2 0.0 copy-done.8
  29.2 1.1 %mixing.1 = (bf16[256,256]{1,0:T(8,128)(2,1)S(1)}, f32[8,256]{1,0:T(8,128)S(1)}) custom-call(f32[16,128]{1,0:T(8,128)S(1)} %bitcast.24, f32[16,256]{1,0:T(8,128)S(1)} %copy-done.8, bf16[2,128,32]{2,1,0:T(8,128)(2,1)S(1)} %copy-done.6, f32[3,2,64,128]{3,2,1,0:T(8,128)S(1)} %get-tuple-element.27.mapped), custom_call_target="tpu_custom_call" | custom-call | flops 960000000 | bytes 5440000 | tf_op jit(solution)/shard_map/mixing/pallas_call | solution.py:582
  30.2 10.5 %all_to_all.33 = bf16[16,16,256]{2,1,0:T(8,128)(2,1)S(1)} all-to-all(bf16[16,16,256]{2,1,0:T(8,128)(2,1)S(1)} %bitcast.23), channel_id=1, replica_groups=mesh['groups'=2,'slab'=16] {'slab'}, dimensions={0} | all-to-all | bytes 262144 | tf_op jit(solution)/shard_map/all_to_all | solution.py:595
  40.8 0.0 copy-done
  40.8 0.0 copy-done.2
  40.8 0.0 copy-done.3
  40.8 0.0 copy-done.4
  40.8 0.0 copy-done.5
  40.8 0.0 copy-start.7
  40.8 12.5 %layer.1 = (f32[4,128,128]{2,1,0:T(8,128)S(1)}, bf16[256,384]{1,0:T(8,128)(2,1)}) custom-call(bf16[256,256]{1,0:T(8,128)(2,1)S(1)} %bitcast.22, f32[128,4,128]{2,1,0:T(4,128)S(1)} %get-tuple-element.29.conc_z, f32[128,4,128]{2,1,0:T(4,128)S(1)} %get-tuple-element.30.cot_z, f32[4,256]{1,0:T(4,128)S(1)} %get-tuple-element.31.cover_z, f32[3,64]{1,0:T(4,128)S(1)} %copy-done.1, ...), custom_call_target="tpu_custom_call" | custom-call | flops 7440000000 | bytes 42160000 | tf_op jit(solution)/shard_map/layer/pallas_call | solution.py:598
  53.3 3.5 %all-to-all-start.2 = ((bf16[16,16,384]{2,1,0:T(8,128)(2,1)}), bf16[16,16,384]{2,1,0:T(8,128)(2,1)S(1)}, u32[]{:S(2)}, u32[]{:S(2)}) async-start(bf16[16,16,384]{2,1,0:T(8,128)(2,1)} %bitcast.9), calls=%async_computation.2 | async-start | bytes 393216 | tf_op jit(solution)/shard_map/all_to_all | solution.py:622
  56.9 1.1 %copy_bitcast_fusion = (f32[4,16384]{1,0:T(4,128)}, f32[4,16384]{1,0:T(4,128)}) fusion(f32[1,4,128,128]{3,2,1,0:T(8,128)S(1)} %bitcast.20, f32[1,4,128,128]{3,2,1,0:T(8,128)S(1)} %bitcast.19), kind=kLoop, calls=%fused_computation | loop fusion | bytes 1048576 | tf_op jit(solution)/shard_map/reshape | solution.py:652
  58.0 7.8 %all-to-all-done.2 = bf16[16,16,384]{2,1,0:T(8,128)(2,1)S(1)} async-done(((bf16[16,16,384]{2,1,0:T(8,128)(2,1)}), bf16[16,16,384]{2,1,0:T(8,128)(2,1)S(1)}, u32[]{:S(2)}, u32[]{:S(2)}) %all-to-all-start.2) | async-done | bytes 196640 | tf_op jit(solution)/shard_map/all_to_all | solution.py:622
  65.8 0.0 copy-done.7
  65.8 4.2 %outer.1 = (f32[2,64,64,128]{3,2,1,0:T(8,128)}, f32[64,64]{1,0:T(8,128)}) custom-call(bf16[256,384]{1,0:T(8,128)(2,1)S(1)} %bitcast.21, f32[8,256]{1,0:T(8,128)S(1)} %get-tuple-element.34.spec, bf16[64,128]{1,0:T(8,128)(2,1)S(1)} %copy-done.7, f32[3,64]{1,0:T(4,128)S(1)} %copy-done.1), custom_call_target="tpu_custom_call" | custom-call | flops 2520000000 | bytes 14280000 | tf_op jit(solution)/shard_map/outer/pallas_call | solution.py:626
Async XLA Ops:
  1.9 20.9 %copy-start.1 = (f32[3,64]{1,0:T(4,128)S(1)}, f32[3,64]{1,0:T(4,128)}, u32[]{:S(2)}) copy-start(f32[3,64]{1,0:T(4,128)} %lift.5) | copy-start | bytes 2308
  1.9 4.3 %collective-permute-start.1 = (bf16[4,144,128]{2,1,0:T(8,128)(2,1)S(1)}, bf16[4,144,128]{2,1,0:T(8,128)(2,1)S(1)}, u32[]{:S(2)}, u32[]{:S(2)}) collective-permute-start(bf16[4,144,128]{2,1,0:T(8,128)(2,1)S(1)} %get-tuple-element.23), channel_id=1, source_target_pairs={{1,0},{2,1},{3,2},{4,3},{5,4},{6,5},{7,6},{8,7},{9,8},{10,9},{11,1... | collective-permute-start | bytes 442376 | tf_op jit(solution)/shard_map/ppermute | solution.py:534
  3.2 4.0 %collective-permute-start = (bf16[4,144,128]{2,1,0:T(8,128)(2,1)S(1)}, bf16[4,144,128]{2,1,0:T(8,128)(2,1)S(1)}, u32[]{:S(2)}, u32[]{:S(2)}) collective-permute-start(bf16[4,144,128]{2,1,0:T(8,128)(2,1)S(1)} %get-tuple-element.23), channel_id=1, source_target_pairs={{0,1},{1,2},{2,3},{3,4},{4,5},{5,6},{6,7},{7,8},{8,9},{9,10},{10,1... | collective-permute-start | bytes 442376 | tf_op jit(solution)/shard_map/ppermute | solution.py:533
  11.3 17.9 %copy-start.6 = (bf16[2,128,32]{2,1,0:T(8,128)(2,1)S(1)}, bf16[2,128,32]{2,1,0:T(8,128)(2,1)}, u32[]{:S(2)}) copy-start(bf16[2,128,32]{2,1,0:T(8,128)(2,1)} %constant.28.clone.bx) | copy-start | bytes 49156
  11.3 17.8 %copy-start.8 = (f32[16,256]{1,0:T(8,128)S(1)}, f32[16,256]{1,0:T(8,128)}, u32[]{:S(2)}) copy-start(f32[16,256]{1,0:T(8,128)} %constant.27.clone.ax) | copy-start | bytes 49156
  11.3 29.4 %copy-start = (bf16[64,64]{1,0:T(8,128)(2,1)S(1)}, bf16[64,64]{1,0:T(8,128)(2,1)}, u32[]{:S(2)}) copy-start(bf16[64,64]{1,0:T(8,128)(2,1)} %point_weight.1) | copy-start | bytes 24580
  11.3 29.4 %copy-start.2 = (f32[64]{0:T(128)S(1)}, f32[64]{0:T(128)}, u32[]{:S(2)}) copy-start(f32[64]{0:T(128)} %param.33) | copy-start | bytes 772
  11.4 29.4 %copy-start.3 = (f32[64]{0:T(128)S(1)}, f32[64]{0:T(128)}, u32[]{:S(2)}) copy-start(f32[64]{0:T(128)} %param.34) | copy-start | bytes 772
  11.4 29.4 %copy-start.4 = (bf16[256,2048]{1,0:T(8,128)(2,1)S(1)}, bf16[256,2048]{1,0:T(8,128)(2,1)}, u32[]{:S(2)}) copy-start(bf16[256,2048]{1,0:T(8,128)(2,1)} %constant.25.clone.ez) | copy-start | bytes 3145732
  11.4 29.4 %copy-start.5 = (bf16[4,144,256]{2,1,0:T(8,128)(2,1)S(1)}, bf16[4,144,256]{2,1,0:T(8,128)(2,1)}, u32[]{:S(2)}) copy-start(bf16[4,144,256]{2,1,0:T(8,128)(2,1)} %constant.26.clone.fwd) | copy-start | bytes 884740
  11.4 17.8 %all-to-all-start = ((f32[16,1,128]{2,1,0:T(1,128)}), f32[16,1,128]{2,1,0:T(1,128)S(1)}, u32[]{:S(2)}, u32[]{:S(2)}) async-start(f32[16,1,128]{2,1,0:T(1,128)} %bitcast.2), calls=%async_computation | async-start | bytes 16384 | tf_op jit(solution)/shard_map/all_to_all | solution.py:580
  40.8 25.0 %copy-start.7 = (bf16[64,128]{1,0:T(8,128)(2,1)S(1)}, bf16[64,128]{1,0:T(8,128)(2,1)}, u32[]{:S(2)}) copy-start(bf16[64,128]{1,0:T(8,128)(2,1)} %constant.29.clone.gx) | copy-start | bytes 49156
  53.3 12.5 %all-to-all-start.2 = ((bf16[16,16,384]{2,1,0:T(8,128)(2,1)}), bf16[16,16,384]{2,1,0:T(8,128)(2,1)S(1)}, u32[]{:S(2)}, u32[]{:S(2)}) async-start(bf16[16,16,384]{2,1,0:T(8,128)(2,1)} %bitcast.9), calls=%async_computation.2 | async-start | bytes 393216 | tf_op jit(solution)/shard_map/all_to_all | solution.py:622

commit v4 on v3

--- a/solution.py
+++ b/solution.py
@@ -18,6 +18,7 @@
 PEAK_SPEED = 0.6
 DIFFUSIVITY = 0.06
 CENTRE = 1.1
+OUT_BLOCKS = 8
 ZG = 4
 
 HI = lax.Precision.HIGHEST
@@ -136,7 +137,20 @@
         packed[x, half:, :] = tail.astype(BF16)
 
 
-def prepare_kernel(cot_hbm, lift, weight_hbm, cot_z, mapped, flat, cot, weight, sems):
+def tanh_units():
+    c1 = math.sqrt(2.0 / math.pi)
+    unit = (c1 * 0.044715) ** (1.0 / 3.0)
+    return unit, c1 / unit
+
+
+def high(v):
+    return v.astype(BF16).astype(F32)
+
+
+def prepare_kernel(
+    cot_hbm, lift, weight_hbm, lift_rows, point_weight, bias, readout,
+    cot_z, mapped, terms, weigh, flat, cot, weight, sems,
+):
     cot_copy = pltpu.make_async_copy(cot_hbm, cot, sems.at[0])
     halves = [pltpu.make_async_copy(weight_hbm.at[p], weight.at[p], sems.at[1 + p]) for p in range(2)]
     for copy in (cot_copy, *halves):
@@ -149,6 +163,33 @@
     for x in range(local_x):
         cot_z[:, x, :] = flat[x].T
     channels = weight.shape[1]
+    rows = local_x * channels
+    unit, _ = tanh_units()
+    factors = jnp.concatenate([lift_rows[...], jnp.zeros((5, channels), F32)], axis=0)
+    pointwise = dot_nt(point_weight[...].astype(F32), factors, HI)
+    eye = (
+        lax.broadcasted_iota(jnp.int32, (channels, channels), 0)
+        == lax.broadcasted_iota(jnp.int32, (channels, channels), 1)
+    ).astype(F32)
+    columns = dot_nt(eye, jnp.concatenate([bias[...], jnp.zeros((7, channels), F32)], axis=0), HI)
+    a0, a1 = unit * pointwise[:, 0:1], unit * pointwise[:, 1:2]
+    a2 = unit * (pointwise[:, 2:3] + columns[:, 0:1]) + CENTRE * a0
+    lane = lax.broadcasted_iota(jnp.int32, (channels, 32), 1)
+    a0_high, a2_high = high(a0), high(a2)
+    for x in range(local_x):
+        block = jnp.zeros((channels, 32), F32)
+        for at, value in (
+            (0, a2_high), (1, a2 - a2_high),
+            (16 + x, a0_high), (20 + x, a0_high), (24 + x, a0 - a0_high), (28 + x, a1),
+        ):
+            block = jnp.where(lane == at, value, block)
+        terms[x * channels : (x + 1) * channels, :] = block.astype(BF16)
+    owner = lax.broadcasted_iota(jnp.int32, (16, rows), 1) // channels
+    slot = lax.broadcasted_iota(jnp.int32, (16, rows), 0)
+    scaled = (0.5 / unit) * jnp.concatenate([readout[...]] * local_x, axis=1)
+    weigh[...] = jnp.where(
+        slot == owner, high(scaled), jnp.where(slot - 8 == owner, scaled - high(scaled), 0.0)
+    ).astype(BF16)
     for p in range(2):
         halves[p].wait()
         acc = [jnp.zeros(weight.shape[2:], F32) for _ in range(3)]
@@ -159,10 +200,14 @@
             mapped[r, p] = acc[r]
 
 
-def transport_kernel(
-    devices, own, own_walls, up, down, index_hbm, profiles_hbm, perm_hbm, back_hbm, wave_hbm, place_c_hbm, place_w_hbm,
-    conc_out, cover_out, conc_z, cover_z, send,
-    buf, index, profiles, perm, back, wave_yt, place_c, place_w, sems,
+def split_parity(spread, at, count):
+    wide = spread.shape[1] // 2
+    return spread[at : at + count, :wide] + spread[at + 4 : at + 4 + count, wide:]
+
+
+def early_kernel(
+    own, own_walls, index_hbm, profiles_hbm, perm_hbm, back_hbm, wave_hbm, place_c_hbm, place_w_hbm,
+    planes, fields, inlet, perm, back, wave_yt, place_c, place_w, index, profiles, sems,
 ):
     moves = (
         (index_hbm, index), (perm_hbm, perm), (profiles_hbm, profiles), (wave_hbm, wave_yt),
@@ -173,36 +218,52 @@
         copy.start()
     local_x = own.shape[0]
     half = own.shape[1]
-    depth = profiles.shape[1]
-    rows = 3 * local_x
-    walls = []
-    for r in range(rows):
-        x = r % local_x
-        if r // local_x == 1:
-            buf[0, r] = own[x].T
-            walls.append(own_walls[x])
-        else:
-            ref = up if r < local_x else down
-            buf[0, r] = (ref[x, :half, :].astype(F32) + CENTRE).T
-            walls.append(ref[x, half:, :].astype(F32)[:8])
+    for x in range(local_x):
+        planes[x] = own[x].T
     for copy in copies[:3]:
         copy.wait()
     profile = index[...].astype(F32)
-    walls.append(jnp.concatenate([profile[:, :half], profile[:, half:], jnp.zeros((6, half), F32)], axis=0))
+    gap = jnp.zeros((3, half), F32)
+    walls = [own_walls[x] for x in range(local_x)]
+    walls.append(jnp.concatenate([profile[:, :half], gap, profile[:, half:], gap], axis=0))
     spread = dot(jnp.concatenate(walls, axis=0), perm[...], HI)
-    fields = [
-        spread[8 * r : 8 * r + 4, : 2 * half] + spread[8 * r + 4 : 8 * r + 8, 2 * half :]
-        for r in range(rows)
-    ]
-    chosen = spread[8 * rows : 8 * rows + 1, : 2 * half] + spread[8 * rows + 1 : 8 * rows + 2, 2 * half :]
+    for x in range(local_x):
+        fields[4 * x : 4 * x + 4] = split_parity(spread, 8 * x, 4)
+    chosen = split_parity(spread, 8 * local_x, 1)
     pick = lax.broadcasted_iota(jnp.int32, (PROFILES, 2 * half), 0).astype(F32)
     onehot = (jnp.abs(pick - chosen) < 0.5).astype(F32)
-    inlet = dot_tn(profiles[...], onehot, HI)
-    inlet = jnp.concatenate([inlet[:, :half], inlet[:, half:]], axis=0)
+    plane = dot_tn(profiles[...], onehot, HI)
+    inlet[...] = jnp.concatenate([plane[:, :half], plane[:, half:]], axis=0)
+    for copy in copies[3:]:
+        copy.wait()
+
+
+def transport_kernel(
+    devices, up, down, own, own_fields, inlet, perm, back, wave_yt, place_c, place_w,
+    conc_out, cover_out, conc_z, cover_z, send, buf,
+):
+    local_x = own.shape[0]
+    half = own.shape[2]
+    depth = own.shape[1] // 2
+    rows = 3 * local_x
+    sides = [r for r in range(rows) if r // local_x != 1]
+    walls = []
+    for r in sides:
+        ref = up if r < local_x else down
+        buf[0, r] = (ref[r % local_x, :half, :].astype(F32) + CENTRE).T
+        walls.append(ref[r % local_x, half:, :].astype(F32)[:8])
+    for x in range(local_x):
+        buf[0, local_x + x] = own[x]
+    spread = dot(jnp.concatenate(walls, axis=0), perm[...], HI)
+    fields = [own_fields[4 * (r % local_x) : 4 * (r % local_x) + 4] for r in range(rows)]
+    for k, r in enumerate(sides):
+        fields[r] = split_parity(spread, 8 * k, 4)
     height = lax.broadcasted_iota(jnp.int32, (depth, half), 0).astype(F32)
     height = (height + 0.5) / depth
     speed = PEAK_SPEED * 4.0 * height * (1.0 - height)
     speed = jnp.concatenate([speed, speed], axis=0)
+    keep = (1.0 - 6.0 * DIFFUSIVITY) - speed
+    carried = DIFFUSIVITY + speed
     first = lax.axis_index("slab") == 0
     last = lax.axis_index("slab") == devices - 1
     cover = [f[0:1] for f in fields]
@@ -213,7 +274,7 @@
             behind = buf[cur, r - 1]
             ahead = buf[cur, r + 1]
             if r == local_x:
-                behind = jnp.where(first, inlet, behind)
+                behind = jnp.where(first, inlet[...], behind)
             if r == 2 * local_x - 1:
                 ahead = jnp.where(last, c, ahead)
             even, odd = c[:depth], c[depth:]
@@ -222,17 +283,15 @@
             )
             below = jnp.concatenate([even[:1], even[:-1], odd[:1], odd[:-1]], axis=0)
             above = jnp.concatenate([even[1:], even[-1:], odd[1:], odd[-1:]], axis=0)
-            laplace = behind + ahead + side + below + above - 6.0 * c
+            around = ahead + side + below + above
             f = fields[r]
             wall = jnp.concatenate([even[:1], odd[:1]], axis=1)
             uptake = f[3:4] * (f[1:2] * wall * (1.0 - cover[r]) - f[2:3] * cover[r])
-            new = c + DIFFUSIVITY * laplace - speed * (c - behind)
+            new = keep * c + carried * behind + DIFFUSIVITY * around
             buf[nxt, r] = new
             buf[nxt, r, 0:1] = new[0:1] - uptake[:, :half]
             buf[nxt, r, depth : depth + 1] = new[depth : depth + 1] - uptake[:, half:]
             cover[r] = cover[r] + uptake
-    for copy in copies[3:]:
-        copy.wait()
     cur = STEPS % 2
     covers = jnp.concatenate(cover[local_x : 2 * local_x], axis=0)
     cover_z[...] = covers
@@ -302,10 +361,10 @@
 
 
 def layer_kernel(
-    own_j, inv, conc_z, cot_z, cover_z, lift, point_weight, bias, readout, ez, fwd,
+    own_j, inv, conc_z, cot_z, cover_z, terms, weigh, readout, ez, fwd,
     pred_out, grad_out, lhs, ext_all, waves, pred, point, pre_a, pre_b, hidden_a, hidden_b, grads_a, grads_b,
 ):
-    channels = lift.shape[1]
+    channels = readout.shape[1]
     local_x = cover_z.shape[0]
     half = cot_z.shape[2]
     span = 2 * half
@@ -315,45 +374,14 @@
     pairs = 2 * KY
     wide = ZG * pairs
     iscale = 1.0 / math.sqrt(KX * KY * KZ)
-    c1 = math.sqrt(2.0 / math.pi)
-    unit = (c1 * 0.044715) ** (1.0 / 3.0)
-    kappa = c1 / unit
-
-    def high(v):
-        return v.astype(BF16).astype(F32)
-
-    factors = jnp.concatenate([lift[...], jnp.zeros((5, channels), F32)], axis=0)
-    mapped = dot_nt(point_weight[...].astype(F32), factors, HI)
-    eye = (
-        lax.broadcasted_iota(jnp.int32, (channels, channels), 0)
-        == lax.broadcasted_iota(jnp.int32, (channels, channels), 1)
-    ).astype(F32)
-    columns = dot_nt(eye, jnp.concatenate([bias[...], jnp.zeros((7, channels), F32)], axis=0), HI)
-    a0, a1 = unit * mapped[:, 0:1], unit * mapped[:, 1:2]
-    a2 = unit * (mapped[:, 2:3] + columns[:, 0:1]) + CENTRE * a0
-
-    lane = lax.broadcasted_iota(jnp.int32, (channels, 32), 1)
-    a0_high, a2_high = high(a0), high(a2)
-    for x in range(local_x):
-        block = jnp.zeros((channels, 32), F32)
-        for at, value in (
-            (0, a2_high), (1, a2 - a2_high),
-            (16 + x, a0_high), (20 + x, a0_high), (24 + x, a0 - a0_high), (28 + x, a1),
-        ):
-            block = jnp.where(lane == at, value, block)
-        block = block.astype(BF16)
-        for g in range(groups):
-            lhs[g, x * channels : (x + 1) * channels, wide : wide + 32] = block
+    unit, kappa = tanh_units()
     flipped = inv[...].astype(F32).T.astype(BF16)
     lifted = (unit * dot(flipped, ez[...])).astype(BF16)
     for g in range(groups):
-        lhs[g, :, :wide] = lifted[:, g * wide : (g + 1) * wide]
+        lhs[g] = lifted[:, g * wide : (g + 1) * wide]
     wide_readout = jnp.concatenate([readout[...]] * local_x, axis=1)
     owner = lax.broadcasted_iota(jnp.int32, (16, rows), 1) // channels
     slot = lax.broadcasted_iota(jnp.int32, (16, rows), 0)
-    scaled = (0.5 / unit) * wide_readout
-    weigh = jnp.where(slot == owner, high(scaled), jnp.where(slot - 8 == owner, scaled - high(scaled), 0.0))
-    weigh = weigh.astype(BF16)
     point[...] = jnp.zeros(point.shape, F32)
     grads_b[...] = jnp.zeros(grads_b.shape, BF16)
     hidden_b[...] = jnp.zeros(hidden_b.shape, BF16)
@@ -367,10 +395,11 @@
         wall = jnp.where(z == 0, cover_z[...], 0.0)
         ext = jnp.concatenate([conc_high, conc - conc_high, conc_high, wall], axis=0).astype(BF16)
         ext_all[z] = ext
-        pre[...] = dot(lhs[g], jnp.concatenate([fwd[i], ext], axis=0))
+        both = jnp.concatenate([lhs[g], terms[...]], axis=1)
+        pre[...] = dot(both, jnp.concatenate([fwd[i], ext], axis=0))
 
     def after(z, hidden, grad):
-        line = dot(weigh, hidden[...])
+        line = dot(weigh[...], hidden[...])
         line = line[:local_x] + line[8 : 8 + local_x]
         pred[z] = line[:, :half]
         pred[depth + z] = line[:, half:]
@@ -426,63 +455,74 @@
         grad_out[:, rows + b * 128 : rows + (b + 1) * 128] = dot(pick, both).astype(BF16)
 
 
-def outer_kernel(own_j, got, spec, gx, lift, modes_out, point_out, v_r, v_i, d_r, d_i, stage):
+def outer_kernel(own_j, got, spec, gx, lift, modes_hbm, point_out, result, factor, stage, sems):
     channels = lift.shape[1]
     modes = spec.shape[1] // 2
     rows = got.shape[1] - 128 * tail_blocks(own_j)
     local_x = rows // channels
-    per = modes_out.shape[1]
-
-    @pl.when(pl.program_id(0) == 0)
-    def _():
-        factors = jnp.concatenate([lift[...], jnp.zeros((5, channels), F32)], axis=0)
-        v = dot_tn(factors, spec[...], HI)
-        v_r[...] = v[:, :modes]
-        v_i[...] = v[:, modes:]
-        blocks = got.shape[0] // own_j
-        halves = rows // 128
-        for h in range(halves):
-            stage[h] = got[:, h * 128 : (h + 1) * 128].astype(F32)
-        lines = [
-            [stage[h, pl.ds(j, blocks, own_j), :] if own_j > 1 else stage[h] for h in range(halves)]
-            for j in range(own_j)
-        ]
-        per_half = 128 // channels
-        parts_r, parts_i = [], []
-        tall = []
-        for x in range(local_x):
-            h, at = x // per_half, (x % per_half) * channels
-            tall.append(jnp.concatenate([lines[j][h][:, at : at + channels] for j in range(own_j)], axis=1))
-        acc = dot(gx[...], jnp.concatenate(tall, axis=0).astype(BF16))
-        acc = acc[: 2 * KX] + acc[2 * KX :]
-        for j in range(own_j):
-            parts_r.append(acc[:KX, j * channels : (j + 1) * channels])
-            parts_i.append(acc[KX:, j * channels : (j + 1) * channels])
-        d_r[...] = jnp.concatenate(parts_r, axis=0).T
-        d_i[...] = jnp.concatenate(parts_i, axis=0).T
-        sums = jnp.zeros((8, 128), F32)
-        for b in range(tail_blocks(own_j)):
-            tail = got[:, rows + b * 128 : rows + (b + 1) * 128]
-            at = lax.broadcasted_iota(jnp.int32, (8, got.shape[0]), 1) % (2 * own_j) + b * 2 * own_j
-            pick = (at == lax.broadcasted_iota(jnp.int32, (8, got.shape[0]), 0)).astype(BF16)
-            sums = sums + dot(pick, tail)
-        sums = sums[:, :channels] + sums[:, channels:]
-        row = lax.broadcasted_iota(jnp.int32, (8, channels), 0)
-        base = jnp.where(row == 2, factors + CENTRE * lift[0:1], factors)
-        point_out[...] = dot_tn(jnp.where(row < 3, sums, 0.0), base, HI)
-
-    start = pl.program_id(0) * per
-    dr = d_r[...]
-    di = d_i[...]
-    for c in range(per):
-        vr = v_r[pl.ds(start + c, 1), :]
-        vi = v_i[pl.ds(start + c, 1), :]
-        modes_out[0, c] = vr * dr + vi * di
-        modes_out[1, c] = vr * di - vi * dr
+    factors = jnp.concatenate([lift[...], jnp.zeros((5, channels), F32)], axis=0)
+    v = dot_tn(factors, spec[...], HI)
+    v_r, v_i = v[:, :modes], v[:, modes:]
+    blocks = got.shape[0] // own_j
+    halves = rows // 128
+    for h in range(halves):
+        stage[h] = got[:, h * 128 : (h + 1) * 128].astype(F32)
+    lines = [
+        [stage[h, pl.ds(j, blocks, own_j), :] if own_j > 1 else stage[h] for h in range(halves)]
+        for j in range(own_j)
+    ]
+    per_half = 128 // channels
+    parts_r, parts_i = [], []
+    tall = []
+    for x in range(local_x):
+        h, at = x // per_half, (x % per_half) * channels
+        tall.append(jnp.concatenate([lines[j][h][:, at : at + channels] for j in range(own_j)], axis=1))
+    acc = dot(gx[...], jnp.concatenate(tall, axis=0).astype(BF16))
+    acc = acc[: 2 * KX] + acc[2 * KX :]
+    for j in range(own_j):
+        parts_r.append(acc[:KX, j * channels : (j + 1) * channels])
+        parts_i.append(acc[KX:, j * channels : (j + 1) * channels])
+    dr = jnp.concatenate(parts_r, axis=0).T
+    di = jnp.concatenate(parts_i, axis=0).T
+    factor[0], factor[1] = v_r, v_i
+    per = channels // OUT_BLOCKS
+
+    def leave(b, q):
+        here = pl.ds(b * per, per)
+        return pltpu.make_async_copy(result.at[q, here], modes_hbm.at[q, here], sems.at[q, b])
+
+    def block(b, carry):
+        for k in range(per):
+            c = b * per + k
+            vr, vi = factor[0, pl.ds(c, 1), :], factor[1, pl.ds(c, 1), :]
+            result[0, c] = vr * dr + vi * di
+            result[1, c] = vr * di - vi * dr
+        leave(b, 0).start()
+        leave(b, 1).start()
+        return carry
+
+    lax.fori_loop(0, OUT_BLOCKS, block, 0)
+    sums = jnp.zeros((8, 128), F32)
+    for b in range(tail_blocks(own_j)):
+        tail = got[:, rows + b * 128 : rows + (b + 1) * 128]
+        at = lax.broadcasted_iota(jnp.int32, (8, got.shape[0]), 1) % (2 * own_j) + b * 2 * own_j
+        pick = (at == lax.broadcasted_iota(jnp.int32, (8, got.shape[0]), 0)).astype(BF16)
+        sums = sums + dot(pick, tail)
+    sums = sums[:, :channels] + sums[:, channels:]
+    row = lax.broadcasted_iota(jnp.int32, (8, channels), 0)
+    base = jnp.where(row == 2, factors + CENTRE * lift[0:1], factors)
+    point_out[...] = dot_tn(jnp.where(row < 3, sums, 0.0), base, HI)
+    for b in range(OUT_BLOCKS):
+        leave(b, 0).wait()
+        leave(b, 1).wait()
 
 
 def params(mib):
     return pltpu.CompilerParams(vmem_limit_bytes=mib * 1024 * 1024)
+
+
+def cost(micros):
+    return pl.CostEstimate(flops=int(micros * 6e8), transcendentals=0, bytes_accessed=int(micros * 3.4e6))
 
 
 def in_hbm(array):
@@ -528,19 +568,21 @@
         + [pltpu.VMEM(cover_init.shape, F32)] * 3
         + [pltpu.VMEM(site_mask.shape, jnp.int32), pltpu.SemaphoreType.DMA((5,))],
         compiler_params=params(4),
-        cost_estimate=pl.CostEstimate(flops=180000000, transcendentals=0, bytes_accessed=1020000),
+        cost_estimate=cost(0.3),
     )(*map(in_hbm, (conc_init, cover_init, rate_on, rate_off, site_mask)))
     up = lax.ppermute(pack, "slab", [(i, i + 1) for i in range(devices - 1)])
     down = lax.ppermute(pack, "slab", [(i + 1, i) for i in range(devices - 1)])
-    cot_z, mapped = pl.pallas_call(
+    cot_z, mapped, terms, weigh = pl.pallas_call(
         prepare_kernel,
         name="prepare",
         out_shape=(
             sds((2 * depth, local_x, half), F32),
             sds((3, 2, channels, modes), F32),
+            sds((local_x * channels, 32), BF16),
+            sds((16, local_x * channels), BF16),
         ),
-        in_specs=hbm(1) + [smem] + hbm(1),
-        out_specs=vmem(2),
+        in_specs=hbm(1) + [smem] + hbm(1) + vmem(4),
+        out_specs=vmem(4),
         scratch_shapes=[
             pltpu.VMEM((local_x, half, 2 * depth), F32),
             pltpu.VMEM(cotangent.shape, F32),
@@ -548,12 +590,29 @@
             pltpu.SemaphoreType.DMA((3,)),
         ],
         compiler_params=params(8),
-        cost_estimate=pl.CostEstimate(flops=1200000000, transcendentals=0, bytes_accessed=6800000),
-    )(in_hbm(cotangent), lift, in_hbm(mode_weight.transpose(1, 2, 3, 0)))
-    fixed = (
-        inlet_index.reshape(1, span), inlet_profiles,
-        tab["perm"], tab["back"], tab["wave_yt"], tab["place_c"], tab["place_w"],
+        cost_estimate=cost(2.0),
+    )(
+        in_hbm(cotangent), lift, in_hbm(mode_weight.transpose(1, 2, 3, 0)),
+        lift, point_weight, point_bias.reshape(1, -1), readout.reshape(1, -1),
     )
+    constants = [tab[k] for k in ("perm", "back", "wave_yt", "place_c", "place_w")]
+    early = pl.pallas_call(
+        early_kernel,
+        name="early",
+        out_shape=(
+            sds((local_x, 2 * depth, half), F32),
+            sds((4 * local_x, span), F32),
+            sds((2 * depth, half), F32),
+            *(sds(v.shape, v.dtype) for v in constants),
+        ),
+        in_specs=vmem(2) + hbm(7),
+        out_specs=vmem(8),
+        scratch_shapes=[
+            pltpu.VMEM((1, span), jnp.int32), pltpu.VMEM(inlet_profiles.shape, F32), pltpu.SemaphoreType.DMA((7,)),
+        ],
+        compiler_params=params(8),
+        cost_estimate=cost(1.5),
+    )(conc, walls, *map(in_hbm, (inlet_index.reshape(1, span), inlet_profiles, *constants)))
     conc_out, cover_out, conc_z, cover_z, send = pl.pallas_call(
         functools.partial(transport_kernel, devices),
         name="transport",
@@ -564,16 +623,12 @@
             sds((local_x, span), F32),
             sds((KY, 4 * local_x * KZ), F32),
         ),
-        in_specs=vmem(4) + hbm(7),
+        in_specs=vmem(10),
         out_specs=vmem(5),
-        scratch_shapes=[pltpu.VMEM((2, 3 * local_x, 2 * depth, half), F32)]
-        + [pltpu.VMEM(v.shape, v.dtype) for v in fixed]
-        + [pltpu.SemaphoreType.DMA((len(fixed),))],
+        scratch_shapes=[pltpu.VMEM((2, 3 * local_x, 2 * depth, half), F32)],
         compiler_params=params(8),
-        cost_estimate=pl.CostEstimate(flops=2220000000, transcendentals=0, bytes_accessed=12580000),
-    )(
-        conc, walls, up, down, *map(in_hbm, fixed),
-    )
+        cost_estimate=cost(3.0),
+    )(up, down, *early)
     if own_j != KZ:
         send = send.reshape(KY, 4 * local_x, KZ // own_j, own_j).transpose(0, 2, 1, 3)
         send = send.reshape(devices, 4 * local_x * own_j)
@@ -590,7 +645,7 @@
         out_specs=vmem(2),
         scratch_shapes=[pltpu.VMEM((local_x * channels // 128, 2 * KY * KZ, 128), F32)],
         compiler_params=params(4),
-        cost_estimate=pl.CostEstimate(flops=960000000, transcendentals=0, bytes_accessed=5440000),
+        cost_estimate=cost(1.6),
     )(got, tab["ax"], tab["bx"], mapped)
     inv = lax.all_to_all(inv, "slab", 0, 0, tiled=True)
     rows = local_x * channels
@@ -602,10 +657,10 @@
             sds((local_x, half, 2 * depth), F32),
             sds((2 * KY * KZ, rows + 128 * tail_blocks(own_j)), BF16),
         ),
-        in_specs=vmem(10),
+        in_specs=vmem(9),
         out_specs=vmem(2),
         scratch_shapes=[
-            pltpu.VMEM((depth // ZG, rows, wide + 32), BF16),
+            pltpu.VMEM((depth // ZG, rows, wide), BF16),
             pltpu.VMEM((depth, 16, span), BF16),
             pltpu.VMEM((depth * 2 * KY, rows), BF16),
             pltpu.VMEM((2 * depth, local_x, half), F32),
@@ -614,37 +669,28 @@
         + [pltpu.VMEM((rows, span), F32)] * 2
         + [pltpu.VMEM((rows, span), BF16)] * 4,
         compiler_params=params(16),
-        cost_estimate=pl.CostEstimate(flops=7440000000, transcendentals=0, bytes_accessed=42160000),
+        cost_estimate=cost(12.4),
     )(
-        inv, conc_z, cot_z, cover_z, lift, point_weight, point_bias.reshape(1, -1), readout.reshape(1, -1),
-        tab["ez"], tab["fwd"],
+        inv, conc_z, cot_z, cover_z, terms, weigh, readout.reshape(1, -1), tab["ez"], tab["fwd"],
     )
     grad = lax.all_to_all(grad, "slab", 0, 0, tiled=True)
-    blocks = 8
-    per = channels // blocks
-    whole = lambda s: pl.BlockSpec(s, lambda i: (0,) * len(s))
     grad_modes, grad_point = pl.pallas_call(
         functools.partial(outer_kernel, own_j),
         name="outer",
-        grid=(blocks,),
         out_shape=(
             sds((2, channels, channels, modes), F32),
             sds((channels, channels), F32),
         ),
-        in_specs=[whole(grad.shape), whole(spec.shape), whole(tab["gx"].shape), whole(lift.shape)],
-        out_specs=(
-            pl.BlockSpec((2, per, channels, modes), lambda i: (0, i, 0, 0)),
-            whole((channels, channels)),
-        ),
+        in_specs=vmem(4),
+        out_specs=hbm(1) + vmem(1),
         scratch_shapes=[
-            pltpu.VMEM((channels, modes), F32),
-            pltpu.VMEM((channels, modes), F32),
-            pltpu.VMEM((channels, modes), F32),
-            pltpu.VMEM((channels, modes), F32),
+            pltpu.VMEM((2, channels, channels, modes), F32),
+            pltpu.VMEM((2, channels, modes), F32),
             pltpu.VMEM((rows // 128, 2 * KY * KZ, 128), F32),
+            pltpu.SemaphoreType.DMA((2, OUT_BLOCKS)),
         ],
-        compiler_params=params(8),
-        cost_estimate=pl.CostEstimate(flops=2520000000, transcendentals=0, bytes_accessed=14280000),
+        compiler_params=params(12),
+        cost_estimate=cost(3.0),
     )(grad, spec, tab["gx"], lift)
     return (
         conc_out.reshape(local_x, plane),

time: 70.4 us -> 68.2 us (0.969)
  waiting for transfers between devices: 12 us -> 10.9 us
    pallas_call x1, Pallas kernels: 4.02 us -> 2.99 us  [body(): pl.pallas_call(functools.partial(transport_kernel, devices), name='transp...]
    ppermute x1, waiting for transfers between devices: 0.97 us -> 0.01 us  [body(): up = lax.ppermute(pack, 'slab', [(i, i + 1) for i in range(devices - 1)])]
    pallas_call x1 -> x2, Pallas kernels: 4.15 us -> 4.79 us  [the longest x1 3.23 us: body(): pl.pallas_call(functools.partial(outer_kernel, own_j), name='outer', out_...]
  transfers between devices with their start and end apart: 4 -> 4, of which waited for: 3 -> 2; matrix products, arithmetic and copies ran while one was open for 2% -> 2% of each run, Pallas kernels for 4% -> 7%
where the time goes in v4:
time: 68.2 us; the launch traced here: 67.8 us
  Pallas kernels  25.7 us (38%)
  starting transfers between devices  18.6 us (27%)
  waiting for transfers between devices  10.9 us (16%)
  blocking collectives  10.7 us (16%)
  local copies, waits for them, and re-layouts  1.18 us (2%)
  between operations  0.8 us (1%)
    pallas_call x1, Pallas kernels, body(): pl.pallas_call(functools.partial(layer_kernel, own_j), name='layer', out_...  12.3 us
    all_to_all x1, starting transfers between devices, body(): got = lax.all_to_all(send, 'slab', 0, 0, tiled=True)  10.7 us
    all_to_all x1, blocking collectives, body(): inv = lax.all_to_all(inv, 'slab', 0, 0, tiled=True)  10.7 us
    all_to_all x1, waiting for transfers between devices, body(): grad = lax.all_to_all(grad, 'slab', 0, 0, tiled=True)  7.8 us
    all_to_all x1, starting transfers between devices, body(): grad = lax.all_to_all(grad, 'slab', 0, 0, tiled=True)  3.52 us
    pallas_call x1, Pallas kernels, body(): pl.pallas_call(prepare_kernel, name='prepare', out_shape=(sds((2 * depth,...  3.24 us
    pallas_call x1, Pallas kernels, body(): pl.pallas_call(functools.partial(outer_kernel, own_j), name='outer', out_...  3.23 us
    all_to_all x1, waiting for transfers between devices, body(): got = lax.all_to_all(send, 'slab', 0, 0, tiled=True)  3.07 us
  transfers between devices with their start and end apart: 4, of which 2 were waited for; matrix products, arithmetic and copies ran while one was open for 2% of the time, Pallas kernels for 7%

profile of v4, /device:TPU:0, one launch (start us, length us, event | category | flops | bytes accessed | tf_op | source)
XLA Modules:
  0.0 67.8 jit_solution(14700978165346884326)
XLA Ops:
  0.6 1.3 %pack.1 = (bf16[4,144,128]{2,1,0:T(8,128)(2,1)S(1)}, f32[4,128,128]{2,1,0:T(8,128)S(1)}, f32[4,8,128]{2,1,0:T(8,128)S(1)}) custom-call(f32[4,16384]{1,0:T(4,128)} %conc_hbm.1, f32[4,256]{1,0:T(4,128)} %cover_hbm.1, f32[4,256]{1,0:T(4,128)} %on_hbm.1, f32[4,256]{1,0:T(4,128)} %off_hbm.1, s32[4,256]{1,0:T(4,128)} %mask_hbm.1), custom_call_target="tpu_custom_call" | custom-call | flops 180000000 | bytes 1020000 | tf_op jit(solution)/shard_map/pack/pallas_call | solution.py:557
  1.9 1.3 %collective-permute-start.1 = (bf16[4,144,128]{2,1,0:T(8,128)(2,1)S(1)}, bf16[4,144,128]{2,1,0:T(8,128)(2,1)S(1)}, u32[]{:S(2)}, u32[]{:S(2)}) collective-permute-start(bf16[4,144,128]{2,1,0:T(8,128)(2,1)S(1)} %get-tuple-element.31), channel_id=1, source_target_pairs={{1,0},{2,1},{3,2},{4,3},{5,4},{6,5},{7,6},{8,7},{9,8},{10,9},{11,1... | collective-permute-start | bytes 442376 | tf_op jit(solution)/shard_map/ppermute | solution.py:574
  3.2 3.0 %collective-permute-start = (bf16[4,144,128]{2,1,0:T(8,128)(2,1)S(1)}, bf16[4,144,128]{2,1,0:T(8,128)(2,1)S(1)}, u32[]{:S(2)}, u32[]{:S(2)}) collective-permute-start(bf16[4,144,128]{2,1,0:T(8,128)(2,1)S(1)} %get-tuple-element.31), channel_id=1, source_target_pairs={{0,1},{1,2},{2,3},{3,4},{4,5},{5,6},{6,7},{7,8},{8,9},{9,10},{10,1... | collective-permute-start | bytes 442376 | tf_op jit(solution)/shard_map/ppermute | solution.py:573
  6.3 0.0 copy-start
  6.3 0.0 copy-start.1
  6.3 0.0 copy-start.2
  6.3 0.0 copy-start.3
  6.3 1.6 %early.1 = (f32[4,128,128]{2,1,0:T(8,128)S(1)}, f32[16,256]{1,0:T(8,128)S(1)}, f32[128,128]{1,0:T(8,128)S(1)}, f32[128,512]{1,0:T(8,128)S(1)}, f32[256,256]{1,0:...) custom-call(f32[4,128,128]{2,1,0:T(8,128)S(1)} %get-tuple-element.32.own, ...), custom_call_target="tpu_custom_call" | custom-call | flops 900000000 | bytes 5100000 | tf_op jit(solution)/shard_map/early/pallas_call | solution.py:599
  7.9 0.0 collective-permute-done.1.down
  7.9 0.0 collective-permute-done.up
  7.9 0.0 copy-start.6
  7.9 0.0 copy-start.8
  7.9 3.0 %transport.1 = (f32[4,128,128]{2,1,0:T(8,128)S(1)}, f32[4,256]{1,0:T(4,128)}, f32[128,4,128]{2,1,0:T(4,128)S(1)}, f32[4,256]{1,0:T(4,128)S(1)}, f32[16,128]{1,0:T(8,128)}) custom-call(bf16[4,144,128]{2,1,0:T(8,128)(2,1)S(1)} %collective-permute-done.up, bf16[4,144,128]{2,1,0:T(8,128)(2,1)S(1)} %collective-permute-done.1.down, ...), custom_call_target="tpu_custom_call" | custom-call | flops 1800000000 | bytes 10200000 | tf_op jit(solution)/shard_map/transport/pallas_call | solution.py:616
  10.9 0.0 copy-start.4
  10.9 0.0 copy-start.5
  10.9 10.7 %all-to-all-start = ((f32[16,1,128]{2,1,0:T(1,128)}), f32[16,1,128]{2,1,0:T(1,128)S(1)}, u32[]{:S(2)}, u32[]{:S(2)}) async-start(f32[16,1,128]{2,1,0:T(1,128)} %bitcast.2), calls=%async_computation | async-start | bytes 16384 | tf_op jit(solution)/shard_map/all_to_all | solution.py:635
  21.7 0.0 copy-done
  21.7 0.0 copy-done.1
  21.7 0.0 copy-done.2
  21.7 0.0 copy-done.3
  21.7 3.2 %prepare.1 = (f32[128,4,128]{2,1,0:T(4,128)S(1)}, f32[3,2,64,128]{3,2,1,0:T(8,128)S(1)}, bf16[256,32]{1,0:T(8,128)(2,1)S(1)}, bf16[16,256]{1,0:T(8,128)(2,1)S(1)}) custom-call(f32[4,16384]{1,0:T(4,128)} %cot_hbm.1, f32[3,64]{1,0:T(4,128)S(1)} %copy-done.1, bf16[2,64,64,128]{3,2,1,0:T(8,128)(2,1)} %bitcast.28, f32[3,64]{1,0:T(4,128)S(1)} %copy-done.1, ...), custom_call_target="tpu_custom_call" | custom-call | flops 1200000000 | bytes 6800000 | tf_op jit(solution)/shard_map/prepare/pallas_call | solution.py:575
  24.9 3.1 %all-to-all-done = f32[16,1,128]{2,1,0:T(1,128)S(1)} async-done(((f32[16,1,128]{2,1,0:T(1,128)}), f32[16,1,128]{2,1,0:T(1,128)S(1)}, u32[]{:S(2)}, u32[]{:S(2)}) %all-to-all-start) | async-done | bytes 8224 | tf_op jit(solution)/shard_map/all_to_all | solution.py:635
  28.0 0.0 copy-done.6
  28.0 0.0 copy-done.8
  28.0 1.1 %mixing.1 = (bf16[256,256]{1,0:T(8,128)(2,1)S(1)}, f32[8,256]{1,0:T(8,128)S(1)}) custom-call(f32[16,128]{1,0:T(8,128)S(1)} %bitcast.24, f32[16,256]{1,0:T(8,128)S(1)} %copy-done.8, bf16[2,128,32]{2,1,0:T(8,128)(2,1)S(1)} %copy-done.6, f32[3,2,64,128]{3,2,1,0:T(8,128)S(1)} %get-tuple-element.45.mapped), custom_call_target="tpu_custom_call" | custom-call | flops 960000000 | bytes 5440000 | tf_op jit(solution)/shard_map/mixing/pallas_call | solution.py:637
  29.1 10.7 %all_to_all.33 = bf16[16,16,256]{2,1,0:T(8,128)(2,1)S(1)} all-to-all(bf16[16,16,256]{2,1,0:T(8,128)(2,1)S(1)} %bitcast.23), channel_id=1, replica_groups=mesh['groups'=2,'slab'=16] {'slab'}, dimensions={0} | all-to-all | bytes 262144 | tf_op jit(solution)/shard_map/all_to_all | solution.py:650
  39.8 0.0 copy-done.4
  39.8 0.0 copy-done.5
  39.8 0.0 copy-start.7
  39.8 12.3 %layer.1 = (f32[4,128,128]{2,1,0:T(8,128)S(1)}, bf16[256,384]{1,0:T(8,128)(2,1)}) custom-call(bf16[256,256]{1,0:T(8,128)(2,1)S(1)} %bitcast.22, f32[128,4,128]{2,1,0:T(4,128)S(1)} %get-tuple-element.47.conc_z, f32[128,4,128]{2,1,0:T(4,128)S(1)} %get-tuple-element.48.cot_z, f32[4,256]{1,0:T(4,128)S(1)} %get-tuple-element.49.cover_z, ...), custom_call_target="tpu_custom_call" | custom-call | flops 7440000000 | bytes 42160000 | tf_op jit(solution)/shard_map/layer/pallas_call | solution.py:653
  52.1 3.5 %all-to-all-start.2 = ((bf16[16,16,384]{2,1,0:T(8,128)(2,1)}), bf16[16,16,384]{2,1,0:T(8,128)(2,1)S(1)}, u32[]{:S(2)}, u32[]{:S(2)}) async-start(bf16[16,16,384]{2,1,0:T(8,128)(2,1)} %bitcast.9), calls=%async_computation.2 | async-start | bytes 393216 | tf_op jit(solution)/shard_map/all_to_all | solution.py:676
  55.6 1.1 %copy_bitcast_fusion = (f32[4,16384]{1,0:T(4,128)}, f32[4,16384]{1,0:T(4,128)}) fusion(f32[1,4,128,128]{3,2,1,0:T(8,128)S(1)} %bitcast.20, f32[1,4,128,128]{3,2,1,0:T(8,128)S(1)} %bitcast.19), kind=kLoop, calls=%fused_computation | loop fusion | bytes 1048576 | tf_op jit(solution)/shard_map/reshape | solution.py:698
  56.8 7.8 %all-to-all-done.2 = bf16[16,16,384]{2,1,0:T(8,128)(2,1)S(1)} async-done(((bf16[16,16,384]{2,1,0:T(8,128)(2,1)}), bf16[16,16,384]{2,1,0:T(8,128)(2,1)S(1)}, u32[]{:S(2)}, u32[]{:S(2)}) %all-to-all-start.2) | async-done | bytes 196640 | tf_op jit(solution)/shard_map/all_to_all | solution.py:676
  64.6 0.0 copy-done.7
  64.6 3.2 %outer.1 = (f32[2,64,64,128]{3,2,1,0:T(8,128)}, f32[64,64]{1,0:T(8,128)}) custom-call(bf16[256,384]{1,0:T(8,128)(2,1)S(1)} %bitcast.21, f32[8,256]{1,0:T(8,128)S(1)} %get-tuple-element.54.spec, bf16[64,128]{1,0:T(8,128)(2,1)S(1)} %copy-done.7, f32[3,64]{1,0:T(4,128)S(1)} %copy-done.1), custom_call_target="tpu_custom_call" | custom-call | flops 1800000000 | bytes 10200000 | tf_op jit(solution)/shard_map/outer/pallas_call | solution.py:677
Async XLA Ops:
  1.9 6.0 %collective-permute-start.1 = (bf16[4,144,128]{2,1,0:T(8,128)(2,1)S(1)}, bf16[4,144,128]{2,1,0:T(8,128)(2,1)S(1)}, u32[]{:S(2)}, u32[]{:S(2)}) collective-permute-start(bf16[4,144,128]{2,1,0:T(8,128)(2,1)S(1)} %get-tuple-element.31), channel_id=1, source_target_pairs={{1,0},{2,1},{3,2},{4,3},{5,4},{6,5},{7,6},{8,7},{9,8},{10,9},{11,1... | collective-permute-start | bytes 442376 | tf_op jit(solution)/shard_map/ppermute | solution.py:574
  3.2 4.7 %collective-permute-start = (bf16[4,144,128]{2,1,0:T(8,128)(2,1)S(1)}, bf16[4,144,128]{2,1,0:T(8,128)(2,1)S(1)}, u32[]{:S(2)}, u32[]{:S(2)}) collective-permute-start(bf16[4,144,128]{2,1,0:T(8,128)(2,1)S(1)} %get-tuple-element.31), channel_id=1, source_target_pairs={{0,1},{1,2},{2,3},{3,4},{4,5},{5,6},{6,7},{7,8},{8,9},{9,10},{10,1... | collective-permute-start | bytes 442376 | tf_op jit(solution)/shard_map/ppermute | solution.py:573
  6.3 15.4 %copy-start = (bf16[64,64]{1,0:T(8,128)(2,1)S(1)}, bf16[64,64]{1,0:T(8,128)(2,1)}, u32[]{:S(2)}) copy-start(bf16[64,64]{1,0:T(8,128)(2,1)} %point_weight.1) | copy-start | bytes 24580
  6.3 15.4 %copy-start.1 = (f32[3,64]{1,0:T(4,128)S(1)}, f32[3,64]{1,0:T(4,128)}, u32[]{:S(2)}) copy-start(f32[3,64]{1,0:T(4,128)} %lift.3) | copy-start | bytes 2308
  6.3 15.4 %copy-start.2 = (f32[64]{0:T(128)S(1)}, f32[64]{0:T(128)}, u32[]{:S(2)}) copy-start(f32[64]{0:T(128)} %param.33) | copy-start | bytes 772
  6.3 15.4 %copy-start.3 = (f32[64]{0:T(128)S(1)}, f32[64]{0:T(128)}, u32[]{:S(2)}) copy-start(f32[64]{0:T(128)} %param.34) | copy-start | bytes 772
  7.9 20.1 %copy-start.6 = (bf16[2,128,32]{2,1,0:T(8,128)(2,1)S(1)}, bf16[2,128,32]{2,1,0:T(8,128)(2,1)}, u32[]{:S(2)}) copy-start(bf16[2,128,32]{2,1,0:T(8,128)(2,1)} %constant.28.clone.bx) | copy-start | bytes 49156
  7.9 20.1 %copy-start.8 = (f32[16,256]{1,0:T(8,128)S(1)}, f32[16,256]{1,0:T(8,128)}, u32[]{:S(2)}) copy-start(f32[16,256]{1,0:T(8,128)} %constant.27.clone.ax) | copy-start | bytes 49156
  10.9 28.8 %copy-start.4 = (bf16[256,2048]{1,0:T(8,128)(2,1)S(1)}, bf16[256,2048]{1,0:T(8,128)(2,1)}, u32[]{:S(2)}) copy-start(bf16[256,2048]{1,0:T(8,128)(2,1)} %constant.25.clone.ez) | copy-start | bytes 3145732
  10.9 28.8 %copy-start.5 = (bf16[4,144,256]{2,1,0:T(8,128)(2,1)S(1)}, bf16[4,144,256]{2,1,0:T(8,128)(2,1)}, u32[]{:S(2)}) copy-start(bf16[4,144,256]{2,1,0:T(8,128)(2,1)} %constant.26.clone.fwd) | copy-start | bytes 884740
  10.9 17.1 %all-to-all-start = ((f32[16,1,128]{2,1,0:T(1,128)}), f32[16,1,128]{2,1,0:T(1,128)S(1)}, u32[]{:S(2)}, u32[]{:S(2)}) async-start(f32[16,1,128]{2,1,0:T(1,128)} %bitcast.2), calls=%async_computation | async-start | bytes 16384 | tf_op jit(solution)/shard_map/all_to_all | solution.py:635
  39.8 24.8 %copy-start.7 = (bf16[64,128]{1,0:T(8,128)(2,1)S(1)}, bf16[64,128]{1,0:T(8,128)(2,1)}, u32[]{:S(2)}) copy-start(bf16[64,128]{1,0:T(8,128)(2,1)} %constant.29.clone.gx) | copy-start | bytes 49156
  52.1 12.5 %all-to-all-start.2 = ((bf16[16,16,384]{2,1,0:T(8,128)(2,1)}), bf16[16,16,384]{2,1,0:T(8,128)(2,1)S(1)}, u32[]{:S(2)}, u32[]{:S(2)}) async-start(bf16[16,16,384]{2,1,0:T(8,128)(2,1)} %bitcast.9), calls=%async_computation.2 | async-start | bytes 393216 | tf_op jit(solution)/shard_map/all_to_all | solution.py:676

commit v5 on v4

--- a/solution.py
+++ b/solution.py
@@ -148,8 +148,8 @@
 
 
 def prepare_kernel(
-    cot_hbm, lift, weight_hbm, lift_rows, point_weight, bias, readout,
-    cot_z, mapped, terms, weigh, flat, cot, weight, sems,
+    cot_hbm, lift, weight_hbm, lift_rows, point_weight, bias, readout, conc_z,
+    cot_z, mapped, terms, weigh, conc_out, flat, cot, weight, sems,
 ):
     cot_copy = pltpu.make_async_copy(cot_hbm, cot, sems.at[0])
     halves = [pltpu.make_async_copy(weight_hbm.at[p], weight.at[p], sems.at[1 + p]) for p in range(2)]
@@ -162,6 +162,10 @@
         flat[:, k, :] = cot[:, k * 128 : (k + 1) * 128]
     for x in range(local_x):
         cot_z[:, x, :] = flat[x].T
+    for x in range(local_x):
+        flat[x] = conc_z[:, x, :].T
+    for k in range(half):
+        conc_out[:, k * 128 : (k + 1) * 128] = flat[:, k, :]
     channels = weight.shape[1]
     rows = local_x * channels
     unit, _ = tanh_units()
@@ -239,8 +243,8 @@
 
 
 def transport_kernel(
-    devices, up, down, own, own_fields, inlet, perm, back, wave_yt, place_c, place_w,
-    conc_out, cover_out, conc_z, cover_z, send, buf,
+    devices, across, within, own, own_fields, inlet, perm, back, wave_yt, place_c, place_w,
+    cover_out, conc_z, cover_z, send, buf,
 ):
     local_x = own.shape[0]
     half = own.shape[2]
@@ -248,10 +252,13 @@
     rows = 3 * local_x
     sides = [r for r in range(rows) if r // local_x != 1]
     walls = []
+    even = lax.axis_index("slab") % 2 == 0
     for r in sides:
-        ref = up if r < local_x else down
-        buf[0, r] = (ref[r % local_x, :half, :].astype(F32) + CENTRE).T
-        walls.append(ref[r % local_x, half:, :].astype(F32)[:8])
+        x = r % local_x
+        near, far = within[x].astype(F32), across[x].astype(F32)
+        here = jnp.where(even, far, near) if r < local_x else jnp.where(even, near, far)
+        buf[0, r] = (here[:half] + CENTRE).T
+        walls.append(here[half : half + 8])
     for x in range(local_x):
         buf[0, local_x + x] = own[x]
     spread = dot(jnp.concatenate(walls, axis=0), perm[...], HI)
@@ -309,7 +316,6 @@
     )
     cover_out[...] = dot(covers, back[...], HI)
     for i in range(local_x):
-        conc_out[i] = planes[i].T
         conc_z[:, i, :] = planes[i]
 
 
@@ -360,9 +366,16 @@
     return -(-3 // (2 * own_j))
 
 
+def extra_rows(conc_z, cover_z, z):
+    depth = conc_z.shape[0] // 2
+    conc = jnp.concatenate([conc_z[z], conc_z[depth + z]], axis=1) - CENTRE
+    wall = jnp.where(z == 0, cover_z[...], 0.0)
+    return jnp.concatenate([high(conc), conc - high(conc), high(conc), wall], axis=0).astype(BF16)
+
+
 def layer_kernel(
-    own_j, inv, conc_z, cot_z, cover_z, terms, weigh, readout, ez, fwd,
-    pred_out, grad_out, lhs, ext_all, waves, pred, point, pre_a, pre_b, hidden_a, hidden_b, grads_a, grads_b,
+    own_j, inv, conc_z, cot_z, cover_z, terms, readout, ez, fwd,
+    grad_out, lhs, waves, ext_all, point, pre_a, pre_b, grads_a, grads_b,
 ):
     channels = readout.shape[1]
     local_x = cover_z.shape[0]
@@ -384,25 +397,17 @@
     slot = lax.broadcasted_iota(jnp.int32, (16, rows), 0)
     point[...] = jnp.zeros(point.shape, F32)
     grads_b[...] = jnp.zeros(grads_b.shape, BF16)
-    hidden_b[...] = jnp.zeros(hidden_b.shape, BF16)
     by = fwd[0, :pairs, :]
-    pres, hiddens, grads = (pre_a, pre_b), (hidden_a, hidden_b), (grads_a, grads_b)
+    pres, grads = (pre_a, pre_b), (grads_a, grads_b)
 
     def before(g, i, pre):
         z = g * ZG + i
-        conc = jnp.concatenate([conc_z[z], conc_z[depth + z]], axis=1) - CENTRE
-        conc_high = high(conc)
-        wall = jnp.where(z == 0, cover_z[...], 0.0)
-        ext = jnp.concatenate([conc_high, conc - conc_high, conc_high, wall], axis=0).astype(BF16)
+        ext = extra_rows(conc_z, cover_z, z)
         ext_all[z] = ext
         both = jnp.concatenate([lhs[g], terms[...]], axis=1)
         pre[...] = dot(both, jnp.concatenate([fwd[i], ext], axis=0))
 
-    def after(z, hidden, grad):
-        line = dot(weigh[...], hidden[...])
-        line = line[:local_x] + line[8 : 8 + local_x]
-        pred[z] = line[:, :half]
-        pred[depth + z] = line[:, half:]
+    def after(z, grad):
         sums = dot_nt(jnp.concatenate([by, ext_all[z]], axis=0), grad[...])
         waves[pl.ds(pl.multiple_of(z * pairs, pairs), pairs), :] = sums[:pairs].astype(BF16)
         point[:16] += sums[pairs:]
@@ -418,7 +423,7 @@
                 before(g, i + 1, pres[other])
             else:
                 before(jnp.minimum(g + 1, groups - 1), 0, pres[other])
-            after(jnp.maximum(z - 1, 0), hiddens[other], grads[other])
+            after(jnp.maximum(z - 1, 0), grads[other])
             cot = jnp.concatenate([cot_z[z], cot_z[depth + z]], axis=1)
             for x in range(local_x):
                 here = slice(x * channels, (x + 1) * channels)
@@ -426,16 +431,13 @@
                 u = y * (y * y + kappa)
                 t = jnp.tanh(u)
                 s = 1.0 + t
-                hiddens[this][here, :] = (y * s).astype(BF16)
                 slope = u - (2.0 / 3.0 * kappa) * y
                 grad = s * (1.0 / 3.0 + slope * (1.0 - t)) * cot[x : x + 1]
                 grads[this][here, :] = grad.astype(BF16)
         return carry
 
     lax.fori_loop(0, groups, group, 0)
-    after(depth - 1, hidden_b, grads_b)
-    for x in range(local_x):
-        pred_out[x] = pred[:, x, :].T
+    after(depth - 1, grads_b)
     total = dot(ez[...], waves[...])
     grad_row = 1.5 * wide_readout
     grad_out[:, :rows] = (total * (iscale * grad_row)).astype(BF16)
@@ -453,6 +455,53 @@
         row = lax.broadcasted_iota(jnp.int32, (out_rows, 16), 0) % (2 * own_j) + b * 2 * own_j
         pick = (row == lax.broadcasted_iota(jnp.int32, (out_rows, 16), 1)).astype(BF16)
         grad_out[:, rows + b * 128 : rows + (b + 1) * 128] = dot(pick, both).astype(BF16)
+
+
+def predict_kernel(
+    lhs, conc_z, cover_z, terms, weigh, fwd, pred_out, pred, flat, pre_a, pre_b, hidden_a, hidden_b
+):
+    local_x = pred_out.shape[0]
+    half = conc_z.shape[2]
+    groups = lhs.shape[0]
+    depth = groups * ZG
+    _, kappa = tanh_units()
+    pres, hiddens = (pre_a, pre_b), (hidden_a, hidden_b)
+    hidden_b[...] = jnp.zeros(hidden_b.shape, BF16)
+
+    def before(g, i, pre):
+        both = jnp.concatenate([lhs[g], terms[...]], axis=1)
+        pre[...] = dot(both, jnp.concatenate([fwd[i], extra_rows(conc_z, cover_z, g * ZG + i)], axis=0))
+
+    def after(z, hidden):
+        line = dot(weigh[...], hidden[...])
+        line = line[:local_x] + line[8 : 8 + local_x]
+        pred[z] = line[:, :half]
+        pred[depth + z] = line[:, half:]
+
+    before(0, 0, pre_a)
+
+    def group(g, carry):
+        for i in range(ZG):
+            z = g * ZG + i
+            this, other = i % 2, (i + 1) % 2
+            if i < ZG - 1:
+                before(g, i + 1, pres[other])
+            else:
+                before(jnp.minimum(g + 1, groups - 1), 0, pres[other])
+            after(jnp.maximum(z - 1, 0), hiddens[other])
+            for k in range(local_x):
+                here = slice(k * pre_a.shape[0] // local_x, (k + 1) * pre_a.shape[0] // local_x)
+                y = pres[this][here, :]
+                t = jnp.tanh(y * (y * y + kappa))
+                hiddens[this][here, :] = (y * (1.0 + t)).astype(BF16)
+        return carry
+
+    lax.fori_loop(0, groups, group, 0)
+    after(depth - 1, hidden_b)
+    for x in range(local_x):
+        flat[x] = pred[:, x, :].T
+    for k in range(half):
+        pred_out[:, k * 128 : (k + 1) * 128] = flat[:, k, :]
 
 
 def outer_kernel(own_j, got, spec, gx, lift, modes_hbm, point_out, result, factor, stage, sems):
@@ -570,31 +619,9 @@
         compiler_params=params(4),
         cost_estimate=cost(0.3),
     )(*map(in_hbm, (conc_init, cover_init, rate_on, rate_off, site_mask)))
-    up = lax.ppermute(pack, "slab", [(i, i + 1) for i in range(devices - 1)])
-    down = lax.ppermute(pack, "slab", [(i + 1, i) for i in range(devices - 1)])
-    cot_z, mapped, terms, weigh = pl.pallas_call(
-        prepare_kernel,
-        name="prepare",
-        out_shape=(
-            sds((2 * depth, local_x, half), F32),
-            sds((3, 2, channels, modes), F32),
-            sds((local_x * channels, 32), BF16),
-            sds((16, local_x * channels), BF16),
-        ),
-        in_specs=hbm(1) + [smem] + hbm(1) + vmem(4),
-        out_specs=vmem(4),
-        scratch_shapes=[
-            pltpu.VMEM((local_x, half, 2 * depth), F32),
-            pltpu.VMEM(cotangent.shape, F32),
-            pltpu.VMEM((2, channels, channels, modes), BF16),
-            pltpu.SemaphoreType.DMA((3,)),
-        ],
-        compiler_params=params(8),
-        cost_estimate=cost(2.0),
-    )(
-        in_hbm(cotangent), lift, in_hbm(mode_weight.transpose(1, 2, 3, 0)),
-        lift, point_weight, point_bias.reshape(1, -1), readout.reshape(1, -1),
-    )
+    seams = [(i, i + 1) for i in range(1, devices - 1, 2)]
+    across = lax.ppermute(pack, "slab", seams + [(j, i) for i, j in seams])
+    within = lax.ppermute(pack, "slab", [(i, i ^ 1) for i in range(devices)])
     constants = [tab[k] for k in ("perm", "back", "wave_yt", "place_c", "place_w")]
     early = pl.pallas_call(
         early_kernel,
@@ -613,22 +640,45 @@
         compiler_params=params(8),
         cost_estimate=cost(1.5),
     )(conc, walls, *map(in_hbm, (inlet_index.reshape(1, span), inlet_profiles, *constants)))
-    conc_out, cover_out, conc_z, cover_z, send = pl.pallas_call(
+    cover_out, conc_z, cover_z, send = pl.pallas_call(
         functools.partial(transport_kernel, devices),
         name="transport",
         out_shape=(
-            sds((local_x, half, 2 * depth), F32),
             sds((local_x, span), F32),
             sds((2 * depth, local_x, half), F32),
             sds((local_x, span), F32),
             sds((KY, 4 * local_x * KZ), F32),
         ),
         in_specs=vmem(10),
-        out_specs=vmem(5),
+        out_specs=vmem(4),
         scratch_shapes=[pltpu.VMEM((2, 3 * local_x, 2 * depth, half), F32)],
         compiler_params=params(8),
         cost_estimate=cost(3.0),
-    )(up, down, *early)
+    )(across, within, *early)
+    cot_z, mapped, terms, weigh, conc_out = pl.pallas_call(
+        prepare_kernel,
+        name="prepare",
+        out_shape=(
+            sds((2 * depth, local_x, half), F32),
+            sds((3, 2, channels, modes), F32),
+            sds((local_x * channels, 32), BF16),
+            sds((16, local_x * channels), BF16),
+            sds(conc_init.shape, F32),
+        ),
+        in_specs=hbm(1) + [smem] + hbm(1) + vmem(5),
+        out_specs=vmem(5),
+        scratch_shapes=[
+            pltpu.VMEM((local_x, half, 2 * depth), F32),
+            pltpu.VMEM(cotangent.shape, F32),
+            pltpu.VMEM((2, channels, channels, modes), BF16),
+            pltpu.SemaphoreType.DMA((3,)),
+        ],
+        compiler_params=params(8),
+        cost_estimate=cost(2.0),
+    )(
+        in_hbm(cotangent), lift, in_hbm(mode_weight.transpose(1, 2, 3, 0)),
+        lift, point_weight, point_bias.reshape(1, -1), readout.reshape(1, -1), conc_z,
+    )
     if own_j != KZ:
         send = send.reshape(KY, 4 * local_x, KZ // own_j, own_j).transpose(0, 2, 1, 3)
         send = send.reshape(devices, 4 * local_x * own_j)
@@ -650,30 +700,38 @@
     inv = lax.all_to_all(inv, "slab", 0, 0, tiled=True)
     rows = local_x * channels
     wide = ZG * 2 * KY
-    pred, grad = pl.pallas_call(
+    grad, lhs = pl.pallas_call(
         functools.partial(layer_kernel, own_j),
         name="layer",
         out_shape=(
-            sds((local_x, half, 2 * depth), F32),
             sds((2 * KY * KZ, rows + 128 * tail_blocks(own_j)), BF16),
+            sds((depth // ZG, rows, wide), BF16),
         ),
-        in_specs=vmem(9),
+        in_specs=vmem(8),
         out_specs=vmem(2),
         scratch_shapes=[
-            pltpu.VMEM((depth // ZG, rows, wide), BF16),
+            pltpu.VMEM((depth * 2 * KY, rows), BF16),
             pltpu.VMEM((depth, 16, span), BF16),
-            pltpu.VMEM((depth * 2 * KY, rows), BF16),
-            pltpu.VMEM((2 * depth, local_x, half), F32),
             pltpu.VMEM((24, rows), F32),
         ]
         + [pltpu.VMEM((rows, span), F32)] * 2
-        + [pltpu.VMEM((rows, span), BF16)] * 4,
+        + [pltpu.VMEM((rows, span), BF16)] * 2,
         compiler_params=params(16),
-        cost_estimate=cost(12.4),
-    )(
-        inv, conc_z, cot_z, cover_z, terms, weigh, readout.reshape(1, -1), tab["ez"], tab["fwd"],
-    )
+        cost_estimate=cost(11.0),
+    )(inv, conc_z, cot_z, cover_z, terms, readout.reshape(1, -1), tab["ez"], tab["fwd"])
     grad = lax.all_to_all(grad, "slab", 0, 0, tiled=True)
+    pred = pl.pallas_call(
+        predict_kernel,
+        name="predict",
+        out_shape=sds((local_x, plane), F32),
+        in_specs=vmem(6),
+        out_specs=pl.BlockSpec(memory_space=pltpu.VMEM),
+        scratch_shapes=[pltpu.VMEM((2 * depth, local_x, half), F32), pltpu.VMEM((local_x, half, 2 * depth), F32)]
+        + [pltpu.VMEM((rows, span), F32)] * 2
+        + [pltpu.VMEM((rows, span), BF16)] * 2,
+        compiler_params=params(8),
+        cost_estimate=cost(5.5),
+    )(lhs, conc_z, cover_z, terms, weigh, tab["fwd"])
     grad_modes, grad_point = pl.pallas_call(
         functools.partial(outer_kernel, own_j),
         name="outer",
@@ -693,9 +751,9 @@
         cost_estimate=cost(3.0),
     )(grad, spec, tab["gx"], lift)
     return (
-        conc_out.reshape(local_x, plane),
+        conc_out,
         cover_out,
-        pred.reshape(local_x, plane),
+        pred,
         grad_modes.transpose(3, 0, 1, 2),
         grad_point,
     )

time: 68.2 us -> 65.3 us (0.957)
  waiting for transfers between devices: 10.9 us -> 2.94 us
  Pallas kernels: 25.7 us -> 33 us
  starting transfers between devices: 18.6 us -> 16.7 us
  local copies, waits for them, and re-layouts: 1.18 us -> 0.05 us
  blocking collectives: 10.7 us -> 11.5 us
    pallas_call x0 -> x1, Pallas kernels: none -> 8.2 us  [body(): pl.pallas_call(predict_kernel, name='predict', out_shape=sds((local_x, pl...]
    all_to_all x1, waiting for transfers between devices: 7.8 us -> 0.71 us  [body(): grad = lax.all_to_all(grad, 'slab', 0, 0, tiled=True)]
    ppermute x2, starting transfers between devices: 4.33 us -> 1.22 us  [the longest x1 0.66 us: body(): across = lax.ppermute(pack, 'slab', seams + [(j, i) for i, j in seams])]
    pallas_call x1, Pallas kernels: 12.3 us -> 10.6 us  [body(): pl.pallas_call(functools.partial(layer_kernel, own_j), name='layer', out_...]
    all_to_all x1, starting transfers between devices: 10.7 us -> 11.9 us  [body(): got = lax.all_to_all(send, 'slab', 0, 0, tiled=True)]
    reshape x1 -> x0, local copies, waits for them, and re-layouts: 1.13 us -> none  [body(): pred.reshape(local_x, plane)]
    pallas_call x1, Pallas kernels: 3.24 us -> 4.08 us  [body(): pl.pallas_call(prepare_kernel, name='prepare', out_shape=(sds((2 * depth,...]
    all_to_all x1, waiting for transfers between devices: 3.07 us -> 2.23 us  [body(): got = lax.all_to_all(send, 'slab', 0, 0, tiled=True)]
  transfers between devices with their start and end apart: 4 -> 4, of which waited for: 2 -> 2; matrix products, arithmetic and copies ran while one was open for 2% -> 0% of each run, Pallas kernels for 7% -> 21%
where the time goes in v5:
time: 65.3 us; the launch traced here: 65 us
  Pallas kernels  33 us (51%)
  starting transfers between devices  16.7 us (26%)
  blocking collectives  11.5 us (18%)
  waiting for transfers between devices  2.94 us (5%)
  between operations  0.8 us (1%)
    all_to_all x1, starting transfers between devices, body(): got = lax.all_to_all(send, 'slab', 0, 0, tiled=True)  11.9 us
    all_to_all x1, blocking collectives, body(): inv = lax.all_to_all(inv, 'slab', 0, 0, tiled=True)  11.5 us
    pallas_call x1, Pallas kernels, body(): pl.pallas_call(functools.partial(layer_kernel, own_j), name='layer', out_...  10.6 us
    pallas_call x1, Pallas kernels, body(): pl.pallas_call(predict_kernel, name='predict', out_shape=sds((local_x, pl...  8.2 us
    pallas_call x1, Pallas kernels, body(): pl.pallas_call(prepare_kernel, name='prepare', out_shape=(sds((2 * depth,...  4.08 us
    all_to_all x1, starting transfers between devices, body(): grad = lax.all_to_all(grad, 'slab', 0, 0, tiled=True)  3.52 us
    pallas_call x1, Pallas kernels, body(): pl.pallas_call(functools.partial(outer_kernel, own_j), name='outer', out_...  3.23 us
    pallas_call x1, Pallas kernels, body(): pl.pallas_call(functools.partial(transport_kernel, devices), name='transp...  2.97 us
  transfers between devices with their start and end apart: 4, of which 2 were waited for; matrix products, arithmetic and copies ran while one was open for 0% of the time, Pallas kernels for 21%

profile of v5, /device:TPU:0, one launch (start us, length us, event | category | flops | bytes accessed | tf_op | source)
XLA Modules:
  0.0 65.0 jit_solution(7601091361091482752)
XLA Ops:
  0.6 1.3 %pack.1 = (bf16[4,144,128]{2,1,0:T(8,128)(2,1)S(1)}, f32[4,128,128]{2,1,0:T(8,128)S(1)}, f32[4,8,128]{2,1,0:T(8,128)S(1)}) custom-call(f32[4,16384]{1,0:T(4,128)} %conc_hbm.1, f32[4,256]{1,0:T(4,128)} %cover_hbm.1, f32[4,256]{1,0:T(4,128)} %on_hbm.1, f32[4,256]{1,0:T(4,128)} %off_hbm.1, s32[4,256]{1,0:T(4,128)} %mask_hbm.1), custom_call_target="tpu_custom_call" | custom-call | flops 180000000 | bytes 1020000 | tf_op jit(solution)/shard_map/pack/pallas_call | solution.py:606
  1.9 0.6 collective-permute-start.1
  2.5 0.7 %collective-permute-start = (bf16[4,144,128]{2,1,0:T(8,128)(2,1)S(1)}, bf16[4,144,128]{2,1,0:T(8,128)(2,1)S(1)}, u32[]{:S(2)}, u32[]{:S(2)}) collective-permute-start(bf16[4,144,128]{2,1,0:T(8,128)(2,1)S(1)} %get-tuple-element.31), channel_id=1, source_target_pairs={{1,2},{3,4},{5,6},{7,8},{9,10},{11,12},{13,14},{2,1},{4,3},{6,5},{... | collective-permute-start | bytes 442376 | tf_op jit(solution)/shard_map/ppermute | solution.py:623
  3.2 0.0 copy-start
  3.2 0.0 copy-start.1
  3.2 0.0 copy-start.2
  3.2 0.0 copy-start.3
  3.2 1.6 %early.1 = (f32[4,128,128]{2,1,0:T(8,128)S(1)}, f32[16,256]{1,0:T(8,128)S(1)}, f32[128,128]{1,0:T(8,128)S(1)}, f32[128,512]{1,0:T(8,128)S(1)}, f32[256,256]{1,0:...) custom-call(f32[4,128,128]{2,1,0:T(8,128)S(1)} %get-tuple-element.32.own, ...), custom_call_target="tpu_custom_call" | custom-call | flops 900000000 | bytes 5100000 | tf_op jit(solution)/shard_map/early/pallas_call | solution.py:626
  4.8 0.0 collective-permute-done.1.within
  4.8 0.0 collective-permute-done.across
  4.8 0.0 copy-start.6
  4.8 0.0 copy-start.8
  4.8 3.0 %transport.1 = (f32[4,256]{1,0:T(4,128)}, f32[128,4,128]{2,1,0:T(4,128)S(1)}, f32[4,256]{1,0:T(4,128)S(1)}, f32[16,128]{1,0:T(8,128)}) custom-call(bf16[4,144,128]{2,1,0:T(8,128)(2,1)S(1)} %collective-permute-done.across, bf16[4,144,128]{2,1,0:T(8,128)(2,1)S(1)} %collective-permute-done.1.within, f32[4,128,128]{2,1,0:T(8,128)S(1)} %get-tuple-element.34.own, ...), custom_call_target="tpu_custom_call" | custom-call | flops 1800000000 | bytes 10200000 | tf_op jit(solution)/shard_map/transport/pallas_call | solution.py:643
  7.8 0.0 copy-start.4
  7.8 0.0 copy-start.5
  7.8 11.9 %all-to-all-start = ((f32[16,1,128]{2,1,0:T(1,128)}), f32[16,1,128]{2,1,0:T(1,128)S(1)}, u32[]{:S(2)}, u32[]{:S(2)}) async-start(f32[16,1,128]{2,1,0:T(1,128)} %bitcast.5), calls=%async_computation | async-start | bytes 16384 | tf_op jit(solution)/shard_map/all_to_all | solution.py:685
  19.7 0.0 copy-done
  19.7 0.0 copy-done.1
  19.7 0.0 copy-done.2
  19.8 0.0 copy-done.3
  19.8 4.1 %prepare.1 = (f32[128,4,128]{2,1,0:T(4,128)S(1)}, f32[3,2,64,128]{3,2,1,0:T(8,128)S(1)}, bf16[256,32]{1,0:T(8,128)(2,1)S(1)}, bf16[16,256]{1,0:T(8,128)(2,1)S(1)}, f32[4,16384]{1,0:T(4,128)}) custom-call(f32[4,16384]{1,0:T(4,128)} %cot_hbm.1, f32[3,64]{1,0:T(4,128)S(1)} %copy-done.1, bf16[2,64,64,128]{3,2,1,0:T(8,128)(2,1)} %bitcast.20, ...), custom_call_target="tpu_custom_call" | custom-call | flops 1200000000 | bytes 6800000 | tf_op jit(solution)/shard_map/prepare/pallas_call | solution.py:658
  23.9 2.2 %all-to-all-done = f32[16,1,128]{2,1,0:T(1,128)S(1)} async-done(((f32[16,1,128]{2,1,0:T(1,128)}), f32[16,1,128]{2,1,0:T(1,128)S(1)}, u32[]{:S(2)}, u32[]{:S(2)}) %all-to-all-start) | async-done | bytes 8224 | tf_op jit(solution)/shard_map/all_to_all | solution.py:685
  26.1 0.0 copy-done.6
  26.1 0.0 copy-done.8
  26.1 1.1 %mixing.1 = (bf16[256,256]{1,0:T(8,128)(2,1)S(1)}, f32[8,256]{1,0:T(8,128)S(1)}) custom-call(f32[16,128]{1,0:T(8,128)S(1)} %bitcast.16, f32[16,256]{1,0:T(8,128)S(1)} %copy-done.8, bf16[2,128,32]{2,1,0:T(8,128)(2,1)S(1)} %copy-done.6, f32[3,2,64,128]{3,2,1,0:T(8,128)S(1)} %get-tuple-element.46.mapped), custom_call_target="tpu_custom_call" | custom-call | flops 960000000 | bytes 5440000 | tf_op jit(solution)/shard_map/mixing/pallas_call | solution.py:687
  27.2 11.5 %all_to_all.33 = bf16[16,16,256]{2,1,0:T(8,128)(2,1)S(1)} all-to-all(bf16[16,16,256]{2,1,0:T(8,128)(2,1)S(1)} %bitcast.14), channel_id=1, replica_groups=mesh['groups'=2,'slab'=16] {'slab'}, dimensions={0} | all-to-all | bytes 262144 | tf_op jit(solution)/shard_map/all_to_all | solution.py:700
  38.7 0.0 copy-done.4
  38.7 0.0 copy-done.5
  38.7 10.6 %layer.1 = (bf16[256,384]{1,0:T(8,128)(2,1)}, bf16[16,256,128]{2,1,0:T(8,128)(2,1)S(1)}) custom-call(bf16[256,256]{1,0:T(8,128)(2,1)S(1)} %bitcast.15, f32[128,4,128]{2,1,0:T(4,128)S(1)} %get-tuple-element.42.conc_z, f32[128,4,128]{2,1,0:T(4,128)S(1)} %get-tuple-element.48.cot_z, f32[4,256]{1,0:T(4,128)S(1)} %get-tuple-element.49.cover_z, ...), custom_call_target="tpu_custom_call" | custom-call | flops 6600000000 | bytes 37400000 | tf_op jit(solution)/shard_map/layer/pallas_call | solution.py:703
  49.3 3.5 %all-to-all-start.2 = ((bf16[16,16,384]{2,1,0:T(8,128)(2,1)}), bf16[16,16,384]{2,1,0:T(8,128)(2,1)S(1)}, u32[]{:S(2)}, u32[]{:S(2)}) async-start(bf16[16,16,384]{2,1,0:T(8,128)(2,1)} %bitcast.9), calls=%async_computation.2 | async-start | bytes 393216 | tf_op jit(solution)/shard_map/all_to_all | solution.py:722
  52.8 0.0 copy-start.7
  52.8 8.2 %predict.1 = f32[4,16384]{1,0:T(4,128)} custom-call(bf16[16,256,128]{2,1,0:T(8,128)(2,1)S(1)} %get-tuple-element.51.lhs, f32[128,4,128]{2,1,0:T(4,128)S(1)} %get-tuple-element.42.conc_z, f32[4,256]{1,0:T(4,128)S(1)} %get-tuple-element.49.cover_z, bf16[256,32]{1,0:T(8,128)(2,1)S(1)} %get-tuple-element.50.terms, bf16[16,256]{1,0:T(8,128)(2,1)S(1)} %get-tuple-element.52.weigh, ...), custom_call_target="tpu_custom_call" | custom-call | flops 3300000000 | bytes 18700000 | tf_op jit(solution)/shard_map/predict/pallas_call | solution.py:723
  61.0 0.7 %all-to-all-done.2 = bf16[16,16,384]{2,1,0:T(8,128)(2,1)S(1)} async-done(((bf16[16,16,384]{2,1,0:T(8,128)(2,1)}), bf16[16,16,384]{2,1,0:T(8,128)(2,1)S(1)}, u32[]{:S(2)}, u32[]{:S(2)}) %all-to-all-start.2) | async-done | bytes 196640 | tf_op jit(solution)/shard_map/all_to_all | solution.py:722
  61.7 0.0 copy-done.7
  61.7 3.2 %outer.1 = (f32[2,64,64,128]{3,2,1,0:T(8,128)}, f32[64,64]{1,0:T(8,128)}) custom-call(bf16[256,384]{1,0:T(8,128)(2,1)S(1)} %bitcast.13, f32[8,256]{1,0:T(8,128)S(1)} %get-tuple-element.54.spec, bf16[64,128]{1,0:T(8,128)(2,1)S(1)} %copy-done.7, f32[3,64]{1,0:T(4,128)S(1)} %copy-done.1), custom_call_target="tpu_custom_call" | custom-call | flops 1800000000 | bytes 10200000 | tf_op jit(solution)/shard_map/outer/pallas_call | solution.py:735
Async XLA Ops:
  1.9 2.8 %collective-permute-start.1 = (bf16[4,144,128]{2,1,0:T(8,128)(2,1)S(1)}, bf16[4,144,128]{2,1,0:T(8,128)(2,1)S(1)}, u32[]{:S(2)}, u32[]{:S(2)}) collective-permute-start(bf16[4,144,128]{2,1,0:T(8,128)(2,1)S(1)} %get-tuple-element.31), channel_id=1, source_target_pairs={{0,1},{1,0},{2,3},{3,2},{4,5},{5,4},{6,7},{7,6},{8,9},{9,8},{10,11... | collective-permute-start | bytes 442376 | tf_op jit(solution)/shard_map/ppermute | solution.py:624
  2.5 2.3 %collective-permute-start = (bf16[4,144,128]{2,1,0:T(8,128)(2,1)S(1)}, bf16[4,144,128]{2,1,0:T(8,128)(2,1)S(1)}, u32[]{:S(2)}, u32[]{:S(2)}) collective-permute-start(bf16[4,144,128]{2,1,0:T(8,128)(2,1)S(1)} %get-tuple-element.31), channel_id=1, source_target_pairs={{1,2},{3,4},{5,6},{7,8},{9,10},{11,12},{13,14},{2,1},{4,3},{6,5},{... | collective-permute-start | bytes 442376 | tf_op jit(solution)/shard_map/ppermute | solution.py:623
  3.2 16.6 %copy-start = (bf16[64,64]{1,0:T(8,128)(2,1)S(1)}, bf16[64,64]{1,0:T(8,128)(2,1)}, u32[]{:S(2)}) copy-start(bf16[64,64]{1,0:T(8,128)(2,1)} %point_weight.1) | copy-start | bytes 24580
  3.2 16.6 %copy-start.1 = (f32[3,64]{1,0:T(4,128)S(1)}, f32[3,64]{1,0:T(4,128)}, u32[]{:S(2)}) copy-start(f32[3,64]{1,0:T(4,128)} %lift.3) | copy-start | bytes 2308
  3.2 16.6 %copy-start.2 = (f32[64]{0:T(128)S(1)}, f32[64]{0:T(128)}, u32[]{:S(2)}) copy-start(f32[64]{0:T(128)} %param.33) | copy-start | bytes 772
  3.2 16.6 %copy-start.3 = (f32[64]{0:T(128)S(1)}, f32[64]{0:T(128)}, u32[]{:S(2)}) copy-start(f32[64]{0:T(128)} %param.34) | copy-start | bytes 772
  4.8 21.3 %copy-start.6 = (bf16[2,128,32]{2,1,0:T(8,128)(2,1)S(1)}, bf16[2,128,32]{2,1,0:T(8,128)(2,1)}, u32[]{:S(2)}) copy-start(bf16[2,128,32]{2,1,0:T(8,128)(2,1)} %constant.28.clone.bx) | copy-start | bytes 49156
  4.8 21.3 %copy-start.8 = (f32[16,256]{1,0:T(8,128)S(1)}, f32[16,256]{1,0:T(8,128)}, u32[]{:S(2)}) copy-start(f32[16,256]{1,0:T(8,128)} %constant.27.clone.ax) | copy-start | bytes 49156
  7.8 30.9 %copy-start.4 = (bf16[256,2048]{1,0:T(8,128)(2,1)S(1)}, bf16[256,2048]{1,0:T(8,128)(2,1)}, u32[]{:S(2)}) copy-start(bf16[256,2048]{1,0:T(8,128)(2,1)} %constant.25.clone.ez) | copy-start | bytes 3145732
  7.8 30.9 %copy-start.5 = (bf16[4,144,256]{2,1,0:T(8,128)(2,1)S(1)}, bf16[4,144,256]{2,1,0:T(8,128)(2,1)}, u32[]{:S(2)}) copy-start(bf16[4,144,256]{2,1,0:T(8,128)(2,1)} %constant.26.clone.fwd) | copy-start | bytes 884740
  7.8 18.3 %all-to-all-start = ((f32[16,1,128]{2,1,0:T(1,128)}), f32[16,1,128]{2,1,0:T(1,128)S(1)}, u32[]{:S(2)}, u32[]{:S(2)}) async-start(f32[16,1,128]{2,1,0:T(1,128)} %bitcast.5), calls=%async_computation | async-start | bytes 16384 | tf_op jit(solution)/shard_map/all_to_all | solution.py:685
  49.3 12.5 %all-to-all-start.2 = ((bf16[16,16,384]{2,1,0:T(8,128)(2,1)}), bf16[16,16,384]{2,1,0:T(8,128)(2,1)S(1)}, u32[]{:S(2)}, u32[]{:S(2)}) async-start(bf16[16,16,384]{2,1,0:T(8,128)(2,1)} %bitcast.9), calls=%async_computation.2 | async-start | bytes 393216 | tf_op jit(solution)/shard_map/all_to_all | solution.py:722
  52.8 8.9 %copy-start.7 = (bf16[64,128]{1,0:T(8,128)(2,1)S(1)}, bf16[64,128]{1,0:T(8,128)(2,1)}, u32[]{:S(2)}) copy-start(bf16[64,128]{1,0:T(8,128)(2,1)} %constant.29.clone.gx) | copy-start | bytes 49156

commit v6 on v5

--- a/solution.py
+++ b/solution.py
@@ -436,7 +436,10 @@
                 grads[this][here, :] = grad.astype(BF16)
         return carry
 
-    lax.fori_loop(0, groups, group, 0)
+    def pair(h, carry):
+        return group(2 * h + 1, group(2 * h, carry))
+
+    lax.fori_loop(0, groups // 2, pair, 0)
     after(depth - 1, grads_b)
     total = dot(ez[...], waves[...])
     grad_row = 1.5 * wide_readout
@@ -496,7 +499,10 @@
                 hiddens[this][here, :] = (y * (1.0 + t)).astype(BF16)
         return carry
 
-    lax.fori_loop(0, groups, group, 0)
+    def pair(h, carry):
+        return group(2 * h + 1, group(2 * h, carry))
+
+    lax.fori_loop(0, groups // 2, pair, 0)
     after(depth - 1, hidden_b)
     for x in range(local_x):
         flat[x] = pred[:, x, :].T

time: 65.3 us -> 64.7 us (level)
  Pallas kernels: 33 us -> 31.9 us
where the time goes in v6:
time: 64.7 us; the launch traced here: 64.3 us
  Pallas kernels  31.9 us (49%)
  starting transfers between devices  16.7 us (26%)
  blocking collectives  11.5 us (18%)
  waiting for transfers between devices  3.46 us (5%)
  between operations  0.8 us (1%)
    all_to_all x1, starting transfers between devices, body(): got = lax.all_to_all(send, 'slab', 0, 0, tiled=True)  11.9 us
    all_to_all x1, blocking collectives, body(): inv = lax.all_to_all(inv, 'slab', 0, 0, tiled=True)  11.5 us
    pallas_call x1, Pallas kernels, body(): pl.pallas_call(functools.partial(layer_kernel, own_j), name='layer', out_...  9.96 us
    pallas_call x1, Pallas kernels, body(): pl.pallas_call(predict_kernel, name='predict', out_shape=sds((local_x, pl...  7.69 us
    pallas_call x1, Pallas kernels, body(): pl.pallas_call(prepare_kernel, name='prepare', out_shape=(sds((2 * depth,...  4.08 us
    all_to_all x1, starting transfers between devices, body(): grad = lax.all_to_all(grad, 'slab', 0, 0, tiled=True)  3.52 us
    pallas_call x1, Pallas kernels, body(): pl.pallas_call(functools.partial(outer_kernel, own_j), name='outer', out_...  3.23 us
    pallas_call x1, Pallas kernels, body(): pl.pallas_call(functools.partial(transport_kernel, devices), name='transp...  2.97 us
  transfers between devices with their start and end apart: 4, of which 2 were waited for; matrix products, arithmetic and copies ran while one was open for 0% of the time, Pallas kernels for 21%

profile of v6, /device:TPU:0, one launch (start us, length us, event | category | flops | bytes accessed | tf_op | source)
XLA Modules:
  0.0 64.3 jit_solution(5679885935490945762)
XLA Ops:
  0.6 1.3 %pack.1 = (bf16[4,144,128]{2,1,0:T(8,128)(2,1)S(1)}, f32[4,128,128]{2,1,0:T(8,128)S(1)}, f32[4,8,128]{2,1,0:T(8,128)S(1)}) custom-call(f32[4,16384]{1,0:T(4,128)} %conc_hbm.1, f32[4,256]{1,0:T(4,128)} %cover_hbm.1, f32[4,256]{1,0:T(4,128)} %on_hbm.1, f32[4,256]{1,0:T(4,128)} %off_hbm.1, s32[4,256]{1,0:T(4,128)} %mask_hbm.1), custom_call_target="tpu_custom_call" | custom-call | flops 180000000 | bytes 1020000 | tf_op jit(solution)/shard_map/pack/pallas_call | solution.py:612
  1.9 0.6 collective-permute-start.1
  2.5 0.7 %collective-permute-start = (bf16[4,144,128]{2,1,0:T(8,128)(2,1)S(1)}, bf16[4,144,128]{2,1,0:T(8,128)(2,1)S(1)}, u32[]{:S(2)}, u32[]{:S(2)}) collective-permute-start(bf16[4,144,128]{2,1,0:T(8,128)(2,1)S(1)} %get-tuple-element.31), channel_id=1, source_target_pairs={{1,2},{3,4},{5,6},{7,8},{9,10},{11,12},{13,14},{2,1},{4,3},{6,5},{... | collective-permute-start | bytes 442376 | tf_op jit(solution)/shard_map/ppermute | solution.py:629
  3.2 0.0 copy-start
  3.2 0.0 copy-start.1
  3.2 0.0 copy-start.2
  3.2 0.0 copy-start.3
  3.2 1.6 %early.1 = (f32[4,128,128]{2,1,0:T(8,128)S(1)}, f32[16,256]{1,0:T(8,128)S(1)}, f32[128,128]{1,0:T(8,128)S(1)}, f32[128,512]{1,0:T(8,128)S(1)}, f32[256,256]{1,0:...) custom-call(f32[4,128,128]{2,1,0:T(8,128)S(1)} %get-tuple-element.32.own, ...), custom_call_target="tpu_custom_call" | custom-call | flops 900000000 | bytes 5100000 | tf_op jit(solution)/shard_map/early/pallas_call | solution.py:632
  4.8 0.0 collective-permute-done.1.within
  4.8 0.0 collective-permute-done.across
  4.8 0.0 copy-start.6
  4.8 0.0 copy-start.8
  4.8 3.0 %transport.1 = (f32[4,256]{1,0:T(4,128)}, f32[128,4,128]{2,1,0:T(4,128)S(1)}, f32[4,256]{1,0:T(4,128)S(1)}, f32[16,128]{1,0:T(8,128)}) custom-call(bf16[4,144,128]{2,1,0:T(8,128)(2,1)S(1)} %collective-permute-done.across, bf16[4,144,128]{2,1,0:T(8,128)(2,1)S(1)} %collective-permute-done.1.within, f32[4,128,128]{2,1,0:T(8,128)S(1)} %get-tuple-element.34.own, ...), custom_call_target="tpu_custom_call" | custom-call | flops 1800000000 | bytes 10200000 | tf_op jit(solution)/shard_map/transport/pallas_call | solution.py:649
  7.8 0.0 copy-start.4
  7.8 0.0 copy-start.5
  7.8 11.9 %all-to-all-start = ((f32[16,1,128]{2,1,0:T(1,128)}), f32[16,1,128]{2,1,0:T(1,128)S(1)}, u32[]{:S(2)}, u32[]{:S(2)}) async-start(f32[16,1,128]{2,1,0:T(1,128)} %bitcast.5), calls=%async_computation | async-start | bytes 16384 | tf_op jit(solution)/shard_map/all_to_all | solution.py:691
  19.7 0.0 copy-done
  19.7 0.0 copy-done.1
  19.7 0.0 copy-done.2
  19.8 0.0 copy-done.3
  19.8 4.1 %prepare.1 = (f32[128,4,128]{2,1,0:T(4,128)S(1)}, f32[3,2,64,128]{3,2,1,0:T(8,128)S(1)}, bf16[256,32]{1,0:T(8,128)(2,1)S(1)}, bf16[16,256]{1,0:T(8,128)(2,1)S(1)}, f32[4,16384]{1,0:T(4,128)}) custom-call(f32[4,16384]{1,0:T(4,128)} %cot_hbm.1, f32[3,64]{1,0:T(4,128)S(1)} %copy-done.1, bf16[2,64,64,128]{3,2,1,0:T(8,128)(2,1)} %bitcast.20, ...), custom_call_target="tpu_custom_call" | custom-call | flops 1200000000 | bytes 6800000 | tf_op jit(solution)/shard_map/prepare/pallas_call | solution.py:664
  23.9 2.2 %all-to-all-done = f32[16,1,128]{2,1,0:T(1,128)S(1)} async-done(((f32[16,1,128]{2,1,0:T(1,128)}), f32[16,1,128]{2,1,0:T(1,128)S(1)}, u32[]{:S(2)}, u32[]{:S(2)}) %all-to-all-start) | async-done | bytes 8224 | tf_op jit(solution)/shard_map/all_to_all | solution.py:691
  26.1 0.0 copy-done.6
  26.1 0.0 copy-done.8
  26.1 1.1 %mixing.1 = (bf16[256,256]{1,0:T(8,128)(2,1)S(1)}, f32[8,256]{1,0:T(8,128)S(1)}) custom-call(f32[16,128]{1,0:T(8,128)S(1)} %bitcast.16, f32[16,256]{1,0:T(8,128)S(1)} %copy-done.8, bf16[2,128,32]{2,1,0:T(8,128)(2,1)S(1)} %copy-done.6, f32[3,2,64,128]{3,2,1,0:T(8,128)S(1)} %get-tuple-element.46.mapped), custom_call_target="tpu_custom_call" | custom-call | flops 960000000 | bytes 5440000 | tf_op jit(solution)/shard_map/mixing/pallas_call | solution.py:693
  27.2 11.5 %all_to_all.33 = bf16[16,16,256]{2,1,0:T(8,128)(2,1)S(1)} all-to-all(bf16[16,16,256]{2,1,0:T(8,128)(2,1)S(1)} %bitcast.14), channel_id=1, replica_groups=mesh['groups'=2,'slab'=16] {'slab'}, dimensions={0} | all-to-all | bytes 262144 | tf_op jit(solution)/shard_map/all_to_all | solution.py:706
  38.7 0.0 copy-done.4
  38.7 0.0 copy-done.5
  38.7 10.0 %layer.1 = (bf16[256,384]{1,0:T(8,128)(2,1)}, bf16[16,256,128]{2,1,0:T(8,128)(2,1)S(1)}) custom-call(bf16[256,256]{1,0:T(8,128)(2,1)S(1)} %bitcast.15, f32[128,4,128]{2,1,0:T(4,128)S(1)} %get-tuple-element.42.conc_z, f32[128,4,128]{2,1,0:T(4,128)S(1)} %get-tuple-element.48.cot_z, f32[4,256]{1,0:T(4,128)S(1)} %get-tuple-element.49.cover_z, ...), custom_call_target="tpu_custom_call" | custom-call | flops 6600000000 | bytes 37400000 | tf_op jit(solution)/shard_map/layer/pallas_call | solution.py:709
  48.6 3.5 %all-to-all-start.2 = ((bf16[16,16,384]{2,1,0:T(8,128)(2,1)}), bf16[16,16,384]{2,1,0:T(8,128)(2,1)S(1)}, u32[]{:S(2)}, u32[]{:S(2)}) async-start(bf16[16,16,384]{2,1,0:T(8,128)(2,1)} %bitcast.9), calls=%async_computation.2 | async-start | bytes 393216 | tf_op jit(solution)/shard_map/all_to_all | solution.py:728
  52.2 0.0 copy-start.7
  52.2 7.7 %predict.1 = f32[4,16384]{1,0:T(4,128)} custom-call(bf16[16,256,128]{2,1,0:T(8,128)(2,1)S(1)} %get-tuple-element.51.lhs, f32[128,4,128]{2,1,0:T(4,128)S(1)} %get-tuple-element.42.conc_z, f32[4,256]{1,0:T(4,128)S(1)} %get-tuple-element.49.cover_z, bf16[256,32]{1,0:T(8,128)(2,1)S(1)} %get-tuple-element.50.terms, bf16[16,256]{1,0:T(8,128)(2,1)S(1)} %get-tuple-element.52.weigh, ...), custom_call_target="tpu_custom_call" | custom-call | flops 3300000000 | bytes 18700000 | tf_op jit(solution)/shard_map/predict/pallas_call | solution.py:729
  59.9 1.2 %all-to-all-done.2 = bf16[16,16,384]{2,1,0:T(8,128)(2,1)S(1)} async-done(((bf16[16,16,384]{2,1,0:T(8,128)(2,1)}), bf16[16,16,384]{2,1,0:T(8,128)(2,1)S(1)}, u32[]{:S(2)}, u32[]{:S(2)}) %all-to-all-start.2) | async-done | bytes 196640 | tf_op jit(solution)/shard_map/all_to_all | solution.py:728
  61.1 0.0 copy-done.7
  61.1 3.2 %outer.1 = (f32[2,64,64,128]{3,2,1,0:T(8,128)}, f32[64,64]{1,0:T(8,128)}) custom-call(bf16[256,384]{1,0:T(8,128)(2,1)S(1)} %bitcast.13, f32[8,256]{1,0:T(8,128)S(1)} %get-tuple-element.54.spec, bf16[64,128]{1,0:T(8,128)(2,1)S(1)} %copy-done.7, f32[3,64]{1,0:T(4,128)S(1)} %copy-done.1), custom_call_target="tpu_custom_call" | custom-call | flops 1800000000 | bytes 10200000 | tf_op jit(solution)/shard_map/outer/pallas_call | solution.py:741
Async XLA Ops:
  1.9 2.8 %collective-permute-start.1 = (bf16[4,144,128]{2,1,0:T(8,128)(2,1)S(1)}, bf16[4,144,128]{2,1,0:T(8,128)(2,1)S(1)}, u32[]{:S(2)}, u32[]{:S(2)}) collective-permute-start(bf16[4,144,128]{2,1,0:T(8,128)(2,1)S(1)} %get-tuple-element.31), channel_id=1, source_target_pairs={{0,1},{1,0},{2,3},{3,2},{4,5},{5,4},{6,7},{7,6},{8,9},{9,8},{10,11... | collective-permute-start | bytes 442376 | tf_op jit(solution)/shard_map/ppermute | solution.py:630
  2.5 2.3 %collective-permute-start = (bf16[4,144,128]{2,1,0:T(8,128)(2,1)S(1)}, bf16[4,144,128]{2,1,0:T(8,128)(2,1)S(1)}, u32[]{:S(2)}, u32[]{:S(2)}) collective-permute-start(bf16[4,144,128]{2,1,0:T(8,128)(2,1)S(1)} %get-tuple-element.31), channel_id=1, source_target_pairs={{1,2},{3,4},{5,6},{7,8},{9,10},{11,12},{13,14},{2,1},{4,3},{6,5},{... | collective-permute-start | bytes 442376 | tf_op jit(solution)/shard_map/ppermute | solution.py:629
  3.2 16.6 %copy-start = (bf16[64,64]{1,0:T(8,128)(2,1)S(1)}, bf16[64,64]{1,0:T(8,128)(2,1)}, u32[]{:S(2)}) copy-start(bf16[64,64]{1,0:T(8,128)(2,1)} %point_weight.1) | copy-start | bytes 24580
  3.2 16.6 %copy-start.1 = (f32[3,64]{1,0:T(4,128)S(1)}, f32[3,64]{1,0:T(4,128)}, u32[]{:S(2)}) copy-start(f32[3,64]{1,0:T(4,128)} %lift.3) | copy-start | bytes 2308
  3.2 16.6 %copy-start.2 = (f32[64]{0:T(128)S(1)}, f32[64]{0:T(128)}, u32[]{:S(2)}) copy-start(f32[64]{0:T(128)} %param.33) | copy-start | bytes 772
  3.2 16.6 %copy-start.3 = (f32[64]{0:T(128)S(1)}, f32[64]{0:T(128)}, u32[]{:S(2)}) copy-start(f32[64]{0:T(128)} %param.34) | copy-start | bytes 772
  4.8 21.3 %copy-start.6 = (bf16[2,128,32]{2,1,0:T(8,128)(2,1)S(1)}, bf16[2,128,32]{2,1,0:T(8,128)(2,1)}, u32[]{:S(2)}) copy-start(bf16[2,128,32]{2,1,0:T(8,128)(2,1)} %constant.28.clone.bx) | copy-start | bytes 49156
  4.8 21.3 %copy-start.8 = (f32[16,256]{1,0:T(8,128)S(1)}, f32[16,256]{1,0:T(8,128)}, u32[]{:S(2)}) copy-start(f32[16,256]{1,0:T(8,128)} %constant.27.clone.ax) | copy-start | bytes 49156
  7.8 30.9 %copy-start.4 = (bf16[256,2048]{1,0:T(8,128)(2,1)S(1)}, bf16[256,2048]{1,0:T(8,128)(2,1)}, u32[]{:S(2)}) copy-start(bf16[256,2048]{1,0:T(8,128)(2,1)} %constant.25.clone.ez) | copy-start | bytes 3145732
  7.8 30.9 %copy-start.5 = (bf16[4,144,256]{2,1,0:T(8,128)(2,1)S(1)}, bf16[4,144,256]{2,1,0:T(8,128)(2,1)}, u32[]{:S(2)}) copy-start(bf16[4,144,256]{2,1,0:T(8,128)(2,1)} %constant.26.clone.fwd) | copy-start | bytes 884740
  7.8 18.3 %all-to-all-start = ((f32[16,1,128]{2,1,0:T(1,128)}), f32[16,1,128]{2,1,0:T(1,128)S(1)}, u32[]{:S(2)}, u32[]{:S(2)}) async-start(f32[16,1,128]{2,1,0:T(1,128)} %bitcast.5), calls=%async_computation | async-start | bytes 16384 | tf_op jit(solution)/shard_map/all_to_all | solution.py:691
  48.6 12.5 %all-to-all-start.2 = ((bf16[16,16,384]{2,1,0:T(8,128)(2,1)}), bf16[16,16,384]{2,1,0:T(8,128)(2,1)S(1)}, u32[]{:S(2)}, u32[]{:S(2)}) async-start(bf16[16,16,384]{2,1,0:T(8,128)(2,1)} %bitcast.9), calls=%async_computation.2 | async-start | bytes 393216 | tf_op jit(solution)/shard_map/all_to_all | solution.py:728
  52.2 8.9 %copy-start.7 = (bf16[64,128]{1,0:T(8,128)(2,1)S(1)}, bf16[64,128]{1,0:T(8,128)(2,1)}, u32[]{:S(2)}) copy-start(bf16[64,128]{1,0:T(8,128)(2,1)} %constant.29.clone.gx) | copy-start | bytes 49156

commit v7 on v6

--- a/solution.py
+++ b/solution.py
@@ -108,7 +108,7 @@
     bx[:, 0, 0], bx[:, 0, 1] = cg, -sg
     bx[:, 1, 0], bx[:, 1, 1] = sg, cg
     bx = bx.reshape(devices, local_x, 2, 2 * KX).transpose(1, 0, 2, 3) * iscale
-    tab["bx"] = np.stack(split(bx.reshape(2 * total_x, 2 * KX)))
+    tab["bx"] = np.concatenate(split(bx.reshape(2 * total_x, 2 * KX)), axis=1)
     gx = by_owner.transpose(3, 1, 0, 2).reshape(2 * KX, 2 * total_x)
     tab["gx"] = np.concatenate(split(gx), axis=0)
     return tab
@@ -348,10 +348,12 @@
     mixed_i = cr * mapped[0, 1] + ci * mapped[0, 0] + wr * mapped[1, 1] + wi * mapped[1, 0] + ones * mapped[2, 1]
     mixed_r = mixed_r.astype(BF16).astype(F32).T
     mixed_i = mixed_i.astype(BF16).astype(F32).T
+    rhs = [
+        jnp.concatenate([part[j * KX : (j + 1) * KX] for j in range(own_j)], axis=1) for part in (mixed_r, mixed_i)
+    ]
+    all_out = dot(bx[...], jnp.concatenate(rhs + rhs, axis=0).astype(BF16))
     for j in range(own_j):
-        rhs = jnp.concatenate([mixed_r[j * KX : (j + 1) * KX], mixed_i[j * KX : (j + 1) * KX]], axis=0)
-        rhs = rhs.astype(BF16)
-        out = dot(bx[0], rhs) + dot(bx[1], rhs)
+        out = all_out[:, j * channels : (j + 1) * channels]
         line = jnp.concatenate([out[i * blocks : (i + 1) * blocks] for i in range(local_x)], axis=1)
         for h in range(line.shape[1] // 128):
             if own_j == 1:

time: 64.7 us -> 64.6 us (level)
  no operation moved by 1% of the time
where the time goes in v7:
time: 64.6 us; the launch traced here: 64.2 us
  Pallas kernels  31.8 us (49%)
  starting transfers between devices  16.7 us (26%)
  blocking collectives  11.5 us (18%)
  waiting for transfers between devices  3.46 us (5%)
  between operations  0.79 us (1%)
    all_to_all x1, starting transfers between devices, body(): got = lax.all_to_all(send, 'slab', 0, 0, tiled=True)  11.9 us
    all_to_all x1, blocking collectives, body(): inv = lax.all_to_all(inv, 'slab', 0, 0, tiled=True)  11.5 us
    pallas_call x1, Pallas kernels, body(): pl.pallas_call(functools.partial(layer_kernel, own_j), name='layer', out_...  9.96 us
    pallas_call x1, Pallas kernels, body(): pl.pallas_call(predict_kernel, name='predict', out_shape=sds((local_x, pl...  7.69 us
    pallas_call x1, Pallas kernels, body(): pl.pallas_call(prepare_kernel, name='prepare', out_shape=(sds((2 * depth,...  4.08 us
    all_to_all x1, starting transfers between devices, body(): grad = lax.all_to_all(grad, 'slab', 0, 0, tiled=True)  3.52 us
    pallas_call x1, Pallas kernels, body(): pl.pallas_call(functools.partial(outer_kernel, own_j), name='outer', out_...  3.23 us
    pallas_call x1, Pallas kernels, body(): pl.pallas_call(functools.partial(transport_kernel, devices), name='transp...  2.97 us
  transfers between devices with their start and end apart: 4, of which 2 were waited for; matrix products, arithmetic and copies ran while one was open for 0% of the time, Pallas kernels for 21%

profile of v7, /device:TPU:0, one launch (start us, length us, event | category | flops | bytes accessed | tf_op | source)
XLA Modules:
  0.0 64.2 jit_solution(2449244307447834830)
XLA Ops:
  0.6 1.3 %pack.1 = (bf16[4,144,128]{2,1,0:T(8,128)(2,1)S(1)}, f32[4,128,128]{2,1,0:T(8,128)S(1)}, f32[4,8,128]{2,1,0:T(8,128)S(1)}) custom-call(f32[4,16384]{1,0:T(4,128)} %conc_hbm.1, f32[4,256]{1,0:T(4,128)} %cover_hbm.1, f32[4,256]{1,0:T(4,128)} %on_hbm.1, f32[4,256]{1,0:T(4,128)} %off_hbm.1, s32[4,256]{1,0:T(4,128)} %mask_hbm.1), custom_call_target="tpu_custom_call" | custom-call | flops 180000000 | bytes 1020000 | tf_op jit(solution)/shard_map/pack/pallas_call | solution.py:614
  1.9 0.6 collective-permute-start.1
  2.5 0.7 %collective-permute-start = (bf16[4,144,128]{2,1,0:T(8,128)(2,1)S(1)}, bf16[4,144,128]{2,1,0:T(8,128)(2,1)S(1)}, u32[]{:S(2)}, u32[]{:S(2)}) collective-permute-start(bf16[4,144,128]{2,1,0:T(8,128)(2,1)S(1)} %get-tuple-element.31), channel_id=1, source_target_pairs={{1,2},{3,4},{5,6},{7,8},{9,10},{11,12},{13,14},{2,1},{4,3},{6,5},{... | collective-permute-start | bytes 442376 | tf_op jit(solution)/shard_map/ppermute | solution.py:631
  3.2 0.0 copy-start
  3.2 0.0 copy-start.1
  3.2 0.0 copy-start.2
  3.2 0.0 copy-start.3
  3.2 1.6 %early.1 = (f32[4,128,128]{2,1,0:T(8,128)S(1)}, f32[16,256]{1,0:T(8,128)S(1)}, f32[128,128]{1,0:T(8,128)S(1)}, f32[128,512]{1,0:T(8,128)S(1)}, f32[256,256]{1,0:...) custom-call(f32[4,128,128]{2,1,0:T(8,128)S(1)} %get-tuple-element.32.own, ...), custom_call_target="tpu_custom_call" | custom-call | flops 900000000 | bytes 5100000 | tf_op jit(solution)/shard_map/early/pallas_call | solution.py:634
  4.8 0.0 collective-permute-done.1.within
  4.8 0.0 collective-permute-done.across
  4.8 0.0 copy-start.6
  4.8 0.0 copy-start.8
  4.8 3.0 %transport.1 = (f32[4,256]{1,0:T(4,128)}, f32[128,4,128]{2,1,0:T(4,128)S(1)}, f32[4,256]{1,0:T(4,128)S(1)}, f32[16,128]{1,0:T(8,128)}) custom-call(bf16[4,144,128]{2,1,0:T(8,128)(2,1)S(1)} %collective-permute-done.across, bf16[4,144,128]{2,1,0:T(8,128)(2,1)S(1)} %collective-permute-done.1.within, f32[4,128,128]{2,1,0:T(8,128)S(1)} %get-tuple-element.34.own, ...), custom_call_target="tpu_custom_call" | custom-call | flops 1800000000 | bytes 10200000 | tf_op jit(solution)/shard_map/transport/pallas_call | solution.py:651
  7.8 0.0 copy-start.4
  7.8 0.0 copy-start.5
  7.8 11.9 %all-to-all-start = ((f32[16,1,128]{2,1,0:T(1,128)}), f32[16,1,128]{2,1,0:T(1,128)S(1)}, u32[]{:S(2)}, u32[]{:S(2)}) async-start(f32[16,1,128]{2,1,0:T(1,128)} %bitcast.5), calls=%async_computation | async-start | bytes 16384 | tf_op jit(solution)/shard_map/all_to_all | solution.py:693
  19.7 0.0 copy-done
  19.7 0.0 copy-done.1
  19.7 0.0 copy-done.2
  19.8 0.0 copy-done.3
  19.8 4.1 %prepare.1 = (f32[128,4,128]{2,1,0:T(4,128)S(1)}, f32[3,2,64,128]{3,2,1,0:T(8,128)S(1)}, bf16[256,32]{1,0:T(8,128)(2,1)S(1)}, bf16[16,256]{1,0:T(8,128)(2,1)S(1)}, f32[4,16384]{1,0:T(4,128)}) custom-call(f32[4,16384]{1,0:T(4,128)} %cot_hbm.1, f32[3,64]{1,0:T(4,128)S(1)} %copy-done.1, bf16[2,64,64,128]{3,2,1,0:T(8,128)(2,1)} %bitcast.20, ...), custom_call_target="tpu_custom_call" | custom-call | flops 1200000000 | bytes 6800000 | tf_op jit(solution)/shard_map/prepare/pallas_call | solution.py:666
  23.9 2.2 %all-to-all-done = f32[16,1,128]{2,1,0:T(1,128)S(1)} async-done(((f32[16,1,128]{2,1,0:T(1,128)}), f32[16,1,128]{2,1,0:T(1,128)S(1)}, u32[]{:S(2)}, u32[]{:S(2)}) %all-to-all-start) | async-done | bytes 8224 | tf_op jit(solution)/shard_map/all_to_all | solution.py:693
  26.1 0.0 copy-done.6
  26.1 0.0 copy-done.8
  26.1 1.0 %mixing.1 = (bf16[256,256]{1,0:T(8,128)(2,1)S(1)}, f32[8,256]{1,0:T(8,128)S(1)}) custom-call(f32[16,128]{1,0:T(8,128)S(1)} %bitcast.16, f32[16,256]{1,0:T(8,128)S(1)} %copy-done.8, bf16[128,64]{1,0:T(8,128)(2,1)S(1)} %copy-done.6, f32[3,2,64,128]{3,2,1,0:T(8,128)S(1)} %get-tuple-element.46.mapped), custom_call_target="tpu_custom_call" | custom-call | flops 960000000 | bytes 5440000 | tf_op jit(solution)/shard_map/mixing/pallas_call | solution.py:695
  27.0 11.5 %all_to_all.33 = bf16[16,16,256]{2,1,0:T(8,128)(2,1)S(1)} all-to-all(bf16[16,16,256]{2,1,0:T(8,128)(2,1)S(1)} %bitcast.14), channel_id=1, replica_groups=mesh['groups'=2,'slab'=16] {'slab'}, dimensions={0} | all-to-all | bytes 262144 | tf_op jit(solution)/shard_map/all_to_all | solution.py:708
  38.6 0.0 copy-done.4
  38.6 0.0 copy-done.5
  38.6 10.0 %layer.1 = (bf16[256,384]{1,0:T(8,128)(2,1)}, bf16[16,256,128]{2,1,0:T(8,128)(2,1)S(1)}) custom-call(bf16[256,256]{1,0:T(8,128)(2,1)S(1)} %bitcast.15, f32[128,4,128]{2,1,0:T(4,128)S(1)} %get-tuple-element.42.conc_z, f32[128,4,128]{2,1,0:T(4,128)S(1)} %get-tuple-element.48.cot_z, f32[4,256]{1,0:T(4,128)S(1)} %get-tuple-element.49.cover_z, ...), custom_call_target="tpu_custom_call" | custom-call | flops 6600000000 | bytes 37400000 | tf_op jit(solution)/shard_map/layer/pallas_call | solution.py:711
  48.5 3.5 %all-to-all-start.2 = ((bf16[16,16,384]{2,1,0:T(8,128)(2,1)}), bf16[16,16,384]{2,1,0:T(8,128)(2,1)S(1)}, u32[]{:S(2)}, u32[]{:S(2)}) async-start(bf16[16,16,384]{2,1,0:T(8,128)(2,1)} %bitcast.9), calls=%async_computation.2 | async-start | bytes 393216 | tf_op jit(solution)/shard_map/all_to_all | solution.py:730
  52.1 0.0 copy-start.7
  52.1 7.7 %predict.1 = f32[4,16384]{1,0:T(4,128)} custom-call(bf16[16,256,128]{2,1,0:T(8,128)(2,1)S(1)} %get-tuple-element.51.lhs, f32[128,4,128]{2,1,0:T(4,128)S(1)} %get-tuple-element.42.conc_z, f32[4,256]{1,0:T(4,128)S(1)} %get-tuple-element.49.cover_z, bf16[256,32]{1,0:T(8,128)(2,1)S(1)} %get-tuple-element.50.terms, bf16[16,256]{1,0:T(8,128)(2,1)S(1)} %get-tuple-element.52.weigh, ...), custom_call_target="tpu_custom_call" | custom-call | flops 3300000000 | bytes 18700000 | tf_op jit(solution)/shard_map/predict/pallas_call | solution.py:731
  59.8 1.2 %all-to-all-done.2 = bf16[16,16,384]{2,1,0:T(8,128)(2,1)S(1)} async-done(((bf16[16,16,384]{2,1,0:T(8,128)(2,1)}), bf16[16,16,384]{2,1,0:T(8,128)(2,1)S(1)}, u32[]{:S(2)}, u32[]{:S(2)}) %all-to-all-start.2) | async-done | bytes 196640 | tf_op jit(solution)/shard_map/all_to_all | solution.py:730
  61.0 0.0 copy-done.7
  61.0 3.2 %outer.1 = (f32[2,64,64,128]{3,2,1,0:T(8,128)}, f32[64,64]{1,0:T(8,128)}) custom-call(bf16[256,384]{1,0:T(8,128)(2,1)S(1)} %bitcast.13, f32[8,256]{1,0:T(8,128)S(1)} %get-tuple-element.54.spec, bf16[64,128]{1,0:T(8,128)(2,1)S(1)} %copy-done.7, f32[3,64]{1,0:T(4,128)S(1)} %copy-done.1), custom_call_target="tpu_custom_call" | custom-call | flops 1800000000 | bytes 10200000 | tf_op jit(solution)/shard_map/outer/pallas_call | solution.py:743
Async XLA Ops:
  1.9 2.8 %collective-permute-start.1 = (bf16[4,144,128]{2,1,0:T(8,128)(2,1)S(1)}, bf16[4,144,128]{2,1,0:T(8,128)(2,1)S(1)}, u32[]{:S(2)}, u32[]{:S(2)}) collective-permute-start(bf16[4,144,128]{2,1,0:T(8,128)(2,1)S(1)} %get-tuple-element.31), channel_id=1, source_target_pairs={{0,1},{1,0},{2,3},{3,2},{4,5},{5,4},{6,7},{7,6},{8,9},{9,8},{10,11... | collective-permute-start | bytes 442376 | tf_op jit(solution)/shard_map/ppermute | solution.py:632
  2.5 2.3 %collective-permute-start = (bf16[4,144,128]{2,1,0:T(8,128)(2,1)S(1)}, bf16[4,144,128]{2,1,0:T(8,128)(2,1)S(1)}, u32[]{:S(2)}, u32[]{:S(2)}) collective-permute-start(bf16[4,144,128]{2,1,0:T(8,128)(2,1)S(1)} %get-tuple-element.31), channel_id=1, source_target_pairs={{1,2},{3,4},{5,6},{7,8},{9,10},{11,12},{13,14},{2,1},{4,3},{6,5},{... | collective-permute-start | bytes 442376 | tf_op jit(solution)/shard_map/ppermute | solution.py:631
  3.2 16.6 %copy-start = (bf16[64,64]{1,0:T(8,128)(2,1)S(1)}, bf16[64,64]{1,0:T(8,128)(2,1)}, u32[]{:S(2)}) copy-start(bf16[64,64]{1,0:T(8,128)(2,1)} %point_weight.1) | copy-start | bytes 24580
  3.2 16.6 %copy-start.1 = (f32[3,64]{1,0:T(4,128)S(1)}, f32[3,64]{1,0:T(4,128)}, u32[]{:S(2)}) copy-start(f32[3,64]{1,0:T(4,128)} %lift.3) | copy-start | bytes 2308
  3.2 16.6 %copy-start.2 = (f32[64]{0:T(128)S(1)}, f32[64]{0:T(128)}, u32[]{:S(2)}) copy-start(f32[64]{0:T(128)} %param.33) | copy-start | bytes 772
  3.2 16.6 %copy-start.3 = (f32[64]{0:T(128)S(1)}, f32[64]{0:T(128)}, u32[]{:S(2)}) copy-start(f32[64]{0:T(128)} %param.34) | copy-start | bytes 772
  4.8 21.3 %copy-start.6 = (bf16[128,64]{1,0:T(8,128)(2,1)S(1)}, bf16[128,64]{1,0:T(8,128)(2,1)}, u32[]{:S(2)}) copy-start(bf16[128,64]{1,0:T(8,128)(2,1)} %constant.28.clone.bx) | copy-start | bytes 49156
  4.8 21.3 %copy-start.8 = (f32[16,256]{1,0:T(8,128)S(1)}, f32[16,256]{1,0:T(8,128)}, u32[]{:S(2)}) copy-start(f32[16,256]{1,0:T(8,128)} %constant.27.clone.ax) | copy-start | bytes 49156
  7.8 30.8 %copy-start.4 = (bf16[256,2048]{1,0:T(8,128)(2,1)S(1)}, bf16[256,2048]{1,0:T(8,128)(2,1)}, u32[]{:S(2)}) copy-start(bf16[256,2048]{1,0:T(8,128)(2,1)} %constant.25.clone.ez) | copy-start | bytes 3145732
  7.8 30.8 %copy-start.5 = (bf16[4,144,256]{2,1,0:T(8,128)(2,1)S(1)}, bf16[4,144,256]{2,1,0:T(8,128)(2,1)}, u32[]{:S(2)}) copy-start(bf16[4,144,256]{2,1,0:T(8,128)(2,1)} %constant.26.clone.fwd) | copy-start | bytes 884740
  7.8 18.3 %all-to-all-start = ((f32[16,1,128]{2,1,0:T(1,128)}), f32[16,1,128]{2,1,0:T(1,128)S(1)}, u32[]{:S(2)}, u32[]{:S(2)}) async-start(f32[16,1,128]{2,1,0:T(1,128)} %bitcast.5), calls=%async_computation | async-start | bytes 16384 | tf_op jit(solution)/shard_map/all_to_all | solution.py:693
  48.5 12.5 %all-to-all-start.2 = ((bf16[16,16,384]{2,1,0:T(8,128)(2,1)}), bf16[16,16,384]{2,1,0:T(8,128)(2,1)S(1)}, u32[]{:S(2)}, u32[]{:S(2)}) async-start(bf16[16,16,384]{2,1,0:T(8,128)(2,1)} %bitcast.9), calls=%async_computation.2 | async-start | bytes 393216 | tf_op jit(solution)/shard_map/all_to_all | solution.py:730
  52.1 8.9 %copy-start.7 = (bf16[64,128]{1,0:T(8,128)(2,1)S(1)}, bf16[64,128]{1,0:T(8,128)(2,1)}, u32[]{:S(2)}) copy-start(bf16[64,128]{1,0:T(8,128)(2,1)} %constant.29.clone.gx) | copy-start | bytes 49156
